TPU v7x, 32 devices: a whole 2x2x4 slice. The times are simulated.
32 devices in a mesh: wide: 16 (over z, x, core), narrow: 2 (over y).
Axes of the slice: x: 2, y: 2, z: 4, core: 2. Of those that a mesh axis runs over, the one named last changes fastest.
Arguments:
- edge_msg: bfloat16 [8192, 1024], P(('wide', 'narrow')), may hold values from -6 to 6
- basis: bfloat16 [8192, 512], P(('wide', 'narrow')), may hold values from -1.5 to 1.5
- atom_h: bfloat16 [1024, 512], P('narrow'), may hold values from -6 to 6
- edge_source: int32 [8192], P(('wide', 'narrow')), may hold values from 0 to 1023
- edge_target: int32 [8192], P(('wide', 'narrow')), may hold values from 0 to 1023, as said below
- send_rows: int32 [32, 512], P(('wide', 'narrow')), may hold values from 0 to 255
- trip_slot: int32 [8192, 32], P(('wide', 'narrow')), may hold values from 0 to 511, as said below
- w_down: bfloat16 [1024, 64], replicated, may hold values from -0.1875 to 0.1875
- w_bil: bfloat16 [1024, 64], replicated, may hold values from -0.1875 to 0.1875
- w_up: bfloat16 [64, 1024], replicated, may hold values from -0.75 to 0.75
- w_atom_in: bfloat16 [1024, 512], replicated, may hold values from -0.1875 to 0.1875
- atom_gain: float32 [512], replicated, may hold values from 0.5 to 1.5
- w_atom: bfloat16 [512, 512], replicated, may hold values from -0.25 to 0.25
- w_src: bfloat16 [512, 1024], replicated, may hold values from -0.25 to 0.25
- w_tgt: bfloat16 [512, 1024], replicated, may hold values from -0.25 to 0.25
Outputs:
- edge_out: bfloat16 [8192, 1024], P(('wide', 'narrow'))
- atom_out: bfloat16 [1024, 512], P('narrow')
Inputs may be any that keep to these rules, and one draw needn't show every extreme that they name: `edge_target`: the edges of block b target atoms of the narrow block b % 2, that is (b % 2) * 512 to (b % 2 + 1) * 512 - 1, never outside that range, and never falling (sorted) within a block. `trip_slot`: for each receiving block and each wide index p, the slots p * 32 + c that its triplets use form a prefix c < count of 1 to 32 entries; every block has some p with all 32 used.
All inputs are finite; a program needn't handle non-finite values.
Results may differ from a plain program's by a relative error of at most 0.0065.
Values may be sent and summed in bfloat16 or wider, within the bound.
No kernel may reach another device: no remote copies, remote signals or barrier semaphores. Data moves between devices by JAX's collectives and lax.ppermute only.
A program may use at most 64 MiB of HBM per device.

v0:
```python
import jax
import jax.numpy as jnp
from jax import lax
from jax.sharding import PartitionSpec as P


def silu(value):
    return value / (1.0 + jnp.exp(-value))


def atom_update(sums, base_rows, atom_gain, w_atom):
    scale = lax.rsqrt(jnp.mean(sums * sums, axis=-1, keepdims=True) + 1e-06)
    normed = (sums * scale * atom_gain).astype(jnp.bfloat16)
    grown = silu(jnp.dot(normed, w_atom, preferred_element_type=jnp.float32))
    return (base_rows.astype(jnp.float32) + grown).astype(jnp.bfloat16)


def per_device(
    edge_msg,
    basis,
    atom_h,
    edge_source,
    edge_target,
    send_rows,
    trip_slot,
    w_down,
    w_bil,
    w_up,
    w_atom_in,
    atom_gain,
    w_atom,
    w_src,
    w_tgt,
):
    edge_count = edge_msg.shape[0]
    width_trip = w_down.shape[1]
    basis_count = w_bil.shape[0] // width_trip
    triplets = trip_slot.shape[1]
    atom_count = atom_h.shape[0]
    down = silu(jnp.dot(edge_msg, w_down, preferred_element_type=jnp.float32)).astype(jnp.bfloat16)
    outgoing = down[send_rows[0]]
    slot_count = outgoing.shape[0]
    outgoing = outgoing.reshape(slot_count // 2, 2 * width_trip)
    received = lax.all_to_all(outgoing, "wide", split_axis=0, concat_axis=0, tiled=True)
    received = received.reshape(slot_count, width_trip)
    other = received[trip_slot]
    weights = basis.reshape(edge_count, triplets, basis_count)
    mixed = jnp.einsum("etk,etc->ekc", weights, other, preferred_element_type=jnp.float32)
    mixed = mixed.reshape(edge_count, basis_count * width_trip).astype(jnp.bfloat16)
    trip = silu(jnp.dot(mixed, w_bil, preferred_element_type=jnp.float32)).astype(jnp.bfloat16)
    edge_mid = (
        edge_msg.astype(jnp.float32) + jnp.dot(trip, w_up, preferred_element_type=jnp.float32)
    ).astype(jnp.bfloat16)
    message = jnp.dot(edge_mid, w_atom_in, preferred_element_type=jnp.float32).astype(jnp.bfloat16)
    first_atom = lax.axis_index("narrow") * atom_count
    local_target = edge_target - first_atom
    one_hot = (local_target[:, None] == jnp.arange(atom_count, dtype=jnp.int32)[None, :]).astype(
        jnp.bfloat16
    )
    partial_sums = lax.dot_general(
        one_hot, message, (((0,), (0,)), ((), ())), preferred_element_type=jnp.float32
    )
    shares = lax.psum_scatter(partial_sums, "wide", scatter_dimension=0, tiled=True)
    share_rows = shares.shape[0]
    base_rows = lax.dynamic_slice_in_dim(atom_h, lax.axis_index("wide") * share_rows, share_rows, 0)
    updated = atom_update(shares, base_rows, atom_gain, w_atom)
    atom_out = lax.all_gather(updated, "wide", axis=0, tiled=True)
    every_atom = lax.all_gather(atom_out, "narrow", axis=0, tiled=True)
    source_rows = every_atom[edge_source]
    target_rows = jnp.dot(one_hot, atom_out, preferred_element_type=jnp.float32).astype(
        jnp.bfloat16
    )
    update = jnp.dot(source_rows, w_src, preferred_element_type=jnp.float32) + jnp.dot(
        target_rows, w_tgt, preferred_element_type=jnp.float32
    )
    edge_out = (edge_mid.astype(jnp.float32) + silu(update)).astype(jnp.bfloat16)
    return (edge_out, atom_out)


def solution(mesh):
    placed = (
        P(("wide", "narrow"), None),
        P(("wide", "narrow"), None),
        P("narrow", None),
        P(("wide", "narrow")),
        P(("wide", "narrow")),
        P(("wide", "narrow"), None),
        P(("wide", "narrow"), None),
        P(),
        P(),
        P(),
        P(),
        P(),
        P(),
        P(),
        P(),
    )
    return jax.shard_map(
        per_device,
        mesh=mesh,
        in_specs=placed,
        out_specs=(P(("wide", "narrow"), None), P("narrow", None)),
        check_vma=False,
    )
```

profile of v0, /device:TPU:0, one launch (start us, length us, event | category | flops | bytes accessed | tf_op | source)
XLA Modules:
  0.0 171.4 jit_solution(13666013505709908320)
XLA Ops:
  7.2 0.0 copy-start
  7.2 1.5 divide_convert_fusion.1
  8.7 0.0 copy-start.9
  8.7 0.1 copy.19
  8.8 0.7 compare_select_fusion.1
  9.5 1.3 gather_fusion
  10.8 0.7 all_to_all.6
  11.6 7.4 %all-to-all-start = ((bf16[16,16,128]{2,1,0:T(8,128)(2,1)}), bf16[16,16,128]{2,1,0:T(8,128)(2,1)S(1)}, u32[]{:S(2)}, u32[]{:S(2)}) async-start(bf16[16,16,128]{2,1,0:T(8,128)(2,1)} %all_to_all.6), calls=%async_computation | async-start | bytes 131072 | tf_op jit(solution)/shard_map/all_to_all | solution.py:44
  19.0 0.0 reduce-scatter.2.cloned.1.call-start
  19.1 0.1 copy.21
  19.2 2.0 %copy.22 = bf16[256,32,16]{1,2,0:T(8,128)(2,1)} copy(bf16[256,32,16]{0,2,1:T(8,128)(2,1)S(1)} %bitcast.24) | data formatting | bytes 524288 | tf_op jit(solution)/shard_map/reshape | solution.py:47
  21.2 0.1 copy.20
  21.3 0.1 reshape.67
  21.4 4.5 %all-to-all-done = bf16[16,16,128]{2,1,0:T(8,128)(2,1)S(1)} async-done(((bf16[16,16,128]{2,1,0:T(8,128)(2,1)}), bf16[16,16,128]{2,1,0:T(8,128)(2,1)S(1)}, u32[]{:S(2)}, u32[]{:S(2)}) %all-to-all-start) | async-done | bytes 65568 | tf_op jit(solution)/shard_map/all_to_all | solution.py:44
  25.9 0.1 reshape.55
  26.0 24.0 %gather_fusion.1 = bf16[8192,64]{1,0:T(8,128)(2,1)S(1)} fusion(bf16[512,64]{1,0:T(8,128)(2,1)S(1)} %reshape.55, s32[8192]{0:T(1024)S(1)} %broadcast_clamp_fusion), kind=kCustom, calls=%fused_computation.1 | custom fusion | bytes 2129920 | tf_op jit(solution)/shard_map/gather | solution.py:46
  50.1 3.0 %fusion = bf16[256,16,64]{2,1,0:T(8,128)(2,1)} fusion(bf16[256,32,16]{1,2,0:T(8,128)(2,1)} %copy.22, bf16[256,32,64]{2,1,0:T(8,128)(2,1)S(1)} %bitcast.22), kind=kOutput, calls=%fused_computation.4 | convolution fusion | flops 17039360 | bytes 1835008 | tf_op jit(solution)/shard_map/etk,etc->ekc/dot_general | solution.py:48
  53.0 2.0 %copy.23 = bf16[256,16,64]{0,2,1:T(8,128)(2,1)S(1)} copy(bf16[256,16,64]{2,1,0:T(8,128)(2,1)} %fusion) | data formatting | bytes 1048576 | tf_op jit(solution)/shard_map/convert_element_type | solution.py:49
  55.0 1.7 %fusion.1 = bf16[256,1024]{1,0:T(8,128)(2,1)S(1)} fusion(bf16[64,1024]{1,0:T(8,128)(2,1)S(1)} %copy-done.5, bf16[256,1024]{1,0:T(8,128)(2,1)} %param.15, bf16[1024,64]{0,1:T(8,128)(2,1)S(1)} %copy-done.6, bf16[256,1024]{0,1:T(8,128)(2,1)S(1)} %bitcast.23), kind=kOutput, calls=%fused_computation.7 | convolution fusion | flops 67960832 | bytes 1835008 | tf_op jit(solution)/shard_map/dot_general | solution.py:52
  56.8 1.7 fusion.2
  58.5 0.0 reduce-scatter.2.cloned.1.call-update
  58.5 0.0 all-gather.2.cloned.1.call-start
  58.6 55.0 %reduce-scatter.2.cloned.1.call-done = f32[32,512]{1,0:T(8,128)} async-done(((f32[512,512]{1,0:T(8,128)}), f32[32,512]{1,0:T(8,128)}) %reduce-scatter.2.cloned.1.call-update) | async-done | bytes 65552 | tf_op jit(solution)/shard_map/reduce_scatter | solution.py:63
  113.6 1.0 multiply_reduce_fusion
  114.6 1.1 add_convert_fusion.1
  115.7 22.2 %all_gather.6 = bf16[512,512]{1,0:T(8,128)(2,1)} all-gather(bf16[32,512]{1,0:T(8,128)(2,1)S(1)} %add_convert_fusion.1), channel_id=1, replica_groups=mesh['wide'=16,'narrow'=2] {'wide'}, dimensions={0}, use_global_device_ids=true | all-gather | bytes 557056 | tf_op jit(solution)/shard_map/all_gather | solution.py:67
  137.9 0.0 all-gather.2.cloned.1.call-update
  138.0 18.7 %all-gather.2.cloned.1.call-done = bf16[1024,512]{1,0:T(8,128)(2,1)} async-done(((bf16[512,512]{1,0:T(8,128)(2,1)}), bf16[1024,512]{1,0:T(8,128)(2,1)}) %all-gather.2.cloned.1.call-update) | async-done | bytes 1048592 | tf_op jit(solution)/shard_map/all_gather | solution.py:68
  156.6 2.6 %gather_fusion.2 = bf16[256,512]{1,0:T(8,128)(2,1)S(1)} fusion(bf16[1024,512]{1,0:T(8,128)(2,1)} %all-gather.2.cloned.1.call-done, s32[1024]{0:T(1024)S(1)} %pad_clamp_fusion), kind=kCustom, calls=%fused_computation.2 | custom fusion | bytes 525312 | tf_op jit(solution)/shard_map/gather | solution.py:69
  159.2 1.4 fusion.13
  160.6 3.1 %add_convert_fusion = bf16[256,1024]{1,0:T(8,128)(2,1)} fusion(f32[256,1024]{1,0:T(8,128)} %fusion.13, bf16[512,1024]{1,0:T(8,128)(2,1)} %param.29, bf16[512,512]{1,0:T(8,128)(2,1)S(1)} %copy-done.1, bf16[256,1024]{1,0:T(8,128)(2,1)S(1)} %fusion.1, s32[256]{0:T(256)S(1)} %broadcast_subtract_fusion), kind=kOutput, calls=%fused_computation.11 | convolution fusion | flops 404750336 | bytes 3671040 | tf_op jit(solution)/shard_map/dot_general | solution.py:73
  163.8 0.8 copy.25
  (27 shorter events, 0.1 us)
Async XLA Ops:
  7.2 49.6 %copy-start = (bf16[1024,512]{1,0:T(8,128)(2,1)S(1)}, bf16[1024,512]{1,0:T(8,128)(2,1)}, u32[]{:S(2)}) copy-start(bf16[1024,512]{1,0:T(8,128)(2,1)} %param.25) | copy-start | bytes 3145732
  7.2 11.9 %copy-start.4 = (bf16[256,512]{1,0:T(8,128)(2,1)S(1)}, bf16[256,512]{1,0:T(8,128)(2,1)}, u32[]{:S(2)}) copy-start(bf16[256,512]{1,0:T(8,128)(2,1)} %param.16) | copy-start | bytes 786436
  7.2 14.0 %copy-start.7 = (s32[256,32]{0,1:T(8,128)S(1)}, s32[256,32]{0,1:T(8,128)}, u32[]{:S(2)}) copy-start(s32[256,32]{0,1:T(8,128)} %param.21) | copy-start | bytes 98308
  8.7 12.7 %copy-start.9 = (s32[256]{0:T(256)S(1)}, s32[256]{0:T(256)}, u32[]{:S(2)}) copy-start(s32[256]{0:T(256)} %param.19) | copy-start | bytes 3076
  11.6 14.3 %all-to-all-start = ((bf16[16,16,128]{2,1,0:T(8,128)(2,1)}), bf16[16,16,128]{2,1,0:T(8,128)(2,1)S(1)}, u32[]{:S(2)}, u32[]{:S(2)}) async-start(bf16[16,16,128]{2,1,0:T(8,128)(2,1)} %all_to_all.6), calls=%async_computation | async-start | bytes 131072 | tf_op jit(solution)/shard_map/all_to_all | solution.py:44
  19.0 94.6 %reduce-scatter.2.cloned.1.call-start = ((), (), s32[]{:S(2)}) async-start(), calls=%async_computation.2 | async-start | bytes 1114112 | tf_op jit(solution)/shard_map/reduce_scatter | solution.py:63
  50.0 5.0 %copy-start.5 = (bf16[64,1024]{1,0:T(8,128)(2,1)S(1)}, bf16[64,1024]{1,0:T(8,128)(2,1)}, u32[]{:S(2)}) copy-start(bf16[64,1024]{1,0:T(8,128)(2,1)} %param.24) | copy-start | bytes 393220
  50.0 5.0 %copy-start.6 = (bf16[1024,64]{0,1:T(8,128)(2,1)S(1)}, bf16[1024,64]{0,1:T(8,128)(2,1)}, u32[]{:S(2)}) copy-start(bf16[1024,64]{0,1:T(8,128)(2,1)} %param.23) | copy-start | bytes 393220
  56.7 57.8 %copy-start.3 = (bf16[512,512]{1,0:T(8,128)(2,1)S(1)}, bf16[512,512]{1,0:T(8,128)(2,1)}, u32[]{:S(2)}) copy-start(bf16[512,512]{1,0:T(8,128)(2,1)} %param.27) | copy-start | bytes 1572868
  56.8 57.8 %copy-start.8 = (f32[512]{0:T(512)S(1)}, f32[512]{0:T(512)}, u32[]{:S(2)}) copy-start(f32[512]{0:T(512)} %param.26) | copy-start | bytes 6148
  56.8 81.2 %copy-start.10 = (s32[256]{0:T(256)S(1)}, s32[256]{0:T(256)}, u32[]{:S(2)}) copy-start(s32[256]{0:T(256)} %param.18) | copy-start | bytes 3076
  58.5 100.7 %copy-start.2 = (bf16[512,1024]{1,0:T(8,128)(2,1)S(1)}, bf16[512,1024]{1,0:T(8,128)(2,1)}, u32[]{:S(2)}) copy-start(bf16[512,1024]{1,0:T(8,128)(2,1)} %param.28) | copy-start | bytes 3145732
  58.5 98.1 %all-gather.2.cloned.1.call-start = ((), (), s32[]{:S(2)}) async-start(), calls=%async_computation.3 | async-start | bytes 1572864 | tf_op jit(solution)/shard_map/all_gather | solution.py:68
  138.0 22.7 %copy-start.1 = (bf16[512,512]{1,0:T(8,128)(2,1)S(1)}, bf16[512,512]{1,0:T(8,128)(2,1)}, u32[]{:S(2)}) copy-start(bf16[512,512]{1,0:T(8,128)(2,1)} %all_gather.6) | copy-start | bytes 1572868
Sparse Core Ops, SparseCore 0:
  58.6 54.9 reduce-scatter.1
  138.1 18.5 all-gather.1
where the time goes:
time: 172 us; the launch traced here: 171 us
  waiting for transfers between devices  78.2 us (45%)
  local copies, waits for them, and re-layouts  34 us (20%)
  blocking collectives  22.2 us (13%)
  between operations  14.3 us (8%)
  matrix products  13.5 us (8%)
  starting transfers between devices  7.47 us (4%)
    reduce_scatter x1, waiting for transfers between devices, per_device(): lax.psum_scatter(partial_sums, 'wide', scatter_dimension=0, tiled=True)  55 us
    gather x1, local copies, waits for them, and re-layouts, per_device(): other = received[trip_slot]  24 us
    all_gather x1, blocking collectives, per_device(): atom_out = lax.all_gather(updated, 'wide', axis=0, tiled=True)  22.2 us
    all_gather x1, waiting for transfers between devices, per_device(): every_atom = lax.all_gather(atom_out, 'narrow', axis=0, tiled=True)  18.7 us
    all_to_all x1, starting transfers between devices, per_device(): lax.all_to_all(outgoing, 'wide', split_axis=0, concat_axis=0, tiled=True)  7.38 us
    all_to_all x1, waiting for transfers between devices, per_device(): lax.all_to_all(outgoing, 'wide', split_axis=0, concat_axis=0, tiled=True)  4.49 us
  transfers between devices with their start and end apart: 3, of which 3 were waited for; matrix products, arithmetic and copies ran while one was open for 1% of the time, Pallas kernels for 0%

commit v1 on v0

v1 whole, which is shorter than its diff:
```python
import functools

import jax
import jax.numpy as jnp
from jax import lax
from jax.experimental import pallas as pl
from jax.experimental.pallas import tpu as pltpu
from jax.sharding import PartitionSpec as P

F32 = jnp.float32
BF16 = jnp.bfloat16
NT = (((1,), (1,)), ((), ()))


def silu(value):
    return value / (1.0 + jnp.exp(-value))


def dot(a, b):
    return jnp.dot(a, b, preferred_element_type=F32)


def dot_nt(a, b):
    return lax.dot_general(a, b, NT, preferred_element_type=F32)


def iota(shape, dim):
    return lax.broadcasted_iota(jnp.int32, shape, dim)


def column(row):
    return jnp.broadcast_to(row, (8, row.shape[1])).T[:, :1]


def call(kernel, out_shape, vmem, scratch=(), cost=None, name=None):
    return pl.pallas_call(
        kernel,
        out_shape=out_shape,
        scratch_shapes=list(scratch),
        compiler_params=pltpu.CompilerParams(vmem_limit_bytes=vmem),
        cost_estimate=cost,
        name=name,
    )


def cost(flops, moved):
    return pl.CostEstimate(flops=int(flops), bytes_accessed=int(moved), transcendentals=0)


def outgoing_kernel(edge_msg, w_down_t, send_rows, target, out):
    edges = edge_msg.shape[0]
    width = w_down_t.shape[0]
    peers, rows, lanes = out.shape
    half = rows - 8
    slots = peers * half * 2
    down_w = w_down_t[...]
    twice = jnp.concatenate([down_w, down_w], axis=0)
    down = silu(dot_nt(edge_msg[...], twice)).astype(BF16)
    chosen = column(send_rows[...]) == iota((slots, edges), 1)
    picked = dot(jnp.where(chosen, 1.0, 0.0).astype(BF16), down)
    picked = picked.reshape(peers, 2 * half, lanes)
    low = iota((peers, half, lanes), 2) < width
    packed = jnp.where(low, picked[:, :half], picked[:, half:])
    out[:, :half, :] = packed.astype(BF16)
    atoms = target[...]
    count = edges // lanes
    codes = [lax.shift_right_logical(atoms, 8), lax.bitwise_and(atoms, 255)]
    parts = [c[:, i * lanes : (i + 1) * lanes] for c in codes for i in range(count)]
    parts += [jnp.zeros_like(parts[0])] * (8 - len(parts))
    code_rows = jnp.concatenate(parts, axis=0).astype(F32)
    out[:, half:, :] = jnp.broadcast_to(code_rows[None], (peers, 8, lanes)).astype(BF16)


def mixer_kernel(basis, slots_flat, out, spread):
    basis_count, edges, slots = out.shape
    groups, span = slots_flat.shape
    per = edges // groups
    triplets = span // per
    total = basis.shape[1]
    rows, cols = iota((total, total), 0), iota((total, total), 1)
    order = (rows // basis_count == cols % triplets) & (rows % basis_count == cols // triplets)
    by_basis = dot(basis[...], jnp.where(order, 1.0, 0.0).astype(BF16)).astype(BF16)
    pack = 128 // triplets
    rows, cols = iota((128, span), 0), iota((128, span), 1)
    own = iota((edges, span), 0) % per == iota((edges, span), 1) // triplets
    for j in range(pack):
        tile = (rows // triplets == j) & (rows % triplets == cols % triplets)
        tile = jnp.where(tile, 1.0, 0.0).astype(BF16)
        for q in range(basis_count // pack):
            wide = dot(by_basis[:, q * 128 : (q + 1) * 128], tile)
            spread[q * pack + j] = jnp.where(own, wide, 0.0)

    def step(pair, _):
        parts = []
        for h in range(2):
            group = pair * 2 + h
            left = spread[:, pl.ds(pl.multiple_of(group * per, per), per), :]
            left = left.reshape(basis_count * per, span).astype(BF16)
            hot = iota((slots, span), 0) == slots_flat[pl.ds(group, 1), :]
            part = dot_nt(left, jnp.where(hot, 1.0, 0.0).astype(BF16))
            parts.append(part.reshape(basis_count, per, slots))
        both = jnp.concatenate(parts, axis=1).astype(BF16)
        out[:, pl.ds(pl.multiple_of(pair * 2 * per, 2 * per), 2 * per), :] = both
        return 0

    lax.fori_loop(0, groups // 2, step, 0)


def edge_kernel(received, mixer, edge_msg, w_bil_t, w_up, w_atom_in, edge_mid, message):
    peers, rows, lanes = received.shape
    half = rows - 8
    width = w_bil_t.shape[0]
    basis_count = mixer.shape[0]
    got = received[:, :half, :].astype(F32)
    swapped = pltpu.roll(got.reshape(peers * half, lanes), width, 1).reshape(got.shape)
    low = iota(got.shape, 2) < width
    first = jnp.where(low, got, swapped)
    second = jnp.where(low, swapped, got)
    table = jnp.concatenate([first, second], axis=1).reshape(peers * 2 * half, lanes)
    low = iota(table.shape, 1) < width
    even = jnp.where(low, table, 0.0).astype(BF16)
    odd = jnp.where(low, 0.0, table).astype(BF16)
    mixed = [
        (dot(mixer[2 * k], even) + dot(mixer[2 * k + 1], odd)).astype(BF16)
        for k in range(basis_count // 2)
    ]
    mixed = jnp.concatenate(mixed, axis=1)
    trip = silu(dot_nt(mixed, w_bil_t[...])).astype(BF16)
    mid = (edge_msg[...].astype(F32) + dot(trip, w_up[...])).astype(BF16)
    edge_mid[...] = mid
    sent = dot(mid, w_atom_in[...]).T.astype(BF16)
    message[...] = sent.reshape(message.shape)


def target_kernel(received, hot):
    peers, rows, lanes = received.shape
    half = rows - 8
    atoms, total = hot.shape
    edges = total // peers
    count = edges // lanes
    ids = iota((atoms, lanes), 0)

    def step(peer, _):
        codes = received[pl.ds(peer, 1), half:, :].reshape(8, lanes).astype(F32)
        for i in range(count):
            atom = codes[i : i + 1] * 256.0 + codes[count + i : count + i + 1]
            where = pl.ds(pl.multiple_of(peer * edges + i * lanes, lanes), lanes)
            hot[:, where] = jnp.where(ids == atom.astype(jnp.int32), 1.0, 0.0).astype(BF16)
        return 0

    lax.fori_loop(0, peers, step, 0)


def sum_kernel(messages, hot, out):
    peers, feats, edges = messages.shape
    total = jnp.zeros(out.shape, F32)
    for p in range(peers):
        total += dot_nt(messages[p], hot[:, p * edges : (p + 1) * edges])
    out[...] = total.astype(BF16)


def atom_kernel(owners_of, feats, wanted_count, *refs):
    piece_count = len(owners_of)
    pieces = refs[:piece_count]
    gain, atom_h, w_atom, first = refs[piece_count : piece_count + 4]
    wanted = refs[piece_count + 4 : piece_count + 4 + wanted_count]
    atom_out = refs[piece_count + 4 + wanted_count]
    sent = refs[piece_count + 5 + wanted_count : -1]
    sums = refs[-1]
    me = first[1]
    for piece, owners in zip(pieces, owners_of):
        for i, owner in enumerate(owners):
            at = pl.multiple_of(owner(me) * feats, feats)
            sums[pl.ds(at, feats), :] = piece[i * feats : (i + 1) * feats, :].astype(F32)
    values = sums[...]
    scale = lax.rsqrt(jnp.mean(values * values, axis=0, keepdims=True) + 1e-06)
    normed = (values * scale).T * gain[...]
    grown = silu(dot(normed.astype(BF16), w_atom[...]))
    rows = (atom_h[...].astype(F32) + grown).astype(BF16)
    atom_out[...] = rows
    for want, send in zip(wanted, sent):
        local = column(want[...] - first[0])
        hot = local == iota((want.shape[1], rows.shape[0]), 1)
        send[...] = dot(jnp.where(hot, 1.0, 0.0).astype(BF16), rows).astype(BF16)


def local_kernel(atom_out, source, target, first, w_src, w_tgt, out):
    rows = atom_out[...]
    edges = source.shape[1]
    ids = iota((edges, rows.shape[0]), 1)

    def pick(index):
        hot = column(index[...] - first[0]) == ids
        return dot(jnp.where(hot, 1.0, 0.0).astype(BF16), rows).astype(BF16)

    out[...] = dot(pick(source), w_src[...]) + dot(pick(target), w_tgt[...])


def final_kernel(*refs):
    out = refs[-1]
    partial, edge_mid, w_src = refs[:3]
    rows = refs[3:-1]
    update = partial[...]
    if rows:
        got = rows[0][...].astype(F32)
        for r in rows[1:]:
            got = got + r[...].astype(F32)
        update = update + dot(got.astype(BF16), w_src[...])
    out[...] = (edge_mid[...].astype(F32) + silu(update)).astype(BF16)


def stage_factors(wide):
    stages = []
    left = wide
    size = min(4, max(1, wide // 4))
    stride = wide
    for f in (size, max(1, wide // (2 * size)), 2):
        if f > 1 and left % f == 0:
            stride //= f
            left //= f
            stages.append((stride, f))
    return stages


def per_device(
    wide,
    narrow,
    edge_msg,
    basis,
    atom_h,
    edge_source,
    edge_target,
    send_rows,
    trip_slot,
    w_down,
    w_bil,
    w_up,
    w_atom_in,
    atom_gain,
    w_atom,
    w_src,
    w_tgt,
):
    edges, de = edge_msg.shape
    width = w_down.shape[1]
    basis_count = w_bil.shape[0] // width
    triplets = trip_slot.shape[1]
    atoms, da = atom_h.shape
    slots = send_rows.shape[1]
    cap = slots // wide
    feats = da // wide
    lanes = 2 * width
    big = (24 << 20) if slots <= 512 else (60 << 20)
    shape = jax.ShapeDtypeStruct

    first_atom = lax.axis_index("narrow") * atoms
    place = jnp.stack([first_atom, lax.axis_index("wide")]).astype(jnp.int32)
    source = edge_source.reshape(1, edges)
    target = edge_target.reshape(1, edges)

    outgoing = call(
        outgoing_kernel, shape((wide, cap // 2 + 8, lanes), BF16), big, name="outgoing"
    )(edge_msg, w_down.T, send_rows, target - first_atom)
    received = lax.all_to_all(outgoing, "wide", split_axis=0, concat_axis=0, tiled=True)

    wanted = [
        lax.ppermute(source, "narrow", [(i, (i + k) % narrow) for i in range(narrow)])
        for k in range(1, narrow)
    ]
    per = 256 // triplets
    slots_flat = trip_slot.reshape(edges // per, per * triplets)
    mixer = call(
        mixer_kernel,
        shape((basis_count, edges, slots), BF16),
        big,
        scratch=[pltpu.VMEM((basis_count, edges, per * triplets), F32)],
        cost=cost(2 * basis_count * edges * slots * 256, 6 << 20),
        name="mixer",
    )(basis, slots_flat)

    edge_mid, message = call(
        edge_kernel,
        (shape((edges, de), BF16), shape((wide, feats, edges), BF16)),
        big,
        name="edge",
    )(received, mixer, edge_msg, w_bil.T, w_up, w_atom_in)
    messages = lax.all_to_all(message, "wide", split_axis=0, concat_axis=0, tiled=True)
    hot = call(
        target_kernel,
        shape((atoms, wide * edges), BF16),
        big,
        cost=cost(1 << 24, 5 << 20),
        name="targets",
    )(received)
    share = call(sum_kernel, shape((feats, atoms), BF16), big, name="sums")(messages, hot)

    groups = [(share, [lambda me: me])]
    stages = stage_factors(wide)
    for number, (stride, size) in enumerate(stages):
        def moved(k, stride=stride, size=size):
            def owner(me):
                place_in = (me // stride) % size
                return me + ((place_in + size - k) % size - place_in) * stride
            return owner

        fresh = []
        for value, owners in groups:
            got = [(value, owners)]
            for k in range(1, size):
                pairs = []
                for i in range(wide):
                    at = (i // stride) % size
                    pairs.append((i, i + ((at + k) % size - at) * stride))
                back = moved(k)
                got.append(
                    (
                        lax.ppermute(value, "wide", pairs),
                        [lambda me, o=o, back=back: o(back(me)) for o in owners],
                    )
                )
            if size > 2:
                fresh.append(
                    (
                        jnp.concatenate([v for v, _ in got], axis=0),
                        [o for _, os in got for o in os],
                    )
                )
            else:
                fresh.extend(got)
        groups = fresh

    smem = pl.BlockSpec(memory_space=pltpu.SMEM)
    vmem = pl.BlockSpec(memory_space=pltpu.VMEM)
    pieces = [v for v, _ in groups]
    owners_of = [o for _, o in groups]
    outs = pl.pallas_call(
        functools.partial(atom_kernel, owners_of, feats, len(wanted)),
        out_shape=[shape((atoms, da), BF16)] + [shape((edges, da), BF16)] * len(wanted),
        in_specs=[vmem] * (len(pieces) + 3) + [smem] + [vmem] * len(wanted),
        out_specs=[vmem] * (1 + len(wanted)),
        scratch_shapes=[pltpu.VMEM((da, atoms), F32)],
        compiler_params=pltpu.CompilerParams(vmem_limit_bytes=big),
        name="atoms",
    )(*pieces, atom_gain.reshape(1, da), atom_h, w_atom, place, *wanted)
    atom_out, asked = outs[0], outs[1:]
    rows = [
        lax.ppermute(a, "narrow", [(i, (i - k) % narrow) for i in range(narrow)])
        for k, a in enumerate(asked, start=1)
    ]
    partial = pl.pallas_call(
        local_kernel,
        out_shape=shape((edges, de), F32),
        in_specs=[vmem, vmem, vmem, smem, vmem, vmem],
        out_specs=vmem,
        compiler_params=pltpu.CompilerParams(vmem_limit_bytes=big),
        cost_estimate=cost(4 * edges * da * de + 4 * edges * da * atoms, 4 << 20),
        name="local",
    )(atom_out, source, target, place, w_src, w_tgt)
    edge_out = call(final_kernel, shape((edges, de), BF16), big, name="final")(
        partial, edge_mid, w_src, *rows
    )
    return (edge_out, atom_out)


def solution(mesh):
    placed = (
        P(("wide", "narrow"), None),
        P(("wide", "narrow"), None),
        P("narrow", None),
        P(("wide", "narrow")),
        P(("wide", "narrow")),
        P(("wide", "narrow"), None),
        P(("wide", "narrow"), None),
        P(),
        P(),
        P(),
        P(),
        P(),
        P(),
        P(),
        P(),
    )
    return jax.shard_map(
        functools.partial(per_device, mesh.shape["wide"], mesh.shape["narrow"]),
        mesh=mesh,
        in_specs=placed,
        out_specs=(P(("wide", "narrow"), None), P("narrow", None)),
        check_vma=False,
    )
```

time: 172 us -> 75.2 us (0.44)
  waiting for transfers between devices: 78.2 us -> 18.5 us
  blocking collectives: 22.2 us -> 0 us
  local copies, waits for them, and re-layouts: 34 us -> 14.7 us
  Pallas kernels: 0 us -> 18.8 us
  starting transfers between devices: 7.47 us -> 21 us
  matrix products: 13.5 us -> 0 us
  between operations: 14.3 us -> 0.83 us
    reduce_scatter x1 -> x0, waiting for transfers between devices: 55 us -> none  [per_device(): lax.psum_scatter(partial_sums, 'wide', scatter_dimension=0, tiled=True)]
    gather x3 -> x0, local copies, waits for them, and re-layouts: 27.9 us -> none  [the longest x1 24 us: per_device(): other = received[trip_slot]]
    all_gather x1 -> x0, blocking collectives: 22.2 us -> none  [per_device(): atom_out = lax.all_gather(updated, 'wide', axis=0, tiled=True)]
    pallas_call x0 -> x8, Pallas kernels: none -> 18.8 us  [the longest x1 5.95 us: per_device(): call(mixer_kernel, shape((basis_count, edges, slots), BF16), big, scratch...]
    all_gather x1 -> x0, waiting for transfers between devices: 18.7 us -> none  [per_device(): every_atom = lax.all_gather(atom_out, 'narrow', axis=0, tiled=True)]
    unnamed x24 -> x45, local copies, waits for them, and re-layouts: 0.99 us -> 14.6 us
    dot_general x7 -> x0, matrix products: 13.5 us -> none  [the longest x1 3.14 us: per_device(): jnp.dot(target_rows, w_tgt, preferred_element_type=jnp.float32)]
    ppermute x0 -> x8, waiting for transfers between devices: none -> 11.8 us  [the longest x6 6.78 us: per_device(): lax.ppermute(value, 'wide', pairs)]
  transfers between devices with their start and end apart: 3 -> 10, of which waited for: 3 -> 6; matrix products, arithmetic and copies ran while one was open for 1% -> 1% of each run, Pallas kernels for 0% -> 12%
where the time goes in v1:
time: 75.2 us; the launch traced here: 74.6 us
  starting transfers between devices  21 us (28%)
  Pallas kernels  18.8 us (25%)
  waiting for transfers between devices  18.5 us (25%)
  local copies, waits for them, and re-layouts  14.7 us (20%)
  between operations  0.83 us (1%)
  other arithmetic  0.77 us (1%)
    unnamed x45, local copies, waits for them, and re-layouts  14.6 us
    all_to_all x1, starting transfers between devices, per_device(): lax.all_to_all(outgoing, 'wide', split_axis=0, concat_axis=0, tiled=True)  7.39 us
    ppermute x6, waiting for transfers between devices, per_device(): lax.ppermute(value, 'wide', pairs)  6.78 us
    all_to_all x1, waiting for transfers between devices, per_device(): lax.all_to_all(message, 'wide', split_axis=0, concat_axis=0, tiled=True)  6.71 us
    all_to_all x1, starting transfers between devices, per_device(): lax.all_to_all(message, 'wide', split_axis=0, concat_axis=0, tiled=True)  5.99 us
    pallas_call x1, Pallas kernels, per_device(): call(mixer_kernel, shape((basis_count, edges, slots), BF16), big, scratch...  5.95 us
    ppermute x6, starting transfers between devices, per_device(): lax.ppermute(value, 'wide', pairs)  4.55 us
    ppermute x1, waiting for transfers between devices, per_device(): lax.ppermute(a, 'narrow', [(i, (i - k) % narrow) for i in range(narrow)])  3.08 us
  transfers between devices with their start and end apart: 10, of which 6 were waited for; matrix products, arithmetic and copies ran while one was open for 1% of the time, Pallas kernels for 12%

profile of v1, /device:TPU:0, one launch (start us, length us, event | category | flops | bytes accessed | tf_op | source)
XLA Modules:
  0.0 74.6 jit_solution(14710107303110384212)
XLA Ops:
  0.6 0.7 broadcast_subtract_fusion
  1.3 1.0 %copy-done.5 = bf16[256,1024]{1,0:T(8,128)(2,1)S(1)} copy-done((bf16[256,1024]{1,0:T(8,128)(2,1)S(1)}, bf16[256,1024]{1,0:T(8,128)(2,1)}, u32[]{:S(2)}) %copy-start.5) | copy-done | bytes 524312
  2.4 0.9 %copy-done.17 = bf16[1024,64]{0,1:T(8,128)(2,1)S(1)} copy-done((bf16[1024,64]{0,1:T(8,128)(2,1)S(1)}, bf16[1024,64]{0,1:T(8,128)(2,1)}, u32[]{:S(2)}) %copy-start.17) | copy-done | bytes 131096
  3.3 0.7 copy-done.19
  4.0 1.3 %outgoing.1 = bf16[16,24,128]{2,1,0:T(8,128)(2,1)} custom-call(bf16[256,1024]{1,0:T(8,128)(2,1)S(1)} %copy-done.5, bf16[64,1024]{1,0:T(8,128)(2,1)S(1)} %bitcast.9, s32[1,512]{1,0:T(1,128)S(1)} %copy-done.19, s32[1,256]{1,0:T(1,128)S(1)} %bitcast.11), custom_call_target="tpu_custom_call" | custom-call | tf_op jit(solution)/shard_map/outgoing/pallas_call | solution.py:261
  5.2 7.4 %all-to-all-start = ((bf16[16,24,128]{2,1,0:T(8,128)(2,1)}), bf16[16,24,128]{2,1,0:T(8,128)(2,1)S(1)}, u32[]{:S(2)}, u32[]{:S(2)}) async-start(bf16[16,24,128]{2,1,0:T(8,128)(2,1)} %outgoing.1), calls=%async_computation | async-start | bytes 196608 | tf_op jit(solution)/shard_map/all_to_all | solution.py:264
  12.6 0.9 %copy.18 = s32[256,32]{1,0:T(8,128)S(1)} copy(s32[256,32]{0,1:T(8,128)} %param.21) | data formatting | bytes 65536 | tf_op args[6]
  13.6 0.9 %copy-done.14 = bf16[256,512]{1,0:T(8,128)(2,1)S(1)} copy-done((bf16[256,512]{1,0:T(8,128)(2,1)S(1)}, bf16[256,512]{1,0:T(8,128)(2,1)}, u32[]{:S(2)}) %copy-start.14) | copy-done | bytes 262168
  14.6 5.9 %mixer.1 = bf16[16,256,512]{2,1,0:T(8,128)(2,1)S(1)} custom-call(bf16[256,512]{1,0:T(8,128)(2,1)S(1)} %copy-done.14, s32[32,256]{1,0:T(8,128)S(1)} %reshape.17.slots_flat), custom_call_target="tpu_custom_call" | custom-call | flops 1073741824 | bytes 6291456 | tf_op jit(solution)/shard_map/mixer/pallas_call | solution.py:272
  20.5 2.0 %copy-done = bf16[16,256,512]{2,1,0:T(8,128)(2,1)} copy-done((bf16[16,256,512]{2,1,0:T(8,128)(2,1)}, bf16[16,256,512]{2,1,0:T(8,128)(2,1)S(1)}, u32[]{:S(2)}) %copy-start) | copy-done | bytes 4194328
  22.5 2.2 %copy-done.1 = bf16[16,256,512]{2,1,0:T(8,128)(2,1)S(1)} copy-done((bf16[16,256,512]{2,1,0:T(8,128)(2,1)S(1)}, bf16[16,256,512]{2,1,0:T(8,128)(2,1)}, u32[]{:S(2)}) %copy-start.1) | copy-done | bytes 4194328
  24.7 3.0 %edge.1 = (bf16[256,1024]{1,0:T(8,128)(2,1)S(1)}, bf16[16,32,256]{2,1,0:T(8,128)(2,1)}) custom-call(bf16[16,24,128]{2,1,0:T(8,128)(2,1)S(1)} %all-to-all-done.received, bf16[16,256,512]{2,1,0:T(8,128)(2,1)S(1)} %copy-done.1, bf16[256,1024]{1,0:T(8,128)(2,1)S(1)} %copy-done.6, bf16[64,1024]{1,0:T(8,128)(2,1)S(1)} %bitcast.8, bf16[64,1024]{1,0:T(8,128)(2,1)S(1)} %copy-done.16, ...), custom_call_target="tpu_custom_call" | custom-call | tf_op jit(solution)/shard_map/edge/pallas_call | solution.py:281
  27.7 0.8 %copy-done.12 = bf16[256,1024]{1,0:T(8,128)(2,1)} copy-done((bf16[256,1024]{1,0:T(8,128)(2,1)}, bf16[256,1024]{1,0:T(8,128)(2,1)S(1)}, u32[]{:S(2)}) %copy-start.12) | copy-done | bytes 524312
  28.5 6.0 %all-to-all-start.1 = ((bf16[16,32,256]{2,1,0:T(8,128)(2,1)}), bf16[16,32,256]{2,1,0:T(8,128)(2,1)S(1)}, u32[]{:S(2)}, u32[]{:S(2)}) async-start(bf16[16,32,256]{2,1,0:T(8,128)(2,1)} %get-tuple-element.6), calls=%async_computation.1 | async-start | bytes 524288 | tf_op jit(solution)/shard_map/all_to_all | solution.py:287
  34.5 1.3 %targets.1.hot = bf16[512,4096]{1,0:T(8,128)(2,1)S(1)} custom-call(bf16[16,24,128]{2,1,0:T(8,128)(2,1)S(1)} %all-to-all-done.received), custom_call_target="tpu_custom_call" | custom-call | flops 16777216 | bytes 5242880 | tf_op jit(solution)/shard_map/targets/pallas_call | solution.py:288
  35.8 2.0 %copy-done.2 = bf16[512,4096]{1,0:T(8,128)(2,1)} copy-done((bf16[512,4096]{1,0:T(8,128)(2,1)}, bf16[512,4096]{1,0:T(8,128)(2,1)S(1)}, u32[]{:S(2)}) %copy-start.2) | copy-done | bytes 4194328
  37.8 6.7 %all-to-all-done.1.messages = bf16[16,32,256]{2,1,0:T(8,128)(2,1)S(1)} async-done(((bf16[16,32,256]{2,1,0:T(8,128)(2,1)}), bf16[16,32,256]{2,1,0:T(8,128)(2,1)S(1)}, u32[]{:S(2)}, u32[]{:S(2)}) %all-to-all-start.1) | async-done | bytes 262176 | tf_op jit(solution)/shard_map/all_to_all | solution.py:287
  44.5 2.2 %copy-done.3 = bf16[512,4096]{1,0:T(8,128)(2,1)S(1)} copy-done((bf16[512,4096]{1,0:T(8,128)(2,1)S(1)}, bf16[512,4096]{1,0:T(8,128)(2,1)}, u32[]{:S(2)}) %copy-start.3) | copy-done | bytes 4194328
  46.7 1.3 %sums.1 = bf16[32,512]{1,0:T(8,128)(2,1)S(1)} custom-call(bf16[16,32,256]{2,1,0:T(8,128)(2,1)S(1)} %all-to-all-done.1.messages, bf16[512,4096]{1,0:T(8,128)(2,1)S(1)} %copy-done.3), custom_call_target="tpu_custom_call" | custom-call | tf_op jit(solution)/shard_map/sums/pallas_call | solution.py:295
  48.0 1.5 %collective-permute-start.1 = (bf16[32,512]{1,0:T(8,128)(2,1)S(1)}, bf16[32,512]{1,0:T(8,128)(2,1)S(1)}, u32[]{:S(2)}, u32[]{:S(2)}) collective-permute-start(bf16[32,512]{1,0:T(8,128)(2,1)S(1)} %sums.1), channel_id=1, source_target_pairs={{0,16},{2,18},{4,20},{6,22},{8,24},{10,26},{12,28},{14,30},{16,0},... | collective-permute-start | bytes 98312 | tf_op jit(solution)/shard_map/ppermute | solution.py:317
  49.6 2.4 %collective-permute-start.2 = (bf16[32,512]{1,0:T(8,128)(2,1)S(1)}, bf16[32,512]{1,0:T(8,128)(2,1)S(1)}, u32[]{:S(2)}, u32[]{:S(2)}) collective-permute-start(bf16[32,512]{1,0:T(8,128)(2,1)S(1)} %sums.1), channel_id=1, source_target_pairs={{0,24},{2,26},{4,28},{6,30},{8,0},{10,2},{12,4},{14,6},{16,8},{18,... | collective-permute-start | bytes 98312 | tf_op jit(solution)/shard_map/ppermute | solution.py:317
  52.0 1.8 %collective-permute-done = bf16[32,512]{1,0:T(8,128)(2,1)S(1)} collective-permute-done((bf16[32,512]{1,0:T(8,128)(2,1)S(1)}, bf16[32,512]{1,0:T(8,128)(2,1)S(1)}, u32[]{:S(2)}, u32[]{:S(2)}) %collective-permute-start) | collective-permute-done | bytes 32800 | tf_op jit(solution)/shard_map/ppermute | solution.py:317
  54.3 0.6 collective-permute-start.4
  54.9 4.5 %collective-permute-done.4.refs_2_ = bf16[128,512]{1,0:T(8,128)(2,1)S(1)} collective-permute-done((bf16[128,512]{1,0:T(8,128)(2,1)S(1)}, bf16[128,512]{1,0:T(8,128)(2,1)S(1)}, u32[]{:S(2)}, u32[]{:S(2)}) %collective-permute-start.4) | collective-permute-done | bytes 131104 | tf_op jit(solution)/shard_map/ppermute | solution.py:317
  59.4 1.5 %collective-permute-start.6 = (s32[1,256]{1,0:T(1,128)S(1)}, s32[1,256]{1,0:T(1,128)S(1)}, u32[]{:S(2)}, u32[]{:S(2)}) collective-permute-start(s32[1,256]{1,0:T(1,128)S(1)} %bitcast.13), channel_id=1, source_target_pairs={{0,1},{1,0},{2,3},{3,2},{4,5},{5,4},{6,7},{7,6},{8,9},{9,8},{10,11... | collective-permute-start | bytes 3080 | tf_op jit(solution)/shard_map/ppermute | solution.py:267
  61.0 2.0 %collective-permute-done.6.refs_8_ = s32[1,256]{1,0:T(1,128)S(1)} collective-permute-done((s32[1,256]{1,0:T(1,128)S(1)}, s32[1,256]{1,0:T(1,128)S(1)}, u32[]{:S(2)}, u32[]{:S(2)}) %collective-permute-start.6) | collective-permute-done | bytes 1056 | tf_op jit(solution)/shard_map/ppermute | solution.py:267
  63.0 2.7 %atoms.1 = (bf16[512,512]{1,0:T(8,128)(2,1)}, bf16[256,512]{1,0:T(8,128)(2,1)S(1)}) custom-call(bf16[128,512]{1,0:T(8,128)(2,1)S(1)} %pad_maximum_fusion.refs_0_, bf16[128,512]{1,0:T(8,128)(2,1)S(1)} %collective-permute-done.3.refs_1_, bf16[128,512]{1,0:T(8,128)(2,1)S(1)} %collective-permute-done.4.refs_2_, bf16[128,512]{1,0:T(8,128)(2,1)} %collective-permute-done.5.refs_3_, ...), custom_call_target="tpu_custom_call" | custom-call | tf_op jit(solution)/shard_map/atoms/pallas_call | solution.py:336
  65.6 1.5 %collective-permute-start.7 = (bf16[256,512]{1,0:T(8,128)(2,1)S(1)}, bf16[256,512]{1,0:T(8,128)(2,1)S(1)}, u32[]{:S(2)}, u32[]{:S(2)}) collective-permute-start(bf16[256,512]{1,0:T(8,128)(2,1)S(1)} %get-tuple-element.9), channel_id=1, source_target_pairs={{0,1},{1,0},{2,3},{3,2},{4,5},{5,4},{6,7},{7,6},{8,9},{9,8},{10,11... | collective-permute-start | bytes 786440 | tf_op jit(solution)/shard_map/ppermute | solution.py:347
  67.2 1.0 %copy-done.9 = bf16[512,512]{1,0:T(8,128)(2,1)S(1)} copy-done((bf16[512,512]{1,0:T(8,128)(2,1)S(1)}, bf16[512,512]{1,0:T(8,128)(2,1)}, u32[]{:S(2)}) %copy-start.9) | copy-done | bytes 524312
  68.2 1.9 %local.1.refs_0_ = f32[256,1024]{1,0:T(8,128)S(1)} custom-call(bf16[512,512]{1,0:T(8,128)(2,1)S(1)} %copy-done.9, s32[1,256]{1,0:T(1,128)S(1)} %bitcast.14, s32[1,256]{1,0:T(1,128)S(1)} %bitcast.10, s32[2]{0:T(128)S(1)} %pad_add_fusion.refs_7_.first, bf16[512,1024]{1,0:T(8,128)(2,1)S(1)} %copy-done.4, bf16[512,1024]{1,0:T(8,128)(2,1)S(1)} %copy-done.7), custom_call_target="tpu_custom_call" | custom-call | flops 805306368 | bytes 4194304 | tf_op jit(solution)/shard_map/local/pallas_call | solution.py:350
  70.1 3.1 %collective-permute-done.7.refs_3_ = bf16[256,512]{1,0:T(8,128)(2,1)S(1)} collective-permute-done((bf16[256,512]{1,0:T(8,128)(2,1)S(1)}, bf16[256,512]{1,0:T(8,128)(2,1)S(1)}, u32[]{:S(2)}, u32[]{:S(2)}) %collective-permute-start.7) | collective-permute-done | bytes 262176 | tf_op jit(solution)/shard_map/ppermute | solution.py:347
  73.2 1.4 %final.1 = bf16[256,1024]{1,0:T(8,128)(2,1)} custom-call(f32[256,1024]{1,0:T(8,128)S(1)} %local.1.refs_0_, bf16[256,1024]{1,0:T(8,128)(2,1)S(1)} %copy-done.13, bf16[512,1024]{1,0:T(8,128)(2,1)S(1)} %copy-done.4, bf16[256,512]{1,0:T(8,128)(2,1)S(1)} %collective-permute-done.7.refs_3_), custom_call_target="tpu_custom_call" | custom-call | tf_op jit(solution)/shard_map/final/pallas_call | solution.py:359
  (45 shorter events, 0.8 us)
Async XLA Ops:
  1.3 1.0 %copy-start.5 = (bf16[256,1024]{1,0:T(8,128)(2,1)S(1)}, bf16[256,1024]{1,0:T(8,128)(2,1)}, u32[]{:S(2)}) copy-start(bf16[256,1024]{1,0:T(8,128)(2,1)} %edge_msg.3) | copy-start | bytes 1572868
  2.4 0.9 %copy-start.17 = (bf16[1024,64]{0,1:T(8,128)(2,1)S(1)}, bf16[1024,64]{0,1:T(8,128)(2,1)}, u32[]{:S(2)}) copy-start(bf16[1024,64]{0,1:T(8,128)(2,1)} %param.22) | copy-start | bytes 393220
  3.3 0.7 copy-start.19
  3.9 18.5 %copy-start.6 = (bf16[256,1024]{1,0:T(8,128)(2,1)S(1)}, bf16[256,1024]{1,0:T(8,128)(2,1)}, u32[]{:S(2)}) copy-start(bf16[256,1024]{1,0:T(8,128)(2,1)} %edge_msg.3) | copy-start | bytes 1572868
  3.9 18.5 %copy-start.8 = (bf16[1024,512]{1,0:T(8,128)(2,1)S(1)}, bf16[1024,512]{1,0:T(8,128)(2,1)}, u32[]{:S(2)}) copy-start(bf16[1024,512]{1,0:T(8,128)(2,1)} %w_atom_in.1) | copy-start | bytes 3145732
  5.2 17.2 %all-to-all-start = ((bf16[16,24,128]{2,1,0:T(8,128)(2,1)}), bf16[16,24,128]{2,1,0:T(8,128)(2,1)S(1)}, u32[]{:S(2)}, u32[]{:S(2)}) async-start(bf16[16,24,128]{2,1,0:T(8,128)(2,1)} %outgoing.1), calls=%async_computation | async-start | bytes 196608 | tf_op jit(solution)/shard_map/all_to_all | solution.py:264
  13.6 1.0 %copy-start.14 = (bf16[256,512]{1,0:T(8,128)(2,1)S(1)}, bf16[256,512]{1,0:T(8,128)(2,1)}, u32[]{:S(2)}) copy-start(bf16[256,512]{1,0:T(8,128)(2,1)} %basis.1) | copy-start | bytes 786436
  14.6 7.9 %copy-start.15 = (bf16[1024,64]{0,1:T(8,128)(2,1)S(1)}, bf16[1024,64]{0,1:T(8,128)(2,1)}, u32[]{:S(2)}) copy-start(bf16[1024,64]{0,1:T(8,128)(2,1)} %param.23) | copy-start | bytes 393220
  14.6 8.0 %copy-start.16 = (bf16[64,1024]{1,0:T(8,128)(2,1)S(1)}, bf16[64,1024]{1,0:T(8,128)(2,1)}, u32[]{:S(2)}) copy-start(bf16[64,1024]{1,0:T(8,128)(2,1)} %w_up.1) | copy-start | bytes 393220
  20.5 2.0 %copy-start = (bf16[16,256,512]{2,1,0:T(8,128)(2,1)}, bf16[16,256,512]{2,1,0:T(8,128)(2,1)S(1)}, u32[]{:S(2)}) copy-start(bf16[16,256,512]{2,1,0:T(8,128)(2,1)S(1)} %mixer.1) | copy-start | bytes 12582916
  22.5 2.2 %copy-start.1 = (bf16[16,256,512]{2,1,0:T(8,128)(2,1)S(1)}, bf16[16,256,512]{2,1,0:T(8,128)(2,1)}, u32[]{:S(2)}) copy-start(bf16[16,256,512]{2,1,0:T(8,128)(2,1)} %copy-done) | copy-start | bytes 12582916
  27.7 0.8 %copy-start.12 = (bf16[256,1024]{1,0:T(8,128)(2,1)}, bf16[256,1024]{1,0:T(8,128)(2,1)S(1)}, u32[]{:S(2)}) copy-start(bf16[256,1024]{1,0:T(8,128)(2,1)S(1)} %get-tuple-element.8.refs_1_) | copy-start | bytes 1572868
  28.5 16.0 %all-to-all-start.1 = ((bf16[16,32,256]{2,1,0:T(8,128)(2,1)}), bf16[16,32,256]{2,1,0:T(8,128)(2,1)S(1)}, u32[]{:S(2)}, u32[]{:S(2)}) async-start(bf16[16,32,256]{2,1,0:T(8,128)(2,1)} %get-tuple-element.6), calls=%async_computation.1 | async-start | bytes 524288 | tf_op jit(solution)/shard_map/all_to_all | solution.py:287
  34.5 24.9 %copy-start.21 = (s32[256]{0:T(256)S(1)}, s32[256]{0:T(256)}, u32[]{:S(2)}) copy-start(s32[256]{0:T(256)} %param.18) | copy-start | bytes 3076
  34.5 28.5 %copy-start.10 = (bf16[512,512]{1,0:T(8,128)(2,1)S(1)}, bf16[512,512]{1,0:T(8,128)(2,1)}, u32[]{:S(2)}) copy-start(bf16[512,512]{1,0:T(8,128)(2,1)} %refs_5_.1) | copy-start | bytes 1572868
  34.5 28.5 %copy-start.11 = (bf16[512,512]{1,0:T(8,128)(2,1)S(1)}, bf16[512,512]{1,0:T(8,128)(2,1)}, u32[]{:S(2)}) copy-start(bf16[512,512]{1,0:T(8,128)(2,1)} %refs_6_.1) | copy-start | bytes 1572868
  34.5 28.5 %copy-start.20 = (f32[512]{0:T(512)S(1)}, f32[512]{0:T(512)}, u32[]{:S(2)}) copy-start(f32[512]{0:T(512)} %param.26) | copy-start | bytes 6148
  35.8 2.0 %copy-start.2 = (bf16[512,4096]{1,0:T(8,128)(2,1)}, bf16[512,4096]{1,0:T(8,128)(2,1)S(1)}, u32[]{:S(2)}) copy-start(bf16[512,4096]{1,0:T(8,128)(2,1)S(1)} %targets.1.hot) | copy-start | bytes 12582916
  44.5 2.2 %copy-start.3 = (bf16[512,4096]{1,0:T(8,128)(2,1)S(1)}, bf16[512,4096]{1,0:T(8,128)(2,1)}, u32[]{:S(2)}) copy-start(bf16[512,4096]{1,0:T(8,128)(2,1)} %copy-done.2) | copy-start | bytes 12582916
  46.7 20.5 %copy-start.4 = (bf16[512,1024]{1,0:T(8,128)(2,1)S(1)}, bf16[512,1024]{1,0:T(8,128)(2,1)}, u32[]{:S(2)}) copy-start(bf16[512,1024]{1,0:T(8,128)(2,1)} %refs_2_.1) | copy-start | bytes 3145732
  46.7 20.5 %copy-start.7 = (bf16[512,1024]{1,0:T(8,128)(2,1)S(1)}, bf16[512,1024]{1,0:T(8,128)(2,1)}, u32[]{:S(2)}) copy-start(bf16[512,1024]{1,0:T(8,128)(2,1)} %w_tgt.1) | copy-start | bytes 3145732
  46.7 20.5 %copy-start.18 = (s32[256]{0:T(256)S(1)}, s32[256]{0:T(256)}, u32[]{:S(2)}) copy-start(s32[256]{0:T(256)} %param.19) | copy-start | bytes 3076
  48.0 5.8 %collective-permute-start = (bf16[32,512]{1,0:T(8,128)(2,1)S(1)}, bf16[32,512]{1,0:T(8,128)(2,1)S(1)}, u32[]{:S(2)}, u32[]{:S(2)}) collective-permute-start(bf16[32,512]{1,0:T(8,128)(2,1)S(1)} %sums.1), channel_id=1, source_target_pairs={{0,8},{2,10},{4,12},{6,14},{8,16},{10,18},{12,20},{14,22},{16,24},... | collective-permute-start | bytes 98312 | tf_op jit(solution)/shard_map/ppermute | solution.py:317
  48.0 5.8 %collective-permute-start.1 = (bf16[32,512]{1,0:T(8,128)(2,1)S(1)}, bf16[32,512]{1,0:T(8,128)(2,1)S(1)}, u32[]{:S(2)}, u32[]{:S(2)}) collective-permute-start(bf16[32,512]{1,0:T(8,128)(2,1)S(1)} %sums.1), channel_id=1, source_target_pairs={{0,16},{2,18},{4,20},{6,22},{8,24},{10,26},{12,28},{14,30},{16,0},... | collective-permute-start | bytes 98312 | tf_op jit(solution)/shard_map/ppermute | solution.py:317
  49.6 4.7 %collective-permute-start.2 = (bf16[32,512]{1,0:T(8,128)(2,1)S(1)}, bf16[32,512]{1,0:T(8,128)(2,1)S(1)}, u32[]{:S(2)}, u32[]{:S(2)}) collective-permute-start(bf16[32,512]{1,0:T(8,128)(2,1)S(1)} %sums.1), channel_id=1, source_target_pairs={{0,24},{2,26},{4,28},{6,30},{8,0},{10,2},{12,4},{14,6},{16,8},{18,... | collective-permute-start | bytes 98312 | tf_op jit(solution)/shard_map/ppermute | solution.py:317
  54.3 5.0 %collective-permute-start.4 = (bf16[128,512]{1,0:T(8,128)(2,1)S(1)}, bf16[128,512]{1,0:T(8,128)(2,1)S(1)}, u32[]{:S(2)}, u32[]{:S(2)}) collective-permute-start(bf16[128,512]{1,0:T(8,128)(2,1)S(1)} %pad_maximum_fusion.refs_0_), channel_id=1, source_target_pairs={{0,4},{2,6},{4,0},{6,2},{8,12},{10,14},{12,8},{14,10},{16,20},{18,... | collective-permute-start | bytes 393224 | tf_op jit(solution)/shard_map/ppermute | solution.py:317
  54.9 8.1 %collective-permute-start.3 = (bf16[128,512]{1,0:T(8,128)(2,1)S(1)}, bf16[128,512]{1,0:T(8,128)(2,1)S(1)}, u32[]{:S(2)}, u32[]{:S(2)}) collective-permute-start(bf16[128,512]{1,0:T(8,128)(2,1)S(1)} %pad_maximum_fusion.refs_0_), channel_id=1, source_target_pairs={{0,2},{2,0},{4,6},{6,4},{8,10},{10,8},{12,14},{14,12},{16,18},{18,... | collective-permute-start | bytes 393224 | tf_op jit(solution)/shard_map/ppermute | solution.py:317
  59.4 3.6 %collective-permute-start.5 = (bf16[128,512]{1,0:T(8,128)(2,1)S(1)}, bf16[128,512]{1,0:T(8,128)(2,1)}, u32[]{:S(2)}, u32[]{:S(2)}) collective-permute-start(bf16[128,512]{1,0:T(8,128)(2,1)S(1)} %collective-permute-done.4.refs_2_), channel_id=1, source_target_pairs={{0,2},{2,0},{4,6},{6,4},{8,10},{10,8},{12,14},{14,12},{16,18},{18,... | collective-permute-start | bytes 393224 | tf_op jit(solution)/shard_map/ppermute | solution.py:317
  59.4 3.6 %collective-permute-start.6 = (s32[1,256]{1,0:T(1,128)S(1)}, s32[1,256]{1,0:T(1,128)S(1)}, u32[]{:S(2)}, u32[]{:S(2)}) collective-permute-start(s32[1,256]{1,0:T(1,128)S(1)} %bitcast.13), channel_id=1, source_target_pairs={{0,1},{1,0},{2,3},{3,2},{4,5},{5,4},{6,7},{7,6},{8,9},{9,8},{10,11... | collective-permute-start | bytes 3080 | tf_op jit(solution)/shard_map/ppermute | solution.py:267
  60.9 12.3 %copy-start.13 = (bf16[256,1024]{1,0:T(8,128)(2,1)S(1)}, bf16[256,1024]{1,0:T(8,128)(2,1)}, u32[]{:S(2)}) copy-start(bf16[256,1024]{1,0:T(8,128)(2,1)} %copy-done.12) | copy-start | bytes 1572868
  65.6 7.6 %collective-permute-start.7 = (bf16[256,512]{1,0:T(8,128)(2,1)S(1)}, bf16[256,512]{1,0:T(8,128)(2,1)S(1)}, u32[]{:S(2)}, u32[]{:S(2)}) collective-permute-start(bf16[256,512]{1,0:T(8,128)(2,1)S(1)} %get-tuple-element.9), channel_id=1, source_target_pairs={{0,1},{1,0},{2,3},{3,2},{4,5},{5,4},{6,7},{7,6},{8,9},{9,8},{10,11... | collective-permute-start | bytes 786440 | tf_op jit(solution)/shard_map/ppermute | solution.py:347
  67.2 1.0 %copy-start.9 = (bf16[512,512]{1,0:T(8,128)(2,1)S(1)}, bf16[512,512]{1,0:T(8,128)(2,1)}, u32[]{:S(2)}) copy-start(bf16[512,512]{1,0:T(8,128)(2,1)} %get-tuple-element.5.atom_out) | copy-start | bytes 1572868

commit v2 on v1

v2 whole, which is shorter than its diff:
```python
import functools

import jax
import jax.numpy as jnp
from jax import lax
from jax.experimental import pallas as pl
from jax.experimental.pallas import tpu as pltpu
from jax.sharding import PartitionSpec as P

F32 = jnp.float32
BF16 = jnp.bfloat16
NT = (((1,), (1,)), ((), ()))


def silu(value):
    return value / (1.0 + jnp.exp(-value))


def dot(a, b):
    return jnp.dot(a, b, preferred_element_type=F32)


def dot_nt(a, b):
    return lax.dot_general(a, b, NT, preferred_element_type=F32)


def iota(shape, dim):
    return lax.broadcasted_iota(jnp.int32, shape, dim)


def column(row):
    return jnp.broadcast_to(row, (8, row.shape[1])).T[:, :1]


VMEM = pl.BlockSpec(memory_space=pltpu.VMEM)
HBM = pl.BlockSpec(memory_space=pltpu.HBM)


def call(kernel, ins, outs, out_shape, vmem, scratch=(), cost=None, name=None):
    def kept(spec, leaf):
        return pltpu.HBM(leaf.shape, leaf.dtype) if spec is HBM else leaf

    many = isinstance(out_shape, (list, tuple))
    out_shape = [kept(o, s) for o, s in zip(outs, out_shape)] if many else kept(outs, out_shape)
    run = pl.pallas_call(
        kernel,
        out_shape=out_shape,
        in_specs=list(ins),
        out_specs=outs,
        scratch_shapes=list(scratch),
        compiler_params=pltpu.CompilerParams(vmem_limit_bytes=vmem),
        cost_estimate=cost,
        name=name,
    )

    def apply(*args):
        held = [
            pltpu.with_memory_space_constraint(a, pltpu.HBM) if spec is HBM else a
            for spec, a in zip(ins, args)
        ]
        return run(*held)

    return apply


def cost(flops, moved):
    return pl.CostEstimate(flops=int(flops), bytes_accessed=int(moved), transcendentals=0)


def place(axis, size):
    return lax.axis_index(axis) * size


def one_hot(index, count):
    hot = column(index) == iota((index.shape[1], count), 1)
    return jnp.where(hot, 1.0, 0.0).astype(BF16)


def outgoing_kernel(atoms, edge_hbm, w_hbm, rows_hbm, target_hbm, out, edge, w, rows, target, sems):
    edges = edge.shape[0]
    width = w.shape[0]
    peers, block, lanes = out.shape
    half = block - 8
    slots = peers * half * 2
    chunks = sems.shape[0] - 3
    step = edges // chunks
    copies = [
        pltpu.make_async_copy(rows_hbm, rows, sems.at[0]),
        pltpu.make_async_copy(target_hbm, target, sems.at[1]),
        pltpu.make_async_copy(w_hbm, w, sems.at[2]),
    ]
    for i in range(chunks):
        part = pl.ds(i * step, step)
        copies.append(pltpu.make_async_copy(edge_hbm.at[part, :], edge.at[part, :], sems.at[3 + i]))
    for c in copies:
        c.start()
    copies[0].wait()
    copies[1].wait()
    hot = one_hot(rows[...], edges)
    local = target[...] - place("narrow", atoms)
    count = edges // lanes
    codes = [lax.shift_right_logical(local, 8), lax.bitwise_and(local, 255)]
    parts = [c[:, i * lanes : (i + 1) * lanes] for c in codes for i in range(count)]
    parts += [jnp.zeros_like(parts[0])] * (8 - len(parts))
    code_rows = jnp.concatenate(parts, axis=0).astype(F32)
    out[:, half:, :] = jnp.broadcast_to(code_rows[None], (peers, 8, lanes)).astype(BF16)
    copies[2].wait()
    down_w = w[...]
    twice = jnp.concatenate([down_w, down_w], axis=0)
    down = []
    for i in range(chunks):
        copies[3 + i].wait()
        down.append(silu(dot_nt(edge[i * step : (i + 1) * step, :], twice)).astype(BF16))
    picked = dot(hot, jnp.concatenate(down, axis=0))
    picked = picked.reshape(peers, 2 * half, lanes)
    low = iota((peers, half, lanes), 2) < width
    packed = jnp.where(low, picked[:, :half], picked[:, half:])
    out[:, :half, :] = packed.astype(BF16)


def start_first(copies):
    def go(_, carry):
        for c in copies:
            c.start()
        return carry

    lax.fori_loop(0, jnp.minimum(lax.axis_index("wide"), 0) + 1, go, 0)


def mixer_kernel(
    cap, basis_hbm, slots_hbm, kept, rest_hbm, basis, slots_t, flat, spread, rest, sems
):
    kept_count, edges, slots = kept.shape
    basis_count = kept_count + rest_hbm.shape[0]
    triplets = slots_t.shape[0]
    groups, span = flat.shape
    per = edges // groups
    total = basis.shape[1]
    fetch = [
        pltpu.make_async_copy(slots_hbm, slots_t, sems.at[0]),
        pltpu.make_async_copy(basis_hbm, basis, sems.at[1]),
    ]
    start_first(fetch)
    rows, cols = iota((total, total), 0), iota((total, total), 1)
    order = (rows // basis_count == cols % triplets) & (rows % basis_count == cols // triplets)
    order = jnp.where(order, 1.0, 0.0).astype(BF16)
    own = iota((edges, span), 0) % per == iota((edges, span), 1) // triplets
    fetch[0].wait()
    half = cap // 2
    slot = slots_t[...]
    slot = (slot // half) % 2 * (slots // 2) + slot // cap * half + slot % half
    slot = slot.T
    tile = jnp.where(iota((triplets, span), 0) == iota((triplets, span), 1) % triplets, 1.0, 0.0)
    tile = tile.astype(BF16)
    high = lax.shift_right_logical(slot, 8).astype(F32).astype(BF16)
    low = lax.bitwise_and(slot, 255).astype(F32).astype(BF16)
    wide = jnp.where(own, dot(high, tile) * 256.0 + dot(low, tile), 0.0)
    flat[...] = jnp.sum(wide.reshape(groups, per, span), axis=1).astype(jnp.int32)
    fetch[1].wait()
    by_basis = dot(basis[...], order).astype(BF16)
    pack = 128 // triplets
    rows, cols = iota((128, span), 0), iota((128, span), 1)
    for j in range(pack):
        tile = (rows // triplets == j) & (rows % triplets == cols % triplets)
        tile = jnp.where(tile, 1.0, 0.0).astype(BF16)
        for q in range(basis_count // pack):
            wide = dot(by_basis[:, q * 128 : (q + 1) * 128], tile)
            spread[q * pack + j] = jnp.where(own, wide, 0.0)

    def one(pair):
        parts = []
        for h in range(2):
            group = pair * 2 + h
            left = spread[:, pl.ds(pl.multiple_of(group * per, per), per), :]
            left = left.reshape(basis_count * per, span).astype(BF16)
            hot = iota((slots, span), 0) == flat[pl.ds(group, 1), :]
            part = dot_nt(left, jnp.where(hot, 1.0, 0.0).astype(BF16))
            parts.append(part.reshape(basis_count, per, slots))
        both = jnp.concatenate(parts, axis=1).astype(BF16)
        at = pl.ds(pl.multiple_of(pair * 2 * per, 2 * per), 2 * per)
        kept[:, at, :] = both[:kept_count]
        rest[:, at, :] = both[kept_count:]

    def step(i, _):
        one(2 * i)
        one(2 * i + 1)
        return 0

    chunks = sems.shape[0] - 2
    steps = groups // 4 // chunks
    copies = []
    for c in range(chunks):
        lax.fori_loop(c * steps, (c + 1) * steps, step, 0)
        part = pl.ds(c * steps * 4 * per, steps * 4 * per)
        copies.append(
            pltpu.make_async_copy(rest.at[:, part, :], rest_hbm.at[:, part, :], sems.at[2 + c])
        )
        copies[-1].start()
    for c in copies:
        c.wait()


def edge_kernel(
    received,
    kept,
    rest_hbm,
    edge_hbm,
    w_bil_hbm,
    w_up_hbm,
    w_atom_hbm,
    mid_hbm,
    message,
    rest,
    edge_msg,
    w_bil_t,
    w_up,
    w_atom_in,
    edge_mid,
    sems,
):
    peers, rows, lanes = received.shape
    half = rows - 8
    width = w_bil_t.shape[0]
    pairs = [
        (rest_hbm, rest),
        (w_bil_hbm, w_bil_t),
        (w_up_hbm, w_up),
        (edge_hbm, edge_msg),
        (w_atom_hbm, w_atom_in),
    ]
    copies = [pltpu.make_async_copy(a, b, sems.at[i]) for i, (a, b) in enumerate(pairs)]
    start_first(copies)
    got = received[:, :half, :].astype(F32).reshape(peers * half, lanes).T
    table = jnp.concatenate([got[:width], got[width:]], axis=1).astype(BF16)
    mixed = [dot_nt(table, kept[k]).astype(BF16) for k in range(kept.shape[0])]
    copies[0].wait()
    mixed += [dot_nt(table, rest[k]).astype(BF16) for k in range(rest.shape[0])]
    mixed = jnp.concatenate(mixed, axis=0)
    copies[1].wait()
    trip = silu(dot(w_bil_t[...], mixed)).T.astype(BF16)
    copies[2].wait()
    copies[3].wait()
    mid = (edge_msg[...].astype(F32) + dot(trip, w_up[...])).astype(BF16)
    edge_mid[...] = mid
    store = pltpu.make_async_copy(edge_mid, mid_hbm, sems.at[len(pairs)])
    store.start()
    copies[4].wait()
    sent = dot(mid, w_atom_in[...]).T.astype(BF16)
    message[...] = sent.reshape(message.shape)
    store.wait()


def picks_kernel(count, *refs):
    wanted = refs[:count]
    atom_h = refs[count]
    hots, olds = refs[count + 1 : 2 * count + 1], refs[2 * count + 1 :]
    atoms = atom_h.shape[0]
    for want, hot, old in zip(wanted, hots, olds):
        chosen = one_hot(want[...] - place("narrow", atoms), atoms)
        hot[...] = chosen
        old[...] = dot(chosen, atom_h[...]).astype(BF16)


def sum_kernel(messages, received, *refs):
    out = refs[-1]
    peers, feats, edges = messages.shape
    _, rows, lanes = received.shape
    half = rows - 8
    count = edges // lanes
    total = jnp.zeros(out.shape, F32)
    ids = iota((out.shape[1], lanes), 0).astype(F32)
    for p in range(peers):
        codes = received[p, half:, :].astype(F32)
        hot = [
            jnp.where(ids == codes[i : i + 1] * 256.0 + codes[count + i : count + i + 1], 1.0, 0.0)
            for i in range(count)
        ]
        total += dot_nt(messages[p], jnp.concatenate(hot, axis=1).astype(BF16))
    out[...] = total.astype(BF16)


def asked_kernel(owners_of, feats, count, *refs):
    pieces = refs[: len(owners_of)]
    gain, w_atom = refs[len(owners_of) : len(owners_of) + 2]
    at = len(owners_of) + 2
    hots, olds = refs[at : at + count], refs[at + count : at + 2 * count]
    normed_out = refs[at + 2 * count]
    sent = refs[at + 2 * count + 1 : -1]
    sums = refs[-1]
    me = lax.axis_index("wide")
    for piece, owners in zip(pieces, owners_of):
        for i, owner in enumerate(owners):
            to = pl.multiple_of(owner(me) * feats, feats)
            sums[pl.ds(to, feats), :] = piece[i * feats : (i + 1) * feats, :].astype(F32)
    values = sums[...]
    scale = lax.rsqrt(jnp.mean(values * values, axis=0, keepdims=True) + 1e-06)
    normed = (values * scale * column_f32(gain[...])).astype(BF16)
    normed_out[...] = normed
    for hot, old, send in zip(hots, olds, sent):
        rows = dot_nt(hot[...], normed).astype(BF16)
        grown = silu(dot(rows, w_atom[...]))
        send[...] = (old[...].astype(F32) + grown).astype(BF16)


def column_f32(row):
    return jnp.broadcast_to(row, (8, row.shape[1])).T[:, :1]


def local_kernel(
    normed_t, atom_h, w_atom, source, target, w_src, w_tgt, atom_hbm, out, atom_out, sem
):
    atoms = atom_h.shape[0]
    first = place("narrow", atoms)
    same = iota((atoms, atoms), 0) == iota((atoms, atoms), 1)
    normed = dot_nt(jnp.where(same, 1.0, 0.0).astype(BF16), normed_t[...]).astype(BF16)
    grown = silu(dot(normed, w_atom[...]))
    rows = (atom_h[...].astype(F32) + grown).astype(BF16)
    atom_out[...] = rows
    store = pltpu.make_async_copy(atom_out, atom_hbm, sem)
    store.start()
    sources = dot(one_hot(source[...] - first, atoms), rows).astype(BF16)
    targets = dot(one_hot(target[...] - first, atoms), rows).astype(BF16)
    out[...] = dot(sources, w_src[...]) + dot(targets, w_tgt[...])
    store.wait()


def final_kernel(count, *refs):
    partial, mid, w_src = refs[:3]
    rows = refs[3 : 3 + count]
    out = refs[3 + count]
    update = partial[...]
    if rows:
        got = rows[0][...].astype(F32)
        for r in rows[1:]:
            got = got + r[...].astype(F32)
        update = update + dot(got.astype(BF16), w_src[...])
    out[...] = (mid[...].astype(F32) + silu(update)).astype(BF16)


def stage_factors(wide):
    stages = []
    left = wide
    size = min(4, max(1, wide // 4))
    stride = wide
    for f in (size, max(1, wide // (2 * size)), 2):
        if f > 1 and left % f == 0:
            stride //= f
            left //= f
            stages.append((stride, f))
    return stages


def per_device(
    wide,
    narrow,
    edge_msg,
    basis,
    atom_h,
    edge_source,
    edge_target,
    send_rows,
    trip_slot,
    w_down,
    w_bil,
    w_up,
    w_atom_in,
    atom_gain,
    w_atom,
    w_src,
    w_tgt,
):
    edges, de = edge_msg.shape
    width = w_down.shape[1]
    basis_count = w_bil.shape[0] // width
    triplets = trip_slot.shape[1]
    atoms, da = atom_h.shape
    slots = send_rows.shape[1]
    cap = slots // wide
    feats = da // wide
    lanes = 2 * width
    big = (24 << 20) if slots <= 512 else (60 << 20)
    shape = jax.ShapeDtypeStruct

    source = edge_source.reshape(1, edges)
    target = edge_target.reshape(1, edges)
    dma = pltpu.SemaphoreType.DMA

    outgoing = call(
        functools.partial(outgoing_kernel, atoms),
        [HBM] * 4,
        VMEM,
        shape((wide, cap // 2 + 8, lanes), BF16),
        big,
        scratch=[
            pltpu.VMEM((edges, de), BF16),
            pltpu.VMEM((width, de), BF16),
            pltpu.VMEM((1, slots), jnp.int32),
            pltpu.VMEM((1, edges), jnp.int32),
            dma((7,)),
        ],
        name="outgoing",
    )(edge_msg, w_down.T, send_rows, target)
    received = lax.all_to_all(outgoing, "wide", split_axis=0, concat_axis=0, tiled=True)

    per = 256 // triplets
    kept = max(1, min(basis_count - 1, (3 << 20) // (edges * slots * 2)))
    rest_shape = (basis_count - kept, edges, slots)
    mixer = call(
        functools.partial(mixer_kernel, cap),
        [HBM, HBM],
        [VMEM, HBM],
        [shape((kept, edges, slots), BF16), shape(rest_shape, BF16)],
        big,
        scratch=[
            pltpu.VMEM(basis.shape, BF16),
            pltpu.VMEM((triplets, edges), jnp.int32),
            pltpu.VMEM((edges // per, per * triplets), jnp.int32),
            pltpu.VMEM((basis_count, edges, per * triplets), F32),
            pltpu.VMEM(rest_shape, BF16),
            dma((6,)),
        ],
        cost=cost(2 * basis_count * edges * slots * 256, 6 << 20),
        name="mixer",
    )(basis, trip_slot.T)

    edge_mid, message = call(
        edge_kernel,
        [VMEM] * 2 + [HBM] * 5,
        [HBM, VMEM],
        (shape((edges, de), BF16), shape((wide, feats, edges), BF16)),
        big,
        scratch=[
            pltpu.VMEM(rest_shape, BF16),
            pltpu.VMEM((edges, de), BF16),
            pltpu.VMEM((width, basis_count * width), BF16),
            pltpu.VMEM(w_up.shape, BF16),
            pltpu.VMEM(w_atom_in.shape, BF16),
            pltpu.VMEM((edges, de), BF16),
            dma((6,)),
        ],
        name="edge",
    )(received, *mixer, edge_msg, w_bil.T, w_up, w_atom_in)
    messages = lax.all_to_all(message, "wide", split_axis=0, concat_axis=0, tiled=True)

    source_late, _ = lax.optimization_barrier((source, message))
    wanted = [
        lax.ppermute(source_late, "narrow", [(i, (i + k) % narrow) for i in range(narrow)])
        for k in range(1, narrow)
    ]
    picks = []
    if wanted:
        picks = call(
            functools.partial(picks_kernel, len(wanted)),
            [VMEM] * (len(wanted) + 1),
            [VMEM] * (2 * len(wanted)),
            [shape((edges, atoms), BF16)] * len(wanted) + [shape((edges, da), BF16)] * len(wanted),
            big,
            name="picks",
        )(*wanted, atom_h)
    share = call(
        sum_kernel,
        [VMEM, VMEM] + [pl.BlockSpec(memory_space=pl.ANY)] * len(picks),
        VMEM,
        shape((feats, atoms), BF16),
        big,
        name="sums",
    )(messages, received, *picks)

    groups = [(share, [lambda me: me])]
    stages = stage_factors(wide)
    for number, (stride, size) in enumerate(stages):
        mirror = size & (size - 1) == 0

        def turned(at, k, size=size, mirror=mirror):
            return at ^ k if mirror else (at + k) % size

        def moved(k, stride=stride, size=size, turned=turned, mirror=mirror):
            def owner(me):
                at = (me // stride) % size
                return me + (turned(at, k if mirror else size - k) - at) * stride
            return owner

        fresh = []
        for value, owners in groups:
            got = [(value, owners)]
            for k in range(1, size):
                pairs = []
                for i in range(wide):
                    at = (i // stride) % size
                    pairs.append((i, i + (turned(at, k) - at) * stride))
                back = moved(k)
                got.append(
                    (
                        lax.ppermute(value, "wide", pairs),
                        [lambda me, o=o, back=back: o(back(me)) for o in owners],
                    )
                )
            if size > 2:
                fresh.append(
                    (
                        jnp.concatenate([v for v, _ in got], axis=0),
                        [o for _, os in got for o in os],
                    )
                )
            else:
                fresh.extend(got)
        groups = fresh

    pieces = [v for v, _ in groups]
    owners_of = [o for _, o in groups]
    outs = call(
        functools.partial(asked_kernel, owners_of, feats, len(wanted)),
        [VMEM] * (len(pieces) + 2 + len(picks)),
        [VMEM] * (1 + len(wanted)),
        [shape((da, atoms), BF16)] + [shape((edges, da), BF16)] * len(wanted),
        big,
        scratch=[pltpu.VMEM((da, atoms), F32)],
        name="asked",
    )(*pieces, atom_gain.reshape(1, da), w_atom, *picks)
    normed, asked = outs[0], outs[1:]
    rows = [
        lax.ppermute(a, "narrow", [(i, (i - k) % narrow) for i in range(narrow)])
        for k, a in enumerate(asked, start=1)
    ]
    atom_out, partial = call(
        local_kernel,
        [VMEM] * 7,
        [HBM, VMEM],
        (shape((atoms, da), BF16), shape((edges, de), F32)),
        big,
        scratch=[pltpu.VMEM((atoms, da), BF16), dma],
        cost=cost(4 * edges * da * de + 8 * edges * da * atoms, 4 << 20),
        name="local",
    )(normed, atom_h, w_atom, source, target, w_src, w_tgt)
    edge_out = call(
        functools.partial(final_kernel, len(rows)),
        [VMEM] * (3 + len(rows)),
        VMEM,
        shape((edges, de), BF16),
        big,
        name="final",
    )(partial, edge_mid, w_src, *rows)
    return (edge_out, atom_out)


def solution(mesh):
    placed = (
        P(("wide", "narrow"), None),
        P(("wide", "narrow"), None),
        P("narrow", None),
        P(("wide", "narrow")),
        P(("wide", "narrow")),
        P(("wide", "narrow"), None),
        P(("wide", "narrow"), None),
        P(),
        P(),
        P(),
        P(),
        P(),
        P(),
        P(),
        P(),
    )
    return jax.shard_map(
        functools.partial(per_device, mesh.shape["wide"], mesh.shape["narrow"]),
        mesh=mesh,
        in_specs=placed,
        out_specs=(P(("wide", "narrow"), None), P("narrow", None)),
        check_vma=False,
    )
```

time: 75.2 us -> 64.5 us (0.86)
  local copies, waits for them, and re-layouts: 14.7 us -> 3.33 us
  Pallas kernels: 18.8 us -> 19.8 us
  other arithmetic: 0.77 us -> 0.01 us
    unnamed x45 -> x16, local copies, waits for them, and re-layouts: 14.6 us -> 3.33 us
    all_to_all x1, waiting for transfers between devices: 6.71 us -> 4.81 us  [per_device(): lax.all_to_all(message, 'wide', split_axis=0, concat_axis=0, tiled=True)]
    ppermute x6, waiting for transfers between devices: 6.78 us -> 7.97 us  [per_device(): lax.ppermute(value, 'wide', pairs)]
    pallas_call x8, Pallas kernels: 18.8 us -> 19.8 us  [apply(): return run(*held)]
  transfers between devices with their start and end apart: 10 -> 10, of which waited for: 6 -> 9; matrix products, arithmetic and copies ran while one was open for 1% -> 0% of each run, Pallas kernels for 12% -> 14%
where the time goes in v2:
time: 64.5 us; the launch traced here: 64 us
  starting transfers between devices  21 us (33%)
  Pallas kernels  19.8 us (31%)
  waiting for transfers between devices  19.1 us (30%)
  local copies, waits for them, and re-layouts  3.33 us (5%)
  between operations  0.73 us (1%)
    pallas_call x8, Pallas kernels, apply(): return run(*held)  19.8 us
    ppermute x6, waiting for transfers between devices, per_device(): lax.ppermute(value, 'wide', pairs)  7.97 us
    all_to_all x1, starting transfers between devices, per_device(): lax.all_to_all(outgoing, 'wide', split_axis=0, concat_axis=0, tiled=True)  7.39 us
    all_to_all x1, starting transfers between devices, per_device(): lax.all_to_all(message, 'wide', split_axis=0, concat_axis=0, tiled=True)  5.47 us
    ppermute x6, starting transfers between devices, per_device(): lax.ppermute(value, 'wide', pairs)  4.97 us
    all_to_all x1, waiting for transfers between devices, per_device(): lax.all_to_all(message, 'wide', split_axis=0, concat_axis=0, tiled=True)  4.81 us
    ppermute x1, waiting for transfers between devices, per_device(): lax.ppermute(a, 'narrow', [(i, (i - k) % narrow) for i in range(narrow)])  3.61 us
    unnamed x16, local copies, waits for them, and re-layouts  3.33 us
  transfers between devices with their start and end apart: 10, of which 9 were waited for; matrix products, arithmetic and copies ran while one was open for 0% of the time, Pallas kernels for 14%

profile of v2, /device:TPU:0, one launch (start us, length us, event | category | flops | bytes accessed | tf_op | source)
XLA Modules:
  0.0 64.0 jit_solution(9661805548533440849)
XLA Ops:
  0.6 3.0 %outgoing.1 = bf16[16,24,128]{2,1,0:T(8,128)(2,1)} custom-call(bf16[256,1024]{1,0:T(8,128)(2,1)} %edge_hbm.3, bf16[64,1024]{1,0:T(8,128)(2,1)} %bitcast.12, s32[1,512]{1,0:T(1,128)} %rows_hbm.1, s32[1,256]{1,0:T(1,128)} %bitcast.7), custom_call_target="tpu_custom_call" | custom-call | tf_op jit(solution)/shard_map/outgoing/pallas_call | solution.py:61
  3.7 7.4 %all-to-all-start = ((bf16[16,24,128]{2,1,0:T(8,128)(2,1)}), bf16[16,24,128]{2,1,0:T(8,128)(2,1)S(1)}, u32[]{:S(2)}, u32[]{:S(2)}) async-start(bf16[16,24,128]{2,1,0:T(8,128)(2,1)} %outgoing.1), calls=%async_computation | async-start | bytes 196608 | tf_op jit(solution)/shard_map/all_to_all | solution.py:403
  11.1 6.7 %mixer.1 = (bf16[12,256,512]{2,1,0:T(8,128)(2,1)S(1)}, bf16[4,256,512]{2,1,0:T(8,128)(2,1)}) custom-call(bf16[256,512]{1,0:T(8,128)(2,1)} %basis_hbm.1, s32[32,256]{1,0:T(8,128)} %bitcast.13), custom_call_target="tpu_custom_call" | custom-call | flops 1073741824 | bytes 6291456 | tf_op jit(solution)/shard_map/mixer/pallas_call | solution.py:61
  17.8 0.7 %all-to-all-done.received = bf16[16,24,128]{2,1,0:T(8,128)(2,1)S(1)} async-done(((bf16[16,24,128]{2,1,0:T(8,128)(2,1)}), bf16[16,24,128]{2,1,0:T(8,128)(2,1)S(1)}, u32[]{:S(2)}, u32[]{:S(2)}) %all-to-all-start) | async-done | bytes 98336 | tf_op jit(solution)/shard_map/all_to_all | solution.py:403
  18.4 4.0 %edge.1 = (bf16[256,1024]{1,0:T(8,128)(2,1)}, bf16[16,32,256]{2,1,0:T(8,128)(2,1)}) custom-call(bf16[16,24,128]{2,1,0:T(8,128)(2,1)S(1)} %all-to-all-done.received, bf16[12,256,512]{2,1,0:T(8,128)(2,1)S(1)} %get-tuple-element.13.kept, bf16[4,256,512]{2,1,0:T(8,128)(2,1)} %get-tuple-element.14.rest_hbm, bf16[256,1024]{1,0:T(8,128)(2,1)} %edge_hbm.3, ...), custom_call_target="tpu_custom_call" | custom-call | tf_op jit(solution)/shard_map/edge/pallas_call | solution.py:61
  22.4 0.0 copy-start
  22.4 5.5 %all-to-all-start.1 = ((bf16[16,32,256]{2,1,0:T(8,128)(2,1)}), bf16[16,32,256]{2,1,0:T(8,128)(2,1)S(1)}, u32[]{:S(2)}, u32[]{:S(2)}) async-start(bf16[16,32,256]{2,1,0:T(8,128)(2,1)} %get-tuple-element.15), calls=%async_computation.1 | async-start | bytes 524288 | tf_op jit(solution)/shard_map/all_to_all | solution.py:443
  27.9 1.6 %collective-permute-start = (s32[1,256]{1,0:T(1,128)S(1)}, s32[1,256]{1,0:T(1,128)S(1)}, u32[]{:S(2)}, u32[]{:S(2)}) collective-permute-start(s32[1,256]{1,0:T(1,128)S(1)} %bitcast.9), channel_id=1, source_target_pairs={{0,1},{1,0},{2,3},{3,2},{4,5},{5,4},{6,7},{7,6},{8,9},{9,8},{10,11... | collective-permute-start | bytes 3080 | tf_op jit(solution)/shard_map/ppermute | solution.py:447
  29.5 2.0 %collective-permute-done.refs_0_ = s32[1,256]{1,0:T(1,128)S(1)} collective-permute-done((s32[1,256]{1,0:T(1,128)S(1)}, s32[1,256]{1,0:T(1,128)S(1)}, u32[]{:S(2)}, u32[]{:S(2)}) %collective-permute-start) | collective-permute-done | bytes 1056 | tf_op jit(solution)/shard_map/ppermute | solution.py:447
  31.6 1.0 %copy-done.1 = bf16[512,512]{1,0:T(8,128)(2,1)S(1)} copy-done((bf16[512,512]{1,0:T(8,128)(2,1)S(1)}, bf16[512,512]{1,0:T(8,128)(2,1)}, u32[]{:S(2)}) %copy-start.1) | copy-done | bytes 524312
  32.6 0.5 picks.1
  33.1 4.8 %all-to-all-done.1.messages = bf16[16,32,256]{2,1,0:T(8,128)(2,1)S(1)} async-done(((bf16[16,32,256]{2,1,0:T(8,128)(2,1)}), bf16[16,32,256]{2,1,0:T(8,128)(2,1)S(1)}, u32[]{:S(2)}, u32[]{:S(2)}) %all-to-all-start.1) | async-done | bytes 262176 | tf_op jit(solution)/shard_map/all_to_all | solution.py:443
  37.9 1.3 %sums.1 = bf16[32,512]{1,0:T(8,128)(2,1)S(1)} custom-call(bf16[16,32,256]{2,1,0:T(8,128)(2,1)S(1)} %all-to-all-done.1.messages, bf16[16,24,128]{2,1,0:T(8,128)(2,1)S(1)} %all-to-all-done.received, bf16[256,512]{1,0:T(8,128)(2,1)S(1)} %get-tuple-element.17.refs_0_.refs_6_, bf16[256,512]{1,0:T(8,128)(2,1)S(1)} %get-tuple-element.18.refs_1_.refs_7_), custom_call_target="tpu_custom_call" | custom-call | tf_op jit(solution)/shard_map/sums/pallas_call | solution.py:61
  39.3 1.0 %collective-permute-start.3 = (bf16[32,512]{1,0:T(8,128)(2,1)S(1)}, bf16[32,512]{1,0:T(8,128)(2,1)S(1)}, u32[]{:S(2)}, u32[]{:S(2)}) collective-permute-start(bf16[32,512]{1,0:T(8,128)(2,1)S(1)} %sums.1), channel_id=1, source_target_pairs={{0,24},{2,26},{4,28},{6,30},{8,16},{10,18},{12,20},{14,22},{16,8},... | collective-permute-start | bytes 98312 | tf_op jit(solution)/shard_map/ppermute | solution.py:494
  40.3 0.2 collective-permute-start.2
  40.4 3.3 %collective-permute-start.1 = (bf16[32,512]{1,0:T(8,128)(2,1)S(1)}, bf16[32,512]{1,0:T(8,128)(2,1)S(1)}, u32[]{:S(2)}, u32[]{:S(2)}) collective-permute-start(bf16[32,512]{1,0:T(8,128)(2,1)S(1)} %sums.1), channel_id=1, source_target_pairs={{0,8},{2,10},{4,12},{6,14},{8,0},{10,2},{12,4},{14,6},{16,24},{18,... | collective-permute-start | bytes 98312 | tf_op jit(solution)/shard_map/ppermute | solution.py:494
  43.7 1.3 %collective-permute-done.3 = bf16[32,512]{1,0:T(8,128)(2,1)S(1)} collective-permute-done((bf16[32,512]{1,0:T(8,128)(2,1)S(1)}, bf16[32,512]{1,0:T(8,128)(2,1)S(1)}, u32[]{:S(2)}, u32[]{:S(2)}) %collective-permute-start.3) | collective-permute-done | bytes 32800 | tf_op jit(solution)/shard_map/ppermute | solution.py:494
  45.0 0.7 %collective-permute-done.2 = bf16[32,512]{1,0:T(8,128)(2,1)S(1)} collective-permute-done((bf16[32,512]{1,0:T(8,128)(2,1)S(1)}, bf16[32,512]{1,0:T(8,128)(2,1)S(1)}, u32[]{:S(2)}, u32[]{:S(2)}) %collective-permute-start.2) | collective-permute-done | bytes 32800 | tf_op jit(solution)/shard_map/ppermute | solution.py:494
  45.7 0.1 collective-permute-done.1
  45.8 0.6 collective-permute-start.5
  46.4 0.0 collective-permute-start.4
  46.4 4.5 %collective-permute-done.5.refs_2_ = bf16[128,512]{1,0:T(8,128)(2,1)S(1)} collective-permute-done((bf16[128,512]{1,0:T(8,128)(2,1)S(1)}, bf16[128,512]{1,0:T(8,128)(2,1)S(1)}, u32[]{:S(2)}, u32[]{:S(2)}) %collective-permute-start.5) | collective-permute-done | bytes 131104 | tf_op jit(solution)/shard_map/ppermute | solution.py:494
  50.9 0.0 collective-permute-start.6
  50.9 0.0 collective-permute-done.4.refs_1_
  50.9 1.3 %collective-permute-done.6.refs_3_ = bf16[128,512]{1,0:T(8,128)(2,1)S(1)} collective-permute-done((bf16[128,512]{1,0:T(8,128)(2,1)S(1)}, bf16[128,512]{1,0:T(8,128)(2,1)S(1)}, u32[]{:S(2)}, u32[]{:S(2)}) %collective-permute-start.6) | collective-permute-done | bytes 131104 | tf_op jit(solution)/shard_map/ppermute | solution.py:494
  52.2 1.0 %copy-done.2 = bf16[512,512]{1,0:T(8,128)(2,1)S(1)} copy-done((bf16[512,512]{1,0:T(8,128)(2,1)S(1)}, bf16[512,512]{1,0:T(8,128)(2,1)}, u32[]{:S(2)}) %copy-start.2) | copy-done | bytes 524312
  53.3 0.9 %asked.1 = (bf16[512,512]{1,0:T(8,128)(2,1)S(1)}, bf16[256,512]{1,0:T(8,128)(2,1)S(1)}) custom-call(bf16[128,512]{1,0:T(8,128)(2,1)S(1)} %pad_maximum_fusion.refs_0_, bf16[128,512]{1,0:T(8,128)(2,1)S(1)} %collective-permute-done.4.refs_1_, bf16[128,512]{1,0:T(8,128)(2,1)S(1)} %collective-permute-done.5.refs_2_, ...), custom_call_target="tpu_custom_call" | custom-call | tf_op jit(solution)/shard_map/asked/pallas_call | solution.py:61
  54.2 1.6 %collective-permute-start.7 = (bf16[256,512]{1,0:T(8,128)(2,1)S(1)}, bf16[256,512]{1,0:T(8,128)(2,1)S(1)}, u32[]{:S(2)}, u32[]{:S(2)}) collective-permute-start(bf16[256,512]{1,0:T(8,128)(2,1)S(1)} %get-tuple-element.22), channel_id=1, source_target_pairs={{0,1},{1,0},{2,3},{3,2},{4,5},{5,4},{6,7},{7,6},{8,9},{9,8},{10,11... | collective-permute-start | bytes 786440 | tf_op jit(solution)/shard_map/ppermute | solution.py:522
  55.8 1.2 %copy-done.6 = bf16[512,1024]{1,0:T(8,128)(2,1)S(1)} copy-done((bf16[512,1024]{1,0:T(8,128)(2,1)S(1)}, bf16[512,1024]{1,0:T(8,128)(2,1)}, u32[]{:S(2)}) %copy-start.6) | copy-done | bytes 1048600
  57.0 2.0 %local.1 = (bf16[512,512]{1,0:T(8,128)(2,1)}, f32[256,1024]{1,0:T(8,128)S(1)}) custom-call(bf16[512,512]{1,0:T(8,128)(2,1)S(1)} %get-tuple-element.19.normed_t, bf16[512,512]{1,0:T(8,128)(2,1)S(1)} %copy-done.1, bf16[512,512]{1,0:T(8,128)(2,1)S(1)} %copy-done.2, s32[1,256]{1,0:T(1,128)S(1)} %bitcast.10, s32[1,256]{1,0:T(1,128)S(1)} %bitcast.8, ...), custom_call_target="tpu_custom_call" | custom-call | flops 1073741824 | bytes 4194304 | tf_op jit(solution)/shard_map/local/pallas_call | solution.py:61
  59.0 3.6 %collective-permute-done.7.refs_3_ = bf16[256,512]{1,0:T(8,128)(2,1)S(1)} collective-permute-done((bf16[256,512]{1,0:T(8,128)(2,1)S(1)}, bf16[256,512]{1,0:T(8,128)(2,1)S(1)}, u32[]{:S(2)}, u32[]{:S(2)}) %collective-permute-start.7) | collective-permute-done | bytes 262176 | tf_op jit(solution)/shard_map/ppermute | solution.py:522
  62.6 1.4 %final.1 = bf16[256,1024]{1,0:T(8,128)(2,1)} custom-call(f32[256,1024]{1,0:T(8,128)S(1)} %get-tuple-element.20.refs_0_, bf16[256,1024]{1,0:T(8,128)(2,1)S(1)} %copy-done.3, bf16[512,1024]{1,0:T(8,128)(2,1)S(1)} %copy-done, bf16[256,512]{1,0:T(8,128)(2,1)S(1)} %collective-permute-done.7.refs_3_), custom_call_target="tpu_custom_call" | custom-call | tf_op jit(solution)/shard_map/final/pallas_call | solution.py:61
  (13 shorter events, 0.0 us)
Async XLA Ops:
  3.7 14.8 %all-to-all-start = ((bf16[16,24,128]{2,1,0:T(8,128)(2,1)}), bf16[16,24,128]{2,1,0:T(8,128)(2,1)S(1)}, u32[]{:S(2)}, u32[]{:S(2)}) async-start(bf16[16,24,128]{2,1,0:T(8,128)(2,1)} %outgoing.1), calls=%async_computation | async-start | bytes 196608 | tf_op jit(solution)/shard_map/all_to_all | solution.py:403
  18.4 9.5 %copy-start.7 = (s32[256]{0:T(256)S(1)}, s32[256]{0:T(256)}, u32[]{:S(2)}) copy-start(s32[256]{0:T(256)} %param.18) | copy-start | bytes 3076
  18.4 33.8 %copy-start.4 = (f32[512]{0:T(512)S(1)}, f32[512]{0:T(512)}, u32[]{:S(2)}) copy-start(f32[512]{0:T(512)} %param.26) | copy-start | bytes 6148
  18.4 37.4 %copy-start.5 = (s32[256]{0:T(256)S(1)}, s32[256]{0:T(256)}, u32[]{:S(2)}) copy-start(s32[256]{0:T(256)} %param.19) | copy-start | bytes 3076
  22.4 33.4 %copy-start = (bf16[512,1024]{1,0:T(8,128)(2,1)S(1)}, bf16[512,1024]{1,0:T(8,128)(2,1)}, u32[]{:S(2)}) copy-start(bf16[512,1024]{1,0:T(8,128)(2,1)} %refs_2_.1) | copy-start | bytes 3145732
  22.4 15.5 %all-to-all-start.1 = ((bf16[16,32,256]{2,1,0:T(8,128)(2,1)}), bf16[16,32,256]{2,1,0:T(8,128)(2,1)S(1)}, u32[]{:S(2)}, u32[]{:S(2)}) async-start(bf16[16,32,256]{2,1,0:T(8,128)(2,1)} %get-tuple-element.15), calls=%async_computation.1 | async-start | bytes 524288 | tf_op jit(solution)/shard_map/all_to_all | solution.py:443
  27.9 3.6 %collective-permute-start = (s32[1,256]{1,0:T(1,128)S(1)}, s32[1,256]{1,0:T(1,128)S(1)}, u32[]{:S(2)}, u32[]{:S(2)}) collective-permute-start(s32[1,256]{1,0:T(1,128)S(1)} %bitcast.9), channel_id=1, source_target_pairs={{0,1},{1,0},{2,3},{3,2},{4,5},{5,4},{6,7},{7,6},{8,9},{9,8},{10,11... | collective-permute-start | bytes 3080 | tf_op jit(solution)/shard_map/ppermute | solution.py:447
  31.6 1.0 %copy-start.1 = (bf16[512,512]{1,0:T(8,128)(2,1)S(1)}, bf16[512,512]{1,0:T(8,128)(2,1)}, u32[]{:S(2)}) copy-start(bf16[512,512]{1,0:T(8,128)(2,1)} %atom_h.1) | copy-start | bytes 1572868
  37.9 24.7 %copy-start.3 = (bf16[256,1024]{1,0:T(8,128)(2,1)S(1)}, bf16[256,1024]{1,0:T(8,128)(2,1)}, u32[]{:S(2)}) copy-start(bf16[256,1024]{1,0:T(8,128)(2,1)} %get-tuple-element.21.refs_1_) | copy-start | bytes 1572868
  39.3 5.7 %collective-permute-start.3 = (bf16[32,512]{1,0:T(8,128)(2,1)S(1)}, bf16[32,512]{1,0:T(8,128)(2,1)S(1)}, u32[]{:S(2)}, u32[]{:S(2)}) collective-permute-start(bf16[32,512]{1,0:T(8,128)(2,1)S(1)} %sums.1), channel_id=1, source_target_pairs={{0,24},{2,26},{4,28},{6,30},{8,16},{10,18},{12,20},{14,22},{16,8},... | collective-permute-start | bytes 98312 | tf_op jit(solution)/shard_map/ppermute | solution.py:494
  40.3 5.4 %collective-permute-start.2 = (bf16[32,512]{1,0:T(8,128)(2,1)S(1)}, bf16[32,512]{1,0:T(8,128)(2,1)S(1)}, u32[]{:S(2)}, u32[]{:S(2)}) collective-permute-start(bf16[32,512]{1,0:T(8,128)(2,1)S(1)} %sums.1), channel_id=1, source_target_pairs={{0,16},{2,18},{4,20},{6,22},{8,24},{10,26},{12,28},{14,30},{16,0},... | collective-permute-start | bytes 98312 | tf_op jit(solution)/shard_map/ppermute | solution.py:494
  40.4 5.4 %collective-permute-start.1 = (bf16[32,512]{1,0:T(8,128)(2,1)S(1)}, bf16[32,512]{1,0:T(8,128)(2,1)S(1)}, u32[]{:S(2)}, u32[]{:S(2)}) collective-permute-start(bf16[32,512]{1,0:T(8,128)(2,1)S(1)} %sums.1), channel_id=1, source_target_pairs={{0,8},{2,10},{4,12},{6,14},{8,0},{10,2},{12,4},{14,6},{16,24},{18,... | collective-permute-start | bytes 98312 | tf_op jit(solution)/shard_map/ppermute | solution.py:494
  45.8 5.0 %collective-permute-start.5 = (bf16[128,512]{1,0:T(8,128)(2,1)S(1)}, bf16[128,512]{1,0:T(8,128)(2,1)S(1)}, u32[]{:S(2)}, u32[]{:S(2)}) collective-permute-start(bf16[128,512]{1,0:T(8,128)(2,1)S(1)} %pad_maximum_fusion.refs_0_), channel_id=1, source_target_pairs={{0,4},{2,6},{4,0},{6,2},{8,12},{10,14},{12,8},{14,10},{16,20},{18,... | collective-permute-start | bytes 393224 | tf_op jit(solution)/shard_map/ppermute | solution.py:494
  46.4 4.5 %collective-permute-start.4 = (bf16[128,512]{1,0:T(8,128)(2,1)S(1)}, bf16[128,512]{1,0:T(8,128)(2,1)S(1)}, u32[]{:S(2)}, u32[]{:S(2)}) collective-permute-start(bf16[128,512]{1,0:T(8,128)(2,1)S(1)} %pad_maximum_fusion.refs_0_), channel_id=1, source_target_pairs={{0,2},{2,0},{4,6},{6,4},{8,10},{10,8},{12,14},{14,12},{16,18},{18,... | collective-permute-start | bytes 393224 | tf_op jit(solution)/shard_map/ppermute | solution.py:494
  50.9 1.3 %collective-permute-start.6 = (bf16[128,512]{1,0:T(8,128)(2,1)S(1)}, bf16[128,512]{1,0:T(8,128)(2,1)S(1)}, u32[]{:S(2)}, u32[]{:S(2)}) collective-permute-start(bf16[128,512]{1,0:T(8,128)(2,1)S(1)} %collective-permute-done.5.refs_2_), channel_id=1, source_target_pairs={{0,2},{2,0},{4,6},{6,4},{8,10},{10,8},{12,14},{14,12},{16,18},{18,... | collective-permute-start | bytes 393224 | tf_op jit(solution)/shard_map/ppermute | solution.py:494
  52.2 1.0 %copy-start.2 = (bf16[512,512]{1,0:T(8,128)(2,1)S(1)}, bf16[512,512]{1,0:T(8,128)(2,1)}, u32[]{:S(2)}) copy-start(bf16[512,512]{1,0:T(8,128)(2,1)} %w_atom.1) | copy-start | bytes 1572868
  54.2 8.4 %collective-permute-start.7 = (bf16[256,512]{1,0:T(8,128)(2,1)S(1)}, bf16[256,512]{1,0:T(8,128)(2,1)S(1)}, u32[]{:S(2)}, u32[]{:S(2)}) collective-permute-start(bf16[256,512]{1,0:T(8,128)(2,1)S(1)} %get-tuple-element.22), channel_id=1, source_target_pairs={{0,1},{1,0},{2,3},{3,2},{4,5},{5,4},{6,7},{7,6},{8,9},{9,8},{10,11... | collective-permute-start | bytes 786440 | tf_op jit(solution)/shard_map/ppermute | solution.py:522
  55.8 1.2 %copy-start.6 = (bf16[512,1024]{1,0:T(8,128)(2,1)S(1)}, bf16[512,1024]{1,0:T(8,128)(2,1)}, u32[]{:S(2)}) copy-start(bf16[512,1024]{1,0:T(8,128)(2,1)} %w_tgt.1) | copy-start | bytes 3145732

commit v3 on v2

--- a/solution.py
+++ b/solution.py
@@ -34,6 +34,18 @@
 
 VMEM = pl.BlockSpec(memory_space=pltpu.VMEM)
 HBM = pl.BlockSpec(memory_space=pltpu.HBM)
+
+
+def quotient(value, by):
+    if by & (by - 1) == 0:
+        return lax.shift_right_logical(value, by.bit_length() - 1)
+    return lax.div(value, jnp.int32(by))
+
+
+def remainder(value, by):
+    if by & (by - 1) == 0:
+        return lax.bitwise_and(value, by - 1)
+    return lax.rem(value, jnp.int32(by))
 
 
 def call(kernel, ins, outs, out_shape, vmem, scratch=(), cost=None, name=None):
@@ -142,37 +154,51 @@
     ]
     start_first(fetch)
     rows, cols = iota((total, total), 0), iota((total, total), 1)
-    order = (rows // basis_count == cols % triplets) & (rows % basis_count == cols // triplets)
+    order = quotient(rows, basis_count) + remainder(rows, basis_count) * triplets == cols
     order = jnp.where(order, 1.0, 0.0).astype(BF16)
-    own = iota((edges, span), 0) % per == iota((edges, span), 1) // triplets
+    own = remainder(iota((edges, span), 0), per) == quotient(iota((edges, span), 1), triplets)
     fetch[0].wait()
     half = cap // 2
     slot = slots_t[...]
-    slot = (slot // half) % 2 * (slots // 2) + slot // cap * half + slot % half
+    slot = (
+        remainder(quotient(slot, half), 2) * (slots // 2)
+        + quotient(slot, cap) * half
+        + remainder(slot, half)
+    )
     slot = slot.T
-    tile = jnp.where(iota((triplets, span), 0) == iota((triplets, span), 1) % triplets, 1.0, 0.0)
+    turn = remainder(iota((triplets, span), 1), triplets)
+    tile = jnp.where(iota((triplets, span), 0) == turn, 1.0, 0.0)
     tile = tile.astype(BF16)
     high = lax.shift_right_logical(slot, 8).astype(F32).astype(BF16)
     low = lax.bitwise_and(slot, 255).astype(F32).astype(BF16)
     wide = jnp.where(own, dot(high, tile) * 256.0 + dot(low, tile), 0.0)
     flat[...] = jnp.sum(wide.reshape(groups, per, span), axis=1).astype(jnp.int32)
     fetch[1].wait()
-    by_basis = dot(basis[...], order).astype(BF16)
+    by_basis = dot(basis[...], order)
     pack = 128 // triplets
-    rows, cols = iota((128, span), 0), iota((128, span), 1)
-    for j in range(pack):
-        tile = (rows // triplets == j) & (rows % triplets == cols % triplets)
-        tile = jnp.where(tile, 1.0, 0.0).astype(BF16)
-        for q in range(basis_count // pack):
-            wide = dot(by_basis[:, q * 128 : (q + 1) * 128], tile)
-            spread[q * pack + j] = jnp.where(own, wide, 0.0)
+    turn = remainder(iota((edges, 128), 0), pack)
+    for q in range(total // 128):
+        lanes = by_basis[:, q * 128 : (q + 1) * 128]
+        turned = lanes
+        for r in range(1, pack):
+            turned = jnp.where(turn == r, pltpu.roll(lanes, r * triplets, 1), turned)
+        spread[:, q * 128 : (q + 1) * 128] = turned
+    row, lane = iota((per, 128), 0), quotient(iota((per, 128), 1), triplets)
+    mine = [row == lane + c * pack for c in range(span // 128)]
 
     def one(pair):
         parts = []
         for h in range(2):
             group = pair * 2 + h
-            left = spread[:, pl.ds(pl.multiple_of(group * per, per), per), :]
-            left = left.reshape(basis_count * per, span).astype(BF16)
+            values = spread[pl.ds(pl.multiple_of(group * per, per), per), :]
+            left = []
+            for k in range(basis_count):
+                q, j = k // pack, k % pack
+                lanes = values[:, q * 128 : (q + 1) * 128]
+                if j:
+                    lanes = pltpu.roll(lanes, 128 - j * triplets, 1)
+                left.append(jnp.concatenate([jnp.where(m, lanes, 0.0) for m in mine], axis=1))
+            left = jnp.concatenate(left, axis=0).astype(BF16)
             hot = iota((slots, span), 0) == flat[pl.ds(group, 1), :]
             part = dot_nt(left, jnp.where(hot, 1.0, 0.0).astype(BF16))
             parts.append(part.reshape(basis_count, per, slots))
@@ -181,17 +207,20 @@
         kept[:, at, :] = both[:kept_count]
         rest[:, at, :] = both[kept_count:]
 
+    unroll = 4
+
     def step(i, _):
-        one(2 * i)
-        one(2 * i + 1)
+        for u in range(unroll):
+            one(unroll * i + u)
         return 0
 
     chunks = sems.shape[0] - 2
-    steps = groups // 4 // chunks
+    steps = groups // 2 // unroll // chunks
     copies = []
     for c in range(chunks):
         lax.fori_loop(c * steps, (c + 1) * steps, step, 0)
-        part = pl.ds(c * steps * 4 * per, steps * 4 * per)
+        size = steps * unroll * 2 * per
+        part = pl.ds(c * size, size)
         copies.append(
             pltpu.make_async_copy(rest.at[:, part, :], rest_hbm.at[:, part, :], sems.at[2 + c])
         )
@@ -209,15 +238,9 @@
     w_up_hbm,
     w_atom_hbm,
     mid_hbm,
-    message,
-    rest,
-    edge_msg,
-    w_bil_t,
-    w_up,
-    w_atom_in,
-    edge_mid,
-    sems,
+    *refs,
 ):
+    *quarters, rest, edge_msg, w_bil_t, w_up, w_atom_in, edge_mid, message, sems = refs
     peers, rows, lanes = received.shape
     half = rows - 8
     width = w_bil_t.shape[0]
@@ -245,76 +268,96 @@
     store = pltpu.make_async_copy(edge_mid, mid_hbm, sems.at[len(pairs)])
     store.start()
     copies[4].wait()
-    sent = dot(mid, w_atom_in[...]).T.astype(BF16)
-    message[...] = sent.reshape(message.shape)
+    message[...] = dot(mid, w_atom_in[...]).T
+    part = message.shape[0] // len(quarters)
+    mine = lax.axis_index("wide") % len(quarters)
+    for q, quarter in enumerate(quarters):
+        at = pl.multiple_of((mine ^ q) * part, part)
+        quarter[...] = message[pl.ds(at, part), :].astype(BF16)
     store.wait()
 
 
-def picks_kernel(count, *refs):
+def picks_kernel(order, feats, count, *refs):
     wanted = refs[:count]
-    atom_h = refs[count]
-    hots, olds = refs[count + 1 : 2 * count + 1], refs[2 * count + 1 :]
+    atom_h, gain, w_hbm = refs[count : count + 3]
+    hots = refs[count + 3 : 2 * count + 3]
+    olds = refs[2 * count + 3 : 3 * count + 3]
+    gain_out, w_out, w, wide, tall, sem = refs[3 * count + 3 :]
+    fetch = pltpu.make_async_copy(w_hbm, w, sem)
+    fetch.start()
     atoms = atom_h.shape[0]
+    me = lax.axis_index("wide")
+    starts = [pl.multiple_of(where(me) * feats, feats) for where in order]
     for want, hot, old in zip(wanted, hots, olds):
         chosen = one_hot(want[...] - place("narrow", atoms), atoms)
         hot[...] = chosen
         old[...] = dot(chosen, atom_h[...]).astype(BF16)
-
-
-def sum_kernel(messages, received, *refs):
-    out = refs[-1]
-    peers, feats, edges = messages.shape
+    tall[...] = jnp.broadcast_to(gain[...], (tall.shape[1], gain.shape[1])).T
+    blocks = [tall[pl.ds(at, feats), :] for at in starts]
+    gain_out[...] = jnp.concatenate(blocks, axis=0).T[:8]
+    fetch.wait()
+    wide[...] = w[...].astype(F32)
+    blocks = [wide[pl.ds(at, feats), :] for at in starts]
+    w_out[...] = jnp.concatenate(blocks, axis=0).astype(BF16)
+
+
+def sum_kernel(count, later, received, *refs):
+    quarters, outs, total = refs[:count], refs[count + later : -1], refs[-1]
     _, rows, lanes = received.shape
     half = rows - 8
-    count = edges // lanes
-    total = jnp.zeros(out.shape, F32)
-    ids = iota((out.shape[1], lanes), 0).astype(F32)
-    for p in range(peers):
-        codes = received[p, half:, :].astype(F32)
+    edges = quarters[0].shape[1]
+    parts = edges // lanes
+    me = lax.axis_index("wide")
+    ids = iota((total.shape[1], lanes), 0).astype(F32)
+    value = jnp.zeros(total.shape, F32)
+    for q, quarter in enumerate(quarters):
+        codes = received[pl.ds(me ^ q, 1), half:, :].reshape(rows - half, lanes).astype(F32)
         hot = [
-            jnp.where(ids == codes[i : i + 1] * 256.0 + codes[count + i : count + i + 1], 1.0, 0.0)
-            for i in range(count)
+            jnp.where(ids == codes[i : i + 1] * 256.0 + codes[parts + i : parts + i + 1], 1.0, 0.0)
+            for i in range(parts)
         ]
-        total += dot_nt(messages[p], jnp.concatenate(hot, axis=1).astype(BF16))
-    out[...] = total.astype(BF16)
-
-
-def asked_kernel(owners_of, feats, count, *refs):
-    pieces = refs[: len(owners_of)]
-    gain, w_atom = refs[len(owners_of) : len(owners_of) + 2]
-    at = len(owners_of) + 2
-    hots, olds = refs[at : at + count], refs[at + count : at + 2 * count]
-    normed_out = refs[at + 2 * count]
-    sent = refs[at + 2 * count + 1 : -1]
-    sums = refs[-1]
-    me = lax.axis_index("wide")
-    for piece, owners in zip(pieces, owners_of):
-        for i, owner in enumerate(owners):
-            to = pl.multiple_of(owner(me) * feats, feats)
-            sums[pl.ds(to, feats), :] = piece[i * feats : (i + 1) * feats, :].astype(F32)
-    values = sums[...]
-    scale = lax.rsqrt(jnp.mean(values * values, axis=0, keepdims=True) + 1e-06)
-    normed = (values * scale * column_f32(gain[...])).astype(BF16)
-    normed_out[...] = normed
+        value += dot_nt(quarter[...], jnp.concatenate(hot, axis=1).astype(BF16))
+    total[...] = value
+    feats = total.shape[0] // len(outs)
+    for k, out in enumerate(outs):
+        at = pl.multiple_of((me // count ^ k) * feats, feats)
+        out[...] = total[pl.ds(at, feats), :].astype(out.dtype)
+
+
+def add_kernel(count, *refs):
+    value = refs[0][...]
+    for r in refs[1:count]:
+        value = value + r[...].astype(F32)
+    refs[-1][...] = value.astype(BF16)
+
+
+def stacked(pieces):
+    return jnp.concatenate([p[...] for p in pieces], axis=0)
+
+
+def updated(hot, table, gain, w_atom, old):
+    rows = dot_nt(hot, table)
+    scale = lax.rsqrt(jnp.mean(rows * rows, axis=-1, keepdims=True) + 1e-06)
+    normed = (rows * scale * gain).astype(BF16)
+    return (old.astype(F32) + silu(dot(normed, w_atom))).astype(BF16)
+
+
+def asked_kernel(count, *refs):
+    sent = refs[len(refs) - count :]
+    hots, olds = refs[:count], refs[count : 2 * count]
+    gain, w_atom = refs[2 * count : 2 * count + 2]
+    table = stacked(refs[2 * count + 2 : len(refs) - count])
     for hot, old, send in zip(hots, olds, sent):
-        rows = dot_nt(hot[...], normed).astype(BF16)
-        grown = silu(dot(rows, w_atom[...]))
-        send[...] = (old[...].astype(F32) + grown).astype(BF16)
-
-
-def column_f32(row):
-    return jnp.broadcast_to(row, (8, row.shape[1])).T[:, :1]
-
-
-def local_kernel(
-    normed_t, atom_h, w_atom, source, target, w_src, w_tgt, atom_hbm, out, atom_out, sem
-):
+        send[...] = updated(hot[...], table, gain[:1, :], w_atom[...], old[...])
+
+
+def local_kernel(gain, w_atom, atom_h, source, target, w_src, w_tgt, *refs):
+    *pieces, atom_hbm, out, atom_out, sem = refs
     atoms = atom_h.shape[0]
     first = place("narrow", atoms)
     same = iota((atoms, atoms), 0) == iota((atoms, atoms), 1)
-    normed = dot_nt(jnp.where(same, 1.0, 0.0).astype(BF16), normed_t[...]).astype(BF16)
-    grown = silu(dot(normed, w_atom[...]))
-    rows = (atom_h[...].astype(F32) + grown).astype(BF16)
+    same = jnp.where(same, 1.0, 0.0).astype(BF16)
+    rows = updated(same, stacked(pieces), gain[:1, :], w_atom[...], atom_h[...])
     atom_out[...] = rows
     store = pltpu.make_async_copy(atom_out, atom_hbm, sem)
     store.start()
@@ -327,14 +370,27 @@
 def final_kernel(count, *refs):
     partial, mid, w_src = refs[:3]
     rows = refs[3 : 3 + count]
-    out = refs[3 + count]
-    update = partial[...]
+    out_hbm, out, sems = refs[3 + count :]
+    got = None
     if rows:
         got = rows[0][...].astype(F32)
         for r in rows[1:]:
             got = got + r[...].astype(F32)
-        update = update + dot(got.astype(BF16), w_src[...])
-    out[...] = (mid[...].astype(F32) + silu(update)).astype(BF16)
+        got = got.astype(BF16)
+    chunks = sems.shape[0]
+    step = out.shape[1] // chunks
+    stores = []
+    for c in range(chunks):
+        part = slice(c * step, (c + 1) * step)
+        update = partial[:, part]
+        if rows:
+            update = update + dot(got, w_src[:, part])
+        out[:, part] = (mid[:, part].astype(F32) + silu(update)).astype(BF16)
+        at = pl.ds(c * step, step)
+        stores.append(pltpu.make_async_copy(out.at[:, at], out_hbm.at[:, at], sems.at[c]))
+        stores[-1].start()
+    for store in stores:
+        store.wait()
 
 
 def stage_factors(wide):
@@ -348,6 +404,49 @@
             left //= f
             stages.append((stride, f))
     return stages
+
+
+def gathered(share, wide, feats):
+    groups = [(share, [lambda me: me])]
+    stages = stage_factors(wide)
+    for number, (stride, size) in enumerate(stages):
+        mirror = size & (size - 1) == 0
+
+        def turned(at, k, size=size, mirror=mirror):
+            return at ^ k if mirror else (at + k) % size
+
+        def moved(k, stride=stride, size=size, turned=turned, mirror=mirror):
+            def owner(me):
+                at = (me // stride) % size
+                return me + (turned(at, k if mirror else size - k) - at) * stride
+            return owner
+
+        fresh = []
+        for value, owners in groups:
+            got = [(value, owners)]
+            for k in range(1, size):
+                pairs = []
+                for i in range(wide):
+                    at = (i // stride) % size
+                    pairs.append((i, i + (turned(at, k) - at) * stride))
+                back = moved(k)
+                got.append(
+                    (
+                        value if value is None else lax.ppermute(value, "wide", pairs),
+                        [lambda me, o=o, back=back: o(back(me)) for o in owners],
+                    )
+                )
+            if size > 2:
+                fresh.append(
+                    (
+                        None if value is None else jnp.concatenate([v for v, _ in got], axis=0),
+                        [o for _, os in got for o in os],
+                    )
+                )
+            else:
+                fresh.extend(got)
+        groups = fresh
+    return groups
 
 
 def per_device(
@@ -378,6 +477,8 @@
     cap = slots // wide
     feats = da // wide
     lanes = 2 * width
+    low = min(4, wide)
+    high = wide // low
     big = (24 << 20) if slots <= 512 else (60 << 20)
     shape = jax.ShapeDtypeStruct
 
@@ -396,7 +497,7 @@
             pltpu.VMEM((width, de), BF16),
             pltpu.VMEM((1, slots), jnp.int32),
             pltpu.VMEM((1, edges), jnp.int32),
-            dma((7,)),
+            dma((5,)),
         ],
         name="outgoing",
     )(edge_msg, w_down.T, send_rows, target)
@@ -415,7 +516,7 @@
             pltpu.VMEM(basis.shape, BF16),
             pltpu.VMEM((triplets, edges), jnp.int32),
             pltpu.VMEM((edges // per, per * triplets), jnp.int32),
-            pltpu.VMEM((basis_count, edges, per * triplets), F32),
+            pltpu.VMEM(basis.shape, F32),
             pltpu.VMEM(rest_shape, BF16),
             dma((6,)),
         ],
@@ -423,11 +524,11 @@
         name="mixer",
     )(basis, trip_slot.T)
 
-    edge_mid, message = call(
+    edge_mid, *quarters = call(
         edge_kernel,
         [VMEM] * 2 + [HBM] * 5,
-        [HBM, VMEM],
-        (shape((edges, de), BF16), shape((wide, feats, edges), BF16)),
+        [HBM] + [VMEM] * low,
+        [shape((edges, de), BF16)] + [shape((feats * high, edges), BF16)] * low,
         big,
         scratch=[
             pltpu.VMEM(rest_shape, BF16),
@@ -436,108 +537,91 @@
             pltpu.VMEM(w_up.shape, BF16),
             pltpu.VMEM(w_atom_in.shape, BF16),
             pltpu.VMEM((edges, de), BF16),
+            pltpu.VMEM((da, edges), F32),
             dma((6,)),
         ],
         name="edge",
     )(received, *mixer, edge_msg, w_bil.T, w_up, w_atom_in)
-    messages = lax.all_to_all(message, "wide", split_axis=0, concat_axis=0, tiled=True)
-
-    source_late, _ = lax.optimization_barrier((source, message))
+    def mirrored(value, flip):
+        return lax.ppermute(value, "wide", [(i, i ^ flip) for i in range(wide)])
+
+    quarters = quarters[:1] + [mirrored(v, q) for q, v in enumerate(quarters) if q]
+    source_late, quarters[1] = lax.optimization_barrier((source, quarters[1]))
     wanted = [
         lax.ppermute(source_late, "narrow", [(i, (i + k) % narrow) for i in range(narrow)])
         for k in range(1, narrow)
     ]
-    picks = []
-    if wanted:
-        picks = call(
-            functools.partial(picks_kernel, len(wanted)),
-            [VMEM] * (len(wanted) + 1),
-            [VMEM] * (2 * len(wanted)),
-            [shape((edges, atoms), BF16)] * len(wanted) + [shape((edges, da), BF16)] * len(wanted),
-            big,
-            name="picks",
-        )(*wanted, atom_h)
+    def block(owner):
+        return lambda me: owner(me) % low * high + owner(me) // low
+
+    order = [block(o) for _, os in gathered(None, wide, feats) for o in os]
+    *picks, gain_near, w_atom_near = call(
+        functools.partial(picks_kernel, order, feats, len(wanted)),
+        [VMEM] * (len(wanted) + 2) + [HBM],
+        [VMEM] * (2 * len(wanted) + 2),
+        [shape((edges, atoms), BF16)] * len(wanted)
+        + [shape((edges, da), BF16)] * len(wanted)
+        + [shape((8, da), F32), shape(w_atom.shape, BF16)],
+        big,
+        scratch=[
+            pltpu.VMEM(w_atom.shape, BF16),
+            pltpu.VMEM(w_atom.shape, F32),
+            pltpu.VMEM((da, 128), F32),
+            dma,
+        ],
+        cost=cost(1 << 26, 2 << 20),
+        name="picks",
+    )(*wanted, atom_h, atom_gain.reshape(1, da), w_atom)
+    sums = call(
+        functools.partial(sum_kernel, low, len(wanted)),
+        [VMEM] * (1 + low) + [pl.BlockSpec(memory_space=pl.ANY)] * len(wanted),
+        [VMEM] * high,
+        [shape((feats, atoms), F32)] + [shape((feats, atoms), BF16)] * (high - 1),
+        big,
+        scratch=[pltpu.VMEM((feats * high, atoms), F32)],
+        name="sums",
+    )(received, *quarters, *wanted)
+    far = [mirrored(sums[k], k * low) for k in range(high - 1, 0, -1)]
+    sums = [sums[0]] + far[::-1]
     share = call(
-        sum_kernel,
-        [VMEM, VMEM] + [pl.BlockSpec(memory_space=pl.ANY)] * len(picks),
+        functools.partial(add_kernel, high),
+        [VMEM] * high + [pl.BlockSpec(memory_space=pl.ANY)] * len(picks),
         VMEM,
         shape((feats, atoms), BF16),
         big,
-        name="sums",
-    )(messages, received, *picks)
-
-    groups = [(share, [lambda me: me])]
-    stages = stage_factors(wide)
-    for number, (stride, size) in enumerate(stages):
-        mirror = size & (size - 1) == 0
-
-        def turned(at, k, size=size, mirror=mirror):
-            return at ^ k if mirror else (at + k) % size
-
-        def moved(k, stride=stride, size=size, turned=turned, mirror=mirror):
-            def owner(me):
-                at = (me // stride) % size
-                return me + (turned(at, k if mirror else size - k) - at) * stride
-            return owner
-
-        fresh = []
-        for value, owners in groups:
-            got = [(value, owners)]
-            for k in range(1, size):
-                pairs = []
-                for i in range(wide):
-                    at = (i // stride) % size
-                    pairs.append((i, i + (turned(at, k) - at) * stride))
-                back = moved(k)
-                got.append(
-                    (
-                        lax.ppermute(value, "wide", pairs),
-                        [lambda me, o=o, back=back: o(back(me)) for o in owners],
-                    )
-                )
-            if size > 2:
-                fresh.append(
-                    (
-                        jnp.concatenate([v for v, _ in got], axis=0),
-                        [o for _, os in got for o in os],
-                    )
-                )
-            else:
-                fresh.extend(got)
-        groups = fresh
-
-    pieces = [v for v, _ in groups]
-    owners_of = [o for _, o in groups]
-    outs = call(
-        functools.partial(asked_kernel, owners_of, feats, len(wanted)),
-        [VMEM] * (len(pieces) + 2 + len(picks)),
-        [VMEM] * (1 + len(wanted)),
-        [shape((da, atoms), BF16)] + [shape((edges, da), BF16)] * len(wanted),
-        big,
-        scratch=[pltpu.VMEM((da, atoms), F32)],
+        name="add",
+    )(*sums, *picks)
+
+    pieces = [v for v, _ in gathered(share, wide, feats)]
+    asked = call(
+        functools.partial(asked_kernel, len(wanted)),
+        [VMEM] * (len(picks) + 2 + len(pieces)),
+        [VMEM] * len(wanted),
+        [shape((edges, da), BF16)] * len(wanted),
+        big,
         name="asked",
-    )(*pieces, atom_gain.reshape(1, da), w_atom, *picks)
-    normed, asked = outs[0], outs[1:]
+    )(*picks, gain_near, w_atom_near, *pieces)
     rows = [
         lax.ppermute(a, "narrow", [(i, (i - k) % narrow) for i in range(narrow)])
         for k, a in enumerate(asked, start=1)
     ]
     atom_out, partial = call(
         local_kernel,
-        [VMEM] * 7,
+        [VMEM] * (7 + len(pieces)),
         [HBM, VMEM],
         (shape((atoms, da), BF16), shape((edges, de), F32)),
         big,
         scratch=[pltpu.VMEM((atoms, da), BF16), dma],
         cost=cost(4 * edges * da * de + 8 * edges * da * atoms, 4 << 20),
         name="local",
-    )(normed, atom_h, w_atom, source, target, w_src, w_tgt)
+    )(gain_near, w_atom_near, atom_h, source, target, w_src, w_tgt, *pieces)
     edge_out = call(
         functools.partial(final_kernel, len(rows)),
         [VMEM] * (3 + len(rows)),
-        VMEM,
+        HBM,
         shape((edges, de), BF16),
         big,
+        scratch=[pltpu.VMEM((edges, de), BF16), dma((4,))],
         name="final",
     )(partial, edge_mid, w_src, *rows)
     return (edge_out, atom_out)

time: 64.5 us -> 59.7 us (0.926)
  local copies, waits for them, and re-layouts: 3.33 us -> 0.04 us
  Pallas kernels: 19.8 us -> 17.7 us
  starting transfers between devices: 21 us -> 22.6 us
  waiting for transfers between devices: 19.1 us -> 18.3 us
    ppermute x6 -> x12, starting transfers between devices: 4.97 us -> 12.1 us  [the longest x6 6.37 us: mirrored(): return lax.ppermute(value, 'wide', [(i, i ^ flip) for i in range(wide)])]
    all_to_all x1 -> x0, starting transfers between devices: 5.47 us -> none  [per_device(): lax.all_to_all(message, 'wide', split_axis=0, concat_axis=0, tiled=True)]
    all_to_all x1 -> x0, waiting for transfers between devices: 4.81 us -> none  [per_device(): lax.all_to_all(message, 'wide', split_axis=0, concat_axis=0, tiled=True)]
    ppermute x6 -> x12, waiting for transfers between devices: 7.97 us -> 11.8 us  [the longest x6 7.35 us: gathered(): lax.ppermute(value, 'wide', pairs)]
    unnamed x16 -> x14, local copies, waits for them, and re-layouts: 3.33 us -> 0.04 us
    pallas_call x8 -> x9, Pallas kernels: 19.8 us -> 17.7 us  [apply(): return run(*held)]
    ppermute x1, waiting for transfers between devices: 2.04 us -> 0.07 us  [per_device(): lax.ppermute(source_late, 'narrow', [(i, (i + k) % narrow) for i in range...]
    all_to_all x1, waiting for transfers between devices: 0.68 us -> 1.8 us  [per_device(): lax.all_to_all(outgoing, 'wide', split_axis=0, concat_axis=0, tiled=True)]
  transfers between devices with their start and end apart: 10 -> 15, of which waited for: 9 -> 11; matrix products, arithmetic and copies ran while one was open for 0% -> 0% of each run, Pallas kernels for 14% -> 16%
where the time goes in v3:
time: 59.7 us; the launch traced here: 59.5 us
  starting transfers between devices  22.6 us (38%)
  waiting for transfers between devices  18.3 us (31%)
  Pallas kernels  17.7 us (30%)
  between operations  0.78 us (1%)
    pallas_call x9, Pallas kernels, apply(): return run(*held)  17.7 us
    all_to_all x1, starting transfers between devices, per_device(): lax.all_to_all(outgoing, 'wide', split_axis=0, concat_axis=0, tiled=True)  7.4 us
    ppermute x6, waiting for transfers between devices, gathered(): lax.ppermute(value, 'wide', pairs)  7.35 us
    ppermute x6, starting transfers between devices, mirrored(): return lax.ppermute(value, 'wide', [(i, i ^ flip) for i in range(wide)])  6.37 us
    ppermute x6, starting transfers between devices, gathered(): lax.ppermute(value, 'wide', pairs)  5.72 us
    ppermute x1, waiting for transfers between devices, per_device(): lax.ppermute(a, 'narrow', [(i, (i - k) % narrow) for i in range(narrow)])  4.69 us
    ppermute x6, waiting for transfers between devices, mirrored(): return lax.ppermute(value, 'wide', [(i, i ^ flip) for i in range(wide)])  4.41 us
    all_to_all x1, waiting for transfers between devices, per_device(): lax.all_to_all(outgoing, 'wide', split_axis=0, concat_axis=0, tiled=True)  1.8 us
  transfers between devices with their start and end apart: 15, of which 11 were waited for; matrix products, arithmetic and copies ran while one was open for 0% of the time, Pallas kernels for 16%

profile of v3, /device:TPU:0, one launch (start us, length us, event | category | flops | bytes accessed | tf_op | source)
XLA Modules:
  0.0 59.5 jit_solution(18331710078909251220)
XLA Ops:
  0.6 2.5 %outgoing.1 = bf16[16,24,128]{2,1,0:T(8,128)(2,1)} custom-call(bf16[256,1024]{1,0:T(8,128)(2,1)} %edge_hbm.3, bf16[64,1024]{1,0:T(8,128)(2,1)} %bitcast.12, s32[1,512]{1,0:T(1,128)} %rows_hbm.1, s32[1,256]{1,0:T(1,128)} %bitcast.7), custom_call_target="tpu_custom_call" | custom-call | tf_op jit(solution)/shard_map/outgoing/pallas_call | solution.py:73
  3.2 7.4 %all-to-all-start = ((bf16[16,24,128]{2,1,0:T(8,128)(2,1)}), bf16[16,24,128]{2,1,0:T(8,128)(2,1)S(1)}, u32[]{:S(2)}, u32[]{:S(2)}) async-start(bf16[16,24,128]{2,1,0:T(8,128)(2,1)} %outgoing.1), calls=%async_computation | async-start | bytes 196608 | tf_op jit(solution)/shard_map/all_to_all | solution.py:504
  10.6 5.6 %mixer.1 = (bf16[12,256,512]{2,1,0:T(8,128)(2,1)S(1)}, bf16[4,256,512]{2,1,0:T(8,128)(2,1)}) custom-call(bf16[256,512]{1,0:T(8,128)(2,1)} %basis_hbm.1, s32[32,256]{1,0:T(8,128)} %bitcast.13), custom_call_target="tpu_custom_call" | custom-call | flops 1073741824 | bytes 6291456 | tf_op jit(solution)/shard_map/mixer/pallas_call | solution.py:73
  16.1 0.0 copy-start.6
  16.1 1.8 %all-to-all-done.received = bf16[16,24,128]{2,1,0:T(8,128)(2,1)S(1)} async-done(((bf16[16,24,128]{2,1,0:T(8,128)(2,1)}), bf16[16,24,128]{2,1,0:T(8,128)(2,1)S(1)}, u32[]{:S(2)}, u32[]{:S(2)}) %all-to-all-start) | async-done | bytes 98336 | tf_op jit(solution)/shard_map/all_to_all | solution.py:504
  17.9 3.3 %edge.1 = (bf16[256,1024]{1,0:T(8,128)(2,1)}, bf16[128,256]{1,0:T(8,128)(2,1)S(1)}, bf16[128,256]{1,0:T(8,128)(2,1)S(1)}, bf16[128,256]{1,0:T(8,128)(2,1)S(1)}, bf16[128,256]{1,0:T(8,128)(2,1)S(1)}) custom-call(bf16[16,24,128]{2,1,0:T(8,128)(2,1)S(1)} %all-to-all-done.received, bf16[12,256,512]{2,1,0:T(8,128)(2,1)S(1)} %get-tuple-element.21.kept, ...), custom_call_target="tpu_custom_call" | custom-call | tf_op jit(solution)/shard_map/edge/pallas_call | solution.py:73
  21.3 0.1 collective-permute-start
  21.4 0.2 collective-permute-start.2
  21.6 1.6 %collective-permute-start.3 = (bf16[128,256]{1,0:T(8,128)(2,1)S(1)}, bf16[128,256]{1,0:T(8,128)(2,1)S(1)}, u32[]{:S(2)}, u32[]{:S(2)}) collective-permute-start(bf16[128,256]{1,0:T(8,128)(2,1)S(1)} %get-tuple-element.30), channel_id=1, source_target_pairs={{0,6},{2,4},{4,2},{6,0},{8,14},{10,12},{12,10},{14,8},{16,22},{18,... | collective-permute-start | bytes 196616 | tf_op jit(solution)/shard_map/ppermute | solution.py:546
  23.2 1.5 %collective-permute-start.1 = (s32[1,256]{1,0:T(1,128)S(1)}, s32[1,256]{1,0:T(1,128)S(1)}, u32[]{:S(2)}, u32[]{:S(2)}) collective-permute-start(s32[1,256]{1,0:T(1,128)S(1)} %bitcast.9), channel_id=1, source_target_pairs={{0,1},{1,0},{2,3},{3,2},{4,5},{5,4},{6,7},{7,6},{8,9},{9,8},{10,11... | collective-permute-start | bytes 3080 | tf_op jit(solution)/shard_map/ppermute | solution.py:551
  24.7 1.7 %collective-permute-done.2.refs_2_ = bf16[128,256]{1,0:T(8,128)(2,1)S(1)} collective-permute-done((bf16[128,256]{1,0:T(8,128)(2,1)S(1)}, bf16[128,256]{1,0:T(8,128)(2,1)S(1)}, u32[]{:S(2)}, u32[]{:S(2)}) %collective-permute-start.2) | collective-permute-done | bytes 65568 | tf_op jit(solution)/shard_map/ppermute | solution.py:546
  26.4 0.3 collective-permute-done.3.refs_3_
  26.7 0.1 collective-permute-done.1.refs_0_.refs_4_
  26.8 0.5 sums.1
  27.3 0.5 collective-permute-start.4
  27.8 2.4 %collective-permute-start.5 = (bf16[32,512]{1,0:T(8,128)(2,1)S(1)}, bf16[32,512]{1,0:T(8,128)(2,1)S(1)}, u32[]{:S(2)}, u32[]{:S(2)}) collective-permute-start(bf16[32,512]{1,0:T(8,128)(2,1)S(1)} %get-tuple-element.33), channel_id=1, source_target_pairs={{0,16},{2,18},{4,20},{6,22},{8,24},{10,26},{12,28},{14,30},{16,0},... | collective-permute-start | bytes 98312 | tf_op jit(solution)/shard_map/ppermute | solution.py:546
  30.1 1.6 %collective-permute-start.6 = (bf16[32,512]{1,0:T(8,128)(2,1)S(1)}, bf16[32,512]{1,0:T(8,128)(2,1)S(1)}, u32[]{:S(2)}, u32[]{:S(2)}) collective-permute-start(bf16[32,512]{1,0:T(8,128)(2,1)S(1)} %get-tuple-element.34), channel_id=1, source_target_pairs={{0,24},{2,26},{4,28},{6,30},{8,16},{10,18},{12,20},{14,22},{16,8},... | collective-permute-start | bytes 98312 | tf_op jit(solution)/shard_map/ppermute | solution.py:546
  31.8 1.6 %picks.1 = (bf16[256,512]{1,0:T(8,128)(2,1)S(1)}, bf16[256,512]{1,0:T(8,128)(2,1)S(1)}, f32[8,512]{1,0:T(8,128)S(1)}, bf16[512,512]{1,0:T(8,128)(2,1)S(1)}) custom-call(s32[1,256]{1,0:T(1,128)S(1)} %collective-permute-done.1.refs_0_.refs_4_, bf16[512,512]{1,0:T(8,128)(2,1)S(1)} %copy-done.1, f32[1,512]{1,0:T(1,128)S(1)} %bitcast.6, bf16[512,512]{1,0:T(8,128)(2,1)} %refs_3_.1), custom_call_target="tpu_custom_call" | custom-call | flops 67108864 | bytes 2097152 | tf_op jit(solution)/shard_map/picks/pallas_call | solution.py:73
  33.4 2.4 %collective-permute-done.6.refs_3_ = bf16[32,512]{1,0:T(8,128)(2,1)S(1)} collective-permute-done((bf16[32,512]{1,0:T(8,128)(2,1)S(1)}, bf16[32,512]{1,0:T(8,128)(2,1)S(1)}, u32[]{:S(2)}, u32[]{:S(2)}) %collective-permute-start.6) | collective-permute-done | bytes 32800 | tf_op jit(solution)/shard_map/ppermute | solution.py:546
  35.9 1.7 %collective-permute-start.9 = (bf16[32,512]{1,0:T(8,128)(2,1)S(1)}, bf16[32,512]{1,0:T(8,128)(2,1)S(1)}, u32[]{:S(2)}, u32[]{:S(2)}) collective-permute-start(bf16[32,512]{1,0:T(8,128)(2,1)S(1)} %add.1), channel_id=1, source_target_pairs={{0,24},{2,26},{4,28},{6,30},{8,16},{10,18},{12,20},{14,22},{16,8},... | collective-permute-start | bytes 98312 | tf_op jit(solution)/shard_map/ppermute | solution.py:435
  37.6 2.7 %collective-permute-start.7 = (bf16[32,512]{1,0:T(8,128)(2,1)S(1)}, bf16[32,512]{1,0:T(8,128)(2,1)S(1)}, u32[]{:S(2)}, u32[]{:S(2)}) collective-permute-start(bf16[32,512]{1,0:T(8,128)(2,1)S(1)} %add.1), channel_id=1, source_target_pairs={{0,8},{2,10},{4,12},{6,14},{8,0},{10,2},{12,4},{14,6},{16,24},{18,... | collective-permute-start | bytes 98312 | tf_op jit(solution)/shard_map/ppermute | solution.py:435
  40.3 1.3 %collective-permute-done.9 = bf16[32,512]{1,0:T(8,128)(2,1)S(1)} collective-permute-done((bf16[32,512]{1,0:T(8,128)(2,1)S(1)}, bf16[32,512]{1,0:T(8,128)(2,1)S(1)}, u32[]{:S(2)}, u32[]{:S(2)}) %collective-permute-start.9) | collective-permute-done | bytes 32800 | tf_op jit(solution)/shard_map/ppermute | solution.py:435
  41.6 0.9 %collective-permute-done.8 = bf16[32,512]{1,0:T(8,128)(2,1)S(1)} collective-permute-done((bf16[32,512]{1,0:T(8,128)(2,1)S(1)}, bf16[32,512]{1,0:T(8,128)(2,1)S(1)}, u32[]{:S(2)}, u32[]{:S(2)}) %collective-permute-start.8) | collective-permute-done | bytes 32800 | tf_op jit(solution)/shard_map/ppermute | solution.py:435
  42.5 0.1 collective-permute-done.7
  42.6 1.3 %collective-permute-start.11 = (bf16[128,512]{1,0:T(8,128)(2,1)S(1)}, bf16[128,512]{1,0:T(8,128)(2,1)S(1)}, u32[]{:S(2)}, u32[]{:S(2)}) collective-permute-start(bf16[128,512]{1,0:T(8,128)(2,1)S(1)} %pad_maximum_fusion.refs_0_.refs_4_), channel_id=1, source_target_pairs={{0,4},{2,6},{4,0},{6,2},{8,12},{10,14},{12,8},{14,10},{16,20},{18,... | collective-permute-start | bytes 393224 | tf_op jit(solution)/shard_map/ppermute | solution.py:435
  43.8 3.8 %collective-permute-done.11.refs_2_.refs_6_ = bf16[128,512]{1,0:T(8,128)(2,1)S(1)} collective-permute-done((bf16[128,512]{1,0:T(8,128)(2,1)S(1)}, bf16[128,512]{1,0:T(8,128)(2,1)S(1)}, u32[]{:S(2)}, u32[]{:S(2)}) %collective-permute-start.11) | collective-permute-done | bytes 131104 | tf_op jit(solution)/shard_map/ppermute | solution.py:435
  47.6 1.3 %collective-permute-done.12.refs_3_.refs_7_ = bf16[128,512]{1,0:T(8,128)(2,1)S(1)} collective-permute-done((bf16[128,512]{1,0:T(8,128)(2,1)S(1)}, bf16[128,512]{1,0:T(8,128)(2,1)S(1)}, u32[]{:S(2)}, u32[]{:S(2)}) %collective-permute-start.12) | collective-permute-done | bytes 131104 | tf_op jit(solution)/shard_map/ppermute | solution.py:435
  49.0 0.7 %asked.1 = bf16[256,512]{1,0:T(8,128)(2,1)S(1)} custom-call(bf16[256,512]{1,0:T(8,128)(2,1)S(1)} %get-tuple-element.35.refs_4_.refs_0_, bf16[256,512]{1,0:T(8,128)(2,1)S(1)} %get-tuple-element.36.refs_5_.refs_1_, f32[8,512]{1,0:T(8,128)S(1)} %get-tuple-element.25.gain.refs_2_, bf16[512,512]{1,0:T(8,128)(2,1)S(1)} %get-tuple-element.26.w_atom.refs_3_, ...), custom_call_target="tpu_custom_call" | custom-call | tf_op jit(solution)/shard_map/asked/pallas_call | solution.py:73
  49.7 1.6 %collective-permute-start.13 = (bf16[256,512]{1,0:T(8,128)(2,1)S(1)}, bf16[256,512]{1,0:T(8,128)(2,1)S(1)}, u32[]{:S(2)}, u32[]{:S(2)}) collective-permute-start(bf16[256,512]{1,0:T(8,128)(2,1)S(1)} %asked.1), channel_id=1, source_target_pairs={{0,1},{1,0},{2,3},{3,2},{4,5},{5,4},{6,7},{7,6},{8,9},{9,8},{10,11... | collective-permute-start | bytes 786440 | tf_op jit(solution)/shard_map/ppermute | solution.py:605
  51.3 2.1 %local.1 = (bf16[512,512]{1,0:T(8,128)(2,1)}, f32[256,1024]{1,0:T(8,128)S(1)}) custom-call(f32[8,512]{1,0:T(8,128)S(1)} %get-tuple-element.25.gain.refs_2_, bf16[512,512]{1,0:T(8,128)(2,1)S(1)} %get-tuple-element.26.w_atom.refs_3_, bf16[512,512]{1,0:T(8,128)(2,1)S(1)} %copy-done.1, s32[1,256]{1,0:T(1,128)S(1)} %bitcast.10, s32[1,256]{1,0:T(1,128)S(1)} %bitcast.8, ...), custom_call_target="tpu_custom_call" | custom-call | flops 1073741824 | bytes 4194304 | tf_op jit(solution)/shard_map/local/pallas_call | solution.py:73
  53.4 4.7 %collective-permute-done.13.refs_3_ = bf16[256,512]{1,0:T(8,128)(2,1)S(1)} collective-permute-done((bf16[256,512]{1,0:T(8,128)(2,1)S(1)}, bf16[256,512]{1,0:T(8,128)(2,1)S(1)}, u32[]{:S(2)}, u32[]{:S(2)}) %collective-permute-start.13) | collective-permute-done | bytes 262176 | tf_op jit(solution)/shard_map/ppermute | solution.py:605
  58.1 1.3 %final.1 = bf16[256,1024]{1,0:T(8,128)(2,1)} custom-call(f32[256,1024]{1,0:T(8,128)S(1)} %get-tuple-element.37.refs_0_, bf16[256,1024]{1,0:T(8,128)(2,1)S(1)} %copy-done.2, bf16[512,1024]{1,0:T(8,128)(2,1)S(1)} %copy-done, bf16[256,512]{1,0:T(8,128)(2,1)S(1)} %collective-permute-done.13.refs_3_), custom_call_target="tpu_custom_call" | custom-call | tf_op jit(solution)/shard_map/final/pallas_call | solution.py:73
  (22 shorter events, 0.1 us)
Async XLA Ops:
  3.2 14.8 %all-to-all-start = ((bf16[16,24,128]{2,1,0:T(8,128)(2,1)}), bf16[16,24,128]{2,1,0:T(8,128)(2,1)S(1)}, u32[]{:S(2)}, u32[]{:S(2)}) async-start(bf16[16,24,128]{2,1,0:T(8,128)(2,1)} %outgoing.1), calls=%async_computation | async-start | bytes 196608 | tf_op jit(solution)/shard_map/all_to_all | solution.py:504
  16.1 7.1 %copy-start.6 = (s32[256]{0:T(256)S(1)}, s32[256]{0:T(256)}, u32[]{:S(2)}) copy-start(s32[256]{0:T(256)} %param.18) | copy-start | bytes 3076
  17.9 13.8 %copy-start.1 = (bf16[512,512]{1,0:T(8,128)(2,1)S(1)}, bf16[512,512]{1,0:T(8,128)(2,1)}, u32[]{:S(2)}) copy-start(bf16[512,512]{1,0:T(8,128)(2,1)} %atom_h.1) | copy-start | bytes 1572868
  17.9 13.8 %copy-start.3 = (f32[512]{0:T(512)S(1)}, f32[512]{0:T(512)}, u32[]{:S(2)}) copy-start(f32[512]{0:T(512)} %param.26) | copy-start | bytes 6148
  21.2 30.0 %copy-start = (bf16[512,1024]{1,0:T(8,128)(2,1)S(1)}, bf16[512,1024]{1,0:T(8,128)(2,1)}, u32[]{:S(2)}) copy-start(bf16[512,1024]{1,0:T(8,128)(2,1)} %refs_2_.1) | copy-start | bytes 3145732
  21.3 30.0 %copy-start.4 = (s32[256]{0:T(256)S(1)}, s32[256]{0:T(256)}, u32[]{:S(2)}) copy-start(s32[256]{0:T(256)} %param.19) | copy-start | bytes 3076
  21.3 30.0 %copy-start.5 = (bf16[512,1024]{1,0:T(8,128)(2,1)S(1)}, bf16[512,1024]{1,0:T(8,128)(2,1)}, u32[]{:S(2)}) copy-start(bf16[512,1024]{1,0:T(8,128)(2,1)} %w_tgt.1) | copy-start | bytes 3145732
  21.3 1.9 %collective-permute-start = (bf16[128,256]{1,0:T(8,128)(2,1)S(1)}, bf16[128,256]{1,0:T(8,128)(2,1)S(1)}, u32[]{:S(2)}, u32[]{:S(2)}) collective-permute-start(bf16[128,256]{1,0:T(8,128)(2,1)S(1)} %get-tuple-element.23), channel_id=1, source_target_pairs={{0,2},{2,0},{4,6},{6,4},{8,10},{10,8},{12,14},{14,12},{16,18},{18,... | collective-permute-start | bytes 196616 | tf_op jit(solution)/shard_map/ppermute | solution.py:546
  21.4 5.0 %collective-permute-start.2 = (bf16[128,256]{1,0:T(8,128)(2,1)S(1)}, bf16[128,256]{1,0:T(8,128)(2,1)S(1)}, u32[]{:S(2)}, u32[]{:S(2)}) collective-permute-start(bf16[128,256]{1,0:T(8,128)(2,1)S(1)} %get-tuple-element.29), channel_id=1, source_target_pairs={{0,4},{2,6},{4,0},{6,2},{8,12},{10,14},{12,8},{14,10},{16,20},{18,... | collective-permute-start | bytes 196616 | tf_op jit(solution)/shard_map/ppermute | solution.py:546
  21.6 5.1 %collective-permute-start.3 = (bf16[128,256]{1,0:T(8,128)(2,1)S(1)}, bf16[128,256]{1,0:T(8,128)(2,1)S(1)}, u32[]{:S(2)}, u32[]{:S(2)}) collective-permute-start(bf16[128,256]{1,0:T(8,128)(2,1)S(1)} %get-tuple-element.30), channel_id=1, source_target_pairs={{0,6},{2,4},{4,2},{6,0},{8,14},{10,12},{12,10},{14,8},{16,22},{18,... | collective-permute-start | bytes 196616 | tf_op jit(solution)/shard_map/ppermute | solution.py:546
  23.2 3.6 %collective-permute-start.1 = (s32[1,256]{1,0:T(1,128)S(1)}, s32[1,256]{1,0:T(1,128)S(1)}, u32[]{:S(2)}, u32[]{:S(2)}) collective-permute-start(s32[1,256]{1,0:T(1,128)S(1)} %bitcast.9), channel_id=1, source_target_pairs={{0,1},{1,0},{2,3},{3,2},{4,5},{5,4},{6,7},{7,6},{8,9},{9,8},{10,11... | collective-permute-start | bytes 3080 | tf_op jit(solution)/shard_map/ppermute | solution.py:551
  27.3 6.1 %collective-permute-start.4 = (bf16[32,512]{1,0:T(8,128)(2,1)S(1)}, bf16[32,512]{1,0:T(8,128)(2,1)S(1)}, u32[]{:S(2)}, u32[]{:S(2)}) collective-permute-start(bf16[32,512]{1,0:T(8,128)(2,1)S(1)} %get-tuple-element.32), channel_id=1, source_target_pairs={{0,8},{2,10},{4,12},{6,14},{8,0},{10,2},{12,4},{14,6},{16,24},{18,... | collective-permute-start | bytes 98312 | tf_op jit(solution)/shard_map/ppermute | solution.py:546
  27.8 5.6 %collective-permute-start.5 = (bf16[32,512]{1,0:T(8,128)(2,1)S(1)}, bf16[32,512]{1,0:T(8,128)(2,1)S(1)}, u32[]{:S(2)}, u32[]{:S(2)}) collective-permute-start(bf16[32,512]{1,0:T(8,128)(2,1)S(1)} %get-tuple-element.33), channel_id=1, source_target_pairs={{0,16},{2,18},{4,20},{6,22},{8,24},{10,26},{12,28},{14,30},{16,0},... | collective-permute-start | bytes 98312 | tf_op jit(solution)/shard_map/ppermute | solution.py:546
  30.1 5.7 %collective-permute-start.6 = (bf16[32,512]{1,0:T(8,128)(2,1)S(1)}, bf16[32,512]{1,0:T(8,128)(2,1)S(1)}, u32[]{:S(2)}, u32[]{:S(2)}) collective-permute-start(bf16[32,512]{1,0:T(8,128)(2,1)S(1)} %get-tuple-element.34), channel_id=1, source_target_pairs={{0,24},{2,26},{4,28},{6,30},{8,16},{10,18},{12,20},{14,22},{16,8},... | collective-permute-start | bytes 98312 | tf_op jit(solution)/shard_map/ppermute | solution.py:546
  35.9 22.3 %copy-start.2 = (bf16[256,1024]{1,0:T(8,128)(2,1)S(1)}, bf16[256,1024]{1,0:T(8,128)(2,1)}, u32[]{:S(2)}) copy-start(bf16[256,1024]{1,0:T(8,128)(2,1)} %get-tuple-element.38.refs_1_) | copy-start | bytes 1572868
  35.9 5.8 %collective-permute-start.9 = (bf16[32,512]{1,0:T(8,128)(2,1)S(1)}, bf16[32,512]{1,0:T(8,128)(2,1)S(1)}, u32[]{:S(2)}, u32[]{:S(2)}) collective-permute-start(bf16[32,512]{1,0:T(8,128)(2,1)S(1)} %add.1), channel_id=1, source_target_pairs={{0,24},{2,26},{4,28},{6,30},{8,16},{10,18},{12,20},{14,22},{16,8},... | collective-permute-start | bytes 98312 | tf_op jit(solution)/shard_map/ppermute | solution.py:435
  37.6 4.9 %collective-permute-start.8 = (bf16[32,512]{1,0:T(8,128)(2,1)S(1)}, bf16[32,512]{1,0:T(8,128)(2,1)S(1)}, u32[]{:S(2)}, u32[]{:S(2)}) collective-permute-start(bf16[32,512]{1,0:T(8,128)(2,1)S(1)} %add.1), channel_id=1, source_target_pairs={{0,16},{2,18},{4,20},{6,22},{8,24},{10,26},{12,28},{14,30},{16,0},... | collective-permute-start | bytes 98312 | tf_op jit(solution)/shard_map/ppermute | solution.py:435
  37.6 5.0 %collective-permute-start.7 = (bf16[32,512]{1,0:T(8,128)(2,1)S(1)}, bf16[32,512]{1,0:T(8,128)(2,1)S(1)}, u32[]{:S(2)}, u32[]{:S(2)}) collective-permute-start(bf16[32,512]{1,0:T(8,128)(2,1)S(1)} %add.1), channel_id=1, source_target_pairs={{0,8},{2,10},{4,12},{6,14},{8,0},{10,2},{12,4},{14,6},{16,24},{18,... | collective-permute-start | bytes 98312 | tf_op jit(solution)/shard_map/ppermute | solution.py:435
  42.6 5.0 %collective-permute-start.11 = (bf16[128,512]{1,0:T(8,128)(2,1)S(1)}, bf16[128,512]{1,0:T(8,128)(2,1)S(1)}, u32[]{:S(2)}, u32[]{:S(2)}) collective-permute-start(bf16[128,512]{1,0:T(8,128)(2,1)S(1)} %pad_maximum_fusion.refs_0_.refs_4_), channel_id=1, source_target_pairs={{0,4},{2,6},{4,0},{6,2},{8,12},{10,14},{12,8},{14,10},{16,20},{18,... | collective-permute-start | bytes 393224 | tf_op jit(solution)/shard_map/ppermute | solution.py:435
  43.8 3.8 %collective-permute-start.10 = (bf16[128,512]{1,0:T(8,128)(2,1)S(1)}, bf16[128,512]{1,0:T(8,128)(2,1)S(1)}, u32[]{:S(2)}, u32[]{:S(2)}) collective-permute-start(bf16[128,512]{1,0:T(8,128)(2,1)S(1)} %pad_maximum_fusion.refs_0_.refs_4_), channel_id=1, source_target_pairs={{0,2},{2,0},{4,6},{6,4},{8,10},{10,8},{12,14},{14,12},{16,18},{18,... | collective-permute-start | bytes 393224 | tf_op jit(solution)/shard_map/ppermute | solution.py:435
  47.6 1.3 %collective-permute-start.12 = (bf16[128,512]{1,0:T(8,128)(2,1)S(1)}, bf16[128,512]{1,0:T(8,128)(2,1)S(1)}, u32[]{:S(2)}, u32[]{:S(2)}) collective-permute-start(bf16[128,512]{1,0:T(8,128)(2,1)S(1)} %collective-permute-done.11.refs_2_.refs_6_), channel_id=1, source_target_pairs={{0,2},{2,0},{4,6},{6,4},{8,10},{10,8},{12,14},{14,12},{16,18},{18,... | collective-permute-start | bytes 393224 | tf_op jit(solution)/shard_map/ppermute | solution.py:435
  49.7 8.4 %collective-permute-start.13 = (bf16[256,512]{1,0:T(8,128)(2,1)S(1)}, bf16[256,512]{1,0:T(8,128)(2,1)S(1)}, u32[]{:S(2)}, u32[]{:S(2)}) collective-permute-start(bf16[256,512]{1,0:T(8,128)(2,1)S(1)} %asked.1), channel_id=1, source_target_pairs={{0,1},{1,0},{2,3},{3,2},{4,5},{5,4},{6,7},{7,6},{8,9},{9,8},{10,11... | collective-permute-start | bytes 786440 | tf_op jit(solution)/shard_map/ppermute | solution.py:605

commit v4 on v3

--- a/solution.py
+++ b/solution.py
@@ -48,7 +48,7 @@
     return lax.rem(value, jnp.int32(by))
 
 
-def call(kernel, ins, outs, out_shape, vmem, scratch=(), cost=None, name=None):
+def call(kernel, ins, outs, out_shape, vmem, scratch=(), cost=None, name=None, alias=()):
     def kept(spec, leaf):
         return pltpu.HBM(leaf.shape, leaf.dtype) if spec is HBM else leaf
 
@@ -60,6 +60,7 @@
         in_specs=list(ins),
         out_specs=outs,
         scratch_shapes=list(scratch),
+        input_output_aliases=dict(alias),
         compiler_params=pltpu.CompilerParams(vmem_limit_bytes=vmem),
         cost_estimate=cost,
         name=name,
@@ -88,46 +89,55 @@
     return jnp.where(hot, 1.0, 0.0).astype(BF16)
 
 
-def outgoing_kernel(atoms, edge_hbm, w_hbm, rows_hbm, target_hbm, out, edge, w, rows, target, sems):
+def outgoing_kernel(
+    edge_hbm,
+    w_hbm,
+    rows_hbm,
+    basis_hbm,
+    slots_hbm,
+    out,
+    basis,
+    slots_t,
+    edge,
+    w,
+    rows,
+    sems,
+):
     edges = edge.shape[0]
     width = w.shape[0]
-    peers, block, lanes = out.shape
-    half = block - 8
+    peers, half, lanes = out.shape
     slots = peers * half * 2
-    chunks = sems.shape[0] - 3
+    chunks = sems.shape[0] - 4
     step = edges // chunks
     copies = [
         pltpu.make_async_copy(rows_hbm, rows, sems.at[0]),
-        pltpu.make_async_copy(target_hbm, target, sems.at[1]),
-        pltpu.make_async_copy(w_hbm, w, sems.at[2]),
+        pltpu.make_async_copy(w_hbm, w, sems.at[1]),
     ]
     for i in range(chunks):
         part = pl.ds(i * step, step)
-        copies.append(pltpu.make_async_copy(edge_hbm.at[part, :], edge.at[part, :], sems.at[3 + i]))
-    for c in copies:
+        copies.append(pltpu.make_async_copy(edge_hbm.at[part, :], edge.at[part, :], sems.at[2 + i]))
+    extra = [
+        pltpu.make_async_copy(slots_hbm, slots_t, sems.at[2 + chunks]),
+        pltpu.make_async_copy(basis_hbm, basis, sems.at[3 + chunks]),
+    ]
+    for c in copies + extra:
         c.start()
     copies[0].wait()
+    hot = one_hot(rows[...], edges)
     copies[1].wait()
-    hot = one_hot(rows[...], edges)
-    local = target[...] - place("narrow", atoms)
-    count = edges // lanes
-    codes = [lax.shift_right_logical(local, 8), lax.bitwise_and(local, 255)]
-    parts = [c[:, i * lanes : (i + 1) * lanes] for c in codes for i in range(count)]
-    parts += [jnp.zeros_like(parts[0])] * (8 - len(parts))
-    code_rows = jnp.concatenate(parts, axis=0).astype(F32)
-    out[:, half:, :] = jnp.broadcast_to(code_rows[None], (peers, 8, lanes)).astype(BF16)
-    copies[2].wait()
     down_w = w[...]
     twice = jnp.concatenate([down_w, down_w], axis=0)
     down = []
     for i in range(chunks):
-        copies[3 + i].wait()
+        copies[2 + i].wait()
         down.append(silu(dot_nt(edge[i * step : (i + 1) * step, :], twice)).astype(BF16))
     picked = dot(hot, jnp.concatenate(down, axis=0))
     picked = picked.reshape(peers, 2 * half, lanes)
     low = iota((peers, half, lanes), 2) < width
     packed = jnp.where(low, picked[:, :half], picked[:, half:])
-    out[:, :half, :] = packed.astype(BF16)
+    out[...] = packed.astype(BF16)
+    for c in extra:
+        c.wait()
 
 
 def start_first(copies):
@@ -140,7 +150,7 @@
 
 
 def mixer_kernel(
-    cap, basis_hbm, slots_hbm, kept, rest_hbm, basis, slots_t, flat, spread, rest, sems
+    cap, basis, slots_t, kept, rest_hbm, flat, spread, rest, sems
 ):
     kept_count, edges, slots = kept.shape
     basis_count = kept_count + rest_hbm.shape[0]
@@ -148,16 +158,10 @@
     groups, span = flat.shape
     per = edges // groups
     total = basis.shape[1]
-    fetch = [
-        pltpu.make_async_copy(slots_hbm, slots_t, sems.at[0]),
-        pltpu.make_async_copy(basis_hbm, basis, sems.at[1]),
-    ]
-    start_first(fetch)
     rows, cols = iota((total, total), 0), iota((total, total), 1)
     order = quotient(rows, basis_count) + remainder(rows, basis_count) * triplets == cols
     order = jnp.where(order, 1.0, 0.0).astype(BF16)
     own = remainder(iota((edges, span), 0), per) == quotient(iota((edges, span), 1), triplets)
-    fetch[0].wait()
     half = cap // 2
     slot = slots_t[...]
     slot = (
@@ -173,7 +177,6 @@
     low = lax.bitwise_and(slot, 255).astype(F32).astype(BF16)
     wide = jnp.where(own, dot(high, tile) * 256.0 + dot(low, tile), 0.0)
     flat[...] = jnp.sum(wide.reshape(groups, per, span), axis=1).astype(jnp.int32)
-    fetch[1].wait()
     by_basis = dot(basis[...], order)
     pack = 128 // triplets
     turn = remainder(iota((edges, 128), 0), pack)
@@ -214,7 +217,7 @@
             one(unroll * i + u)
         return 0
 
-    chunks = sems.shape[0] - 2
+    chunks = sems.shape[0]
     steps = groups // 2 // unroll // chunks
     copies = []
     for c in range(chunks):
@@ -222,7 +225,7 @@
         size = steps * unroll * 2 * per
         part = pl.ds(c * size, size)
         copies.append(
-            pltpu.make_async_copy(rest.at[:, part, :], rest_hbm.at[:, part, :], sems.at[2 + c])
+            pltpu.make_async_copy(rest.at[:, part, :], rest_hbm.at[:, part, :], sems.at[c])
         )
         copies[-1].start()
     for c in copies:
@@ -230,7 +233,9 @@
 
 
 def edge_kernel(
+    atoms,
     received,
+    target,
     kept,
     rest_hbm,
     edge_hbm,
@@ -241,8 +246,7 @@
     *refs,
 ):
     *quarters, rest, edge_msg, w_bil_t, w_up, w_atom_in, edge_mid, message, sems = refs
-    peers, rows, lanes = received.shape
-    half = rows - 8
+    peers, half, lanes = received.shape
     width = w_bil_t.shape[0]
     pairs = [
         (rest_hbm, rest),
@@ -253,7 +257,7 @@
     ]
     copies = [pltpu.make_async_copy(a, b, sems.at[i]) for i, (a, b) in enumerate(pairs)]
     start_first(copies)
-    got = received[:, :half, :].astype(F32).reshape(peers * half, lanes).T
+    got = received[...].astype(F32).reshape(peers * half, lanes).T
     table = jnp.concatenate([got[:width], got[width:]], axis=1).astype(BF16)
     mixed = [dot_nt(table, kept[k]).astype(BF16) for k in range(kept.shape[0])]
     copies[0].wait()
@@ -267,31 +271,39 @@
     edge_mid[...] = mid
     store = pltpu.make_async_copy(edge_mid, mid_hbm, sems.at[len(pairs)])
     store.start()
+    local = target[...] - place("narrow", atoms)
+    codes = [lax.shift_right_logical(local, 8), lax.bitwise_and(local, 255)]
+    codes += [jnp.zeros_like(local)] * 14
+    codes = jnp.concatenate(codes, axis=0).astype(F32).astype(BF16)
     copies[4].wait()
-    message[...] = dot(mid, w_atom_in[...]).T
+    message[...] = dot(mid, w_atom_in[...]).T.astype(BF16)
     part = message.shape[0] // len(quarters)
     mine = lax.axis_index("wide") % len(quarters)
     for q, quarter in enumerate(quarters):
         at = pl.multiple_of((mine ^ q) * part, part)
-        quarter[...] = message[pl.ds(at, part), :].astype(BF16)
+        quarter[:part, :] = message[pl.ds(at, part), :]
+        quarter[part:, :] = codes
     store.wait()
 
 
 def picks_kernel(order, feats, count, *refs):
     wanted = refs[:count]
     atom_h, gain, w_hbm = refs[count : count + 3]
-    hots = refs[count + 3 : 2 * count + 3]
-    olds = refs[2 * count + 3 : 3 * count + 3]
-    gain_out, w_out, w, wide, tall, sem = refs[3 * count + 3 :]
+    *given, gain_out, w_out, w, wide, tall, sem = refs[count + 3 :]
     fetch = pltpu.make_async_copy(w_hbm, w, sem)
     fetch.start()
     atoms = atom_h.shape[0]
     me = lax.axis_index("wide")
     starts = [pl.multiple_of(where(me) * feats, feats) for where in order]
-    for want, hot, old in zip(wanted, hots, olds):
+    for i, want in enumerate(wanted):
         chosen = one_hot(want[...] - place("narrow", atoms), atoms)
-        hot[...] = chosen
-        old[...] = dot(chosen, atom_h[...]).astype(BF16)
+        value = dot(chosen, atom_h[...]).astype(BF16)
+        at = 0
+        for hot, old in zip(given[2 * i :: 2 * count], given[2 * i + 1 :: 2 * count]):
+            size = hot.shape[0]
+            hot[...] = chosen[at : at + size]
+            old[...] = value[at : at + size]
+            at += size
     tall[...] = jnp.broadcast_to(gain[...], (tall.shape[1], gain.shape[1])).T
     blocks = [tall[pl.ds(at, feats), :] for at in starts]
     gain_out[...] = jnp.concatenate(blocks, axis=0).T[:8]
@@ -301,25 +313,20 @@
     w_out[...] = jnp.concatenate(blocks, axis=0).astype(BF16)
 
 
-def sum_kernel(count, later, received, *refs):
+def sum_kernel(count, later, *refs):
     quarters, outs, total = refs[:count], refs[count + later : -1], refs[-1]
-    _, rows, lanes = received.shape
-    half = rows - 8
-    edges = quarters[0].shape[1]
-    parts = edges // lanes
     me = lax.axis_index("wide")
-    ids = iota((total.shape[1], lanes), 0).astype(F32)
+    part, atoms = total.shape
+    ids = iota((atoms, quarters[0].shape[1]), 0).astype(F32)
     value = jnp.zeros(total.shape, F32)
-    for q, quarter in enumerate(quarters):
-        codes = received[pl.ds(me ^ q, 1), half:, :].reshape(rows - half, lanes).astype(F32)
-        hot = [
-            jnp.where(ids == codes[i : i + 1] * 256.0 + codes[parts + i : parts + i + 1], 1.0, 0.0)
-            for i in range(parts)
-        ]
-        value += dot_nt(quarter[...], jnp.concatenate(hot, axis=1).astype(BF16))
+    for quarter in quarters:
+        codes = quarter[part:, :].astype(F32)
+        hot = jnp.where(ids == codes[0:1] * 256.0 + codes[1:2], 1.0, 0.0)
+        value += dot_nt(quarter[:part, :], hot.astype(BF16))
     total[...] = value
     feats = total.shape[0] // len(outs)
-    for k, out in enumerate(outs):
+    for i, out in enumerate(outs):
+        k = -i % len(outs)
         at = pl.multiple_of((me // count ^ k) * feats, feats)
         out[...] = total[pl.ds(at, feats), :].astype(out.dtype)
 
@@ -344,7 +351,7 @@
 
 def asked_kernel(count, *refs):
     sent = refs[len(refs) - count :]
-    hots, olds = refs[:count], refs[count : 2 * count]
+    hots, olds = refs[: 2 * count : 2], refs[1 : 2 * count : 2]
     gain, w_atom = refs[2 * count : 2 * count + 2]
     table = stacked(refs[2 * count + 2 : len(refs) - count])
     for hot, old, send in zip(hots, olds, sent):
@@ -367,27 +374,26 @@
     store.wait()
 
 
-def final_kernel(count, *refs):
+def final_kernel(count, start, *refs):
     partial, mid, w_src = refs[:3]
     rows = refs[3 : 3 + count]
-    out_hbm, out, sems = refs[3 + count :]
-    got = None
-    if rows:
-        got = rows[0][...].astype(F32)
-        for r in rows[1:]:
-            got = got + r[...].astype(F32)
-        got = got.astype(BF16)
+    out_hbm, out, sems = refs[-3:]
+    size = out.shape[0]
+    these = slice(start, start + size)
+    got = rows[0][...].astype(F32)
+    for r in rows[1:]:
+        got = got + r[...].astype(F32)
+    got = got.astype(BF16)
     chunks = sems.shape[0]
     step = out.shape[1] // chunks
     stores = []
     for c in range(chunks):
         part = slice(c * step, (c + 1) * step)
-        update = partial[:, part]
-        if rows:
-            update = update + dot(got, w_src[:, part])
-        out[:, part] = (mid[:, part].astype(F32) + silu(update)).astype(BF16)
+        update = partial[these, part] + dot(got, w_src[:, part])
+        out[:, part] = (mid[these, part].astype(F32) + silu(update)).astype(BF16)
         at = pl.ds(c * step, step)
-        stores.append(pltpu.make_async_copy(out.at[:, at], out_hbm.at[:, at], sems.at[c]))
+        to = out_hbm.at[pl.ds(start, size), at]
+        stores.append(pltpu.make_async_copy(out.at[:, at], to, sems.at[c]))
         stores[-1].start()
     for store in stores:
         store.wait()
@@ -477,6 +483,8 @@
     cap = slots // wide
     feats = da // wide
     lanes = 2 * width
+    bounds = [0, edges // 2, edges]
+    sizes = [b - a for a, b in zip(bounds, bounds[1:])]
     low = min(4, wide)
     high = wide // low
     big = (24 << 20) if slots <= 512 else (60 << 20)
@@ -486,21 +494,24 @@
     target = edge_target.reshape(1, edges)
     dma = pltpu.SemaphoreType.DMA
 
-    outgoing = call(
-        functools.partial(outgoing_kernel, atoms),
-        [HBM] * 4,
-        VMEM,
-        shape((wide, cap // 2 + 8, lanes), BF16),
+    outgoing, basis_near, slots_near = call(
+        outgoing_kernel,
+        [HBM] * 5,
+        [VMEM] * 3,
+        [
+            shape((wide, cap // 2, lanes), BF16),
+            shape(basis.shape, BF16),
+            shape((triplets, edges), jnp.int32),
+        ],
         big,
         scratch=[
             pltpu.VMEM((edges, de), BF16),
             pltpu.VMEM((width, de), BF16),
             pltpu.VMEM((1, slots), jnp.int32),
-            pltpu.VMEM((1, edges), jnp.int32),
-            dma((5,)),
+            dma((6,)),
         ],
         name="outgoing",
-    )(edge_msg, w_down.T, send_rows, target)
+    )(edge_msg, w_down.T, send_rows, basis, trip_slot.T)
     received = lax.all_to_all(outgoing, "wide", split_axis=0, concat_axis=0, tiled=True)
 
     per = 256 // triplets
@@ -508,27 +519,25 @@
     rest_shape = (basis_count - kept, edges, slots)
     mixer = call(
         functools.partial(mixer_kernel, cap),
-        [HBM, HBM],
+        [VMEM, VMEM],
         [VMEM, HBM],
         [shape((kept, edges, slots), BF16), shape(rest_shape, BF16)],
         big,
         scratch=[
-            pltpu.VMEM(basis.shape, BF16),
-            pltpu.VMEM((triplets, edges), jnp.int32),
             pltpu.VMEM((edges // per, per * triplets), jnp.int32),
             pltpu.VMEM(basis.shape, F32),
             pltpu.VMEM(rest_shape, BF16),
-            dma((6,)),
+            dma((4,)),
         ],
         cost=cost(2 * basis_count * edges * slots * 256, 6 << 20),
         name="mixer",
-    )(basis, trip_slot.T)
+    )(basis_near, slots_near)
 
     edge_mid, *quarters = call(
-        edge_kernel,
-        [VMEM] * 2 + [HBM] * 5,
+        functools.partial(edge_kernel, atoms),
+        [VMEM] * 3 + [HBM] * 5,
         [HBM] + [VMEM] * low,
-        [shape((edges, de), BF16)] + [shape((feats * high, edges), BF16)] * low,
+        [shape((edges, de), BF16)] + [shape((feats * high + 16, edges), BF16)] * low,
         big,
         scratch=[
             pltpu.VMEM(rest_shape, BF16),
@@ -537,11 +546,11 @@
             pltpu.VMEM(w_up.shape, BF16),
             pltpu.VMEM(w_atom_in.shape, BF16),
             pltpu.VMEM((edges, de), BF16),
-            pltpu.VMEM((da, edges), F32),
+            pltpu.VMEM((da, edges), BF16),
             dma((6,)),
         ],
         name="edge",
-    )(received, *mixer, edge_msg, w_bil.T, w_up, w_atom_in)
+    )(received, target, *mixer, edge_msg, w_bil.T, w_up, w_atom_in)
     def mirrored(value, flip):
         return lax.ppermute(value, "wide", [(i, i ^ flip) for i in range(wide)])
 
@@ -558,9 +567,8 @@
     *picks, gain_near, w_atom_near = call(
         functools.partial(picks_kernel, order, feats, len(wanted)),
         [VMEM] * (len(wanted) + 2) + [HBM],
-        [VMEM] * (2 * len(wanted) + 2),
-        [shape((edges, atoms), BF16)] * len(wanted)
-        + [shape((edges, da), BF16)] * len(wanted)
+        [VMEM] * (2 * len(sizes) * len(wanted) + 2),
+        [shape((n, w), BF16) for n in sizes for _ in wanted for w in (atoms, da)]
         + [shape((8, da), F32), shape(w_atom.shape, BF16)],
         big,
         scratch=[
@@ -574,15 +582,14 @@
     )(*wanted, atom_h, atom_gain.reshape(1, da), w_atom)
     sums = call(
         functools.partial(sum_kernel, low, len(wanted)),
-        [VMEM] * (1 + low) + [pl.BlockSpec(memory_space=pl.ANY)] * len(wanted),
+        [VMEM] * low + [pl.BlockSpec(memory_space=pl.ANY)] * len(wanted),
         [VMEM] * high,
         [shape((feats, atoms), F32)] + [shape((feats, atoms), BF16)] * (high - 1),
         big,
         scratch=[pltpu.VMEM((feats * high, atoms), F32)],
         name="sums",
-    )(received, *quarters, *wanted)
-    far = [mirrored(sums[k], k * low) for k in range(high - 1, 0, -1)]
-    sums = [sums[0]] + far[::-1]
+    )(*quarters, *wanted)
+    sums = [sums[0]] + [mirrored(v, -i % high * low) for i, v in enumerate(sums) if i]
     share = call(
         functools.partial(add_kernel, high),
         [VMEM] * high + [pl.BlockSpec(memory_space=pl.ANY)] * len(picks),
@@ -593,18 +600,23 @@
     )(*sums, *picks)
 
     pieces = [v for v, _ in gathered(share, wide, feats)]
-    asked = call(
-        functools.partial(asked_kernel, len(wanted)),
-        [VMEM] * (len(picks) + 2 + len(pieces)),
-        [VMEM] * len(wanted),
-        [shape((edges, da), BF16)] * len(wanted),
-        big,
-        name="asked",
-    )(*picks, gain_near, w_atom_near, *pieces)
-    rows = [
-        lax.ppermute(a, "narrow", [(i, (i - k) % narrow) for i in range(narrow)])
-        for k, a in enumerate(asked, start=1)
-    ]
+    rows = []
+    for h, size in enumerate(sizes):
+        given = picks[2 * len(wanted) * h : 2 * len(wanted) * (h + 1)]
+        asked = call(
+            functools.partial(asked_kernel, len(wanted)),
+            [VMEM] * (len(given) + 2 + len(pieces)),
+            [VMEM] * len(wanted),
+            [shape((size, da), BF16)] * len(wanted),
+            big,
+            name=f"asked{h}",
+        )(*given, gain_near, w_atom_near, *pieces)
+        rows.append(
+            [
+                lax.ppermute(a, "narrow", [(i, (i - k) % narrow) for i in range(narrow)])
+                for k, a in enumerate(asked, start=1)
+            ]
+        )
     atom_out, partial = call(
         local_kernel,
         [VMEM] * (7 + len(pieces)),
@@ -615,15 +627,22 @@
         cost=cost(4 * edges * da * de + 8 * edges * da * atoms, 4 << 20),
         name="local",
     )(gain_near, w_atom_near, atom_h, source, target, w_src, w_tgt, *pieces)
-    edge_out = call(
-        functools.partial(final_kernel, len(rows)),
-        [VMEM] * (3 + len(rows)),
-        HBM,
-        shape((edges, de), BF16),
-        big,
-        scratch=[pltpu.VMEM((edges, de), BF16), dma((4,))],
-        name="final",
-    )(partial, edge_mid, w_src, *rows)
+    edge_out = []
+    for h, got in enumerate(rows):
+        held = 3 + len(got) + len(edge_out)
+        edge_out = [
+            call(
+                functools.partial(final_kernel, len(got), bounds[h]),
+                [VMEM] * (3 + len(got)) + [HBM] * len(edge_out),
+                HBM,
+                shape((edges, de), BF16),
+                big,
+                scratch=[pltpu.VMEM((sizes[h], de), BF16), dma((2,))],
+                name=f"final{h}",
+                alias={held - 1: 0} if edge_out else {},
+            )(partial, edge_mid, w_src, *got, *edge_out)
+        ]
+    edge_out = edge_out[0]
     return (edge_out, atom_out)
 
 

time: 59.7 us -> 58 us (0.972)
  waiting for transfers between devices: 18.3 us -> 16.1 us
    ppermute x1 -> x2, waiting for transfers between devices: 4.69 us -> 2.43 us  [per_device(): lax.ppermute(a, 'narrow', [(i, (i - k) % narrow) for i in range(narrow)])]
    ppermute x6, waiting for transfers between devices: 4.41 us -> 3.23 us  [mirrored(): return lax.ppermute(value, 'wide', [(i, i ^ flip) for i in range(wide)])]
    ppermute x6, waiting for transfers between devices: 7.35 us -> 8.1 us  [gathered(): lax.ppermute(value, 'wide', pairs)]
    ppermute x1 -> x2, starting transfers between devices: 1.59 us -> 2.16 us  [per_device(): lax.ppermute(a, 'narrow', [(i, (i - k) % narrow) for i in range(narrow)])]
    pallas_call x9 -> x11, Pallas kernels: 17.7 us -> 18 us  [apply(): return run(*held)]
  transfers between devices with their start and end apart: 15 -> 16, of which waited for: 11 -> 11; matrix products, arithmetic and copies ran while one was open for 0% -> 0% of each run, Pallas kernels for 16% -> 17%
where the time goes in v4:
time: 58 us; the launch traced here: 57.8 us
  starting transfers between devices  22.9 us (39%)
  Pallas kernels  18 us (31%)
  waiting for transfers between devices  16.1 us (28%)
  between operations  0.79 us (1%)
    pallas_call x11, Pallas kernels, apply(): return run(*held)  18 us
    ppermute x6, waiting for transfers between devices, gathered(): lax.ppermute(value, 'wide', pairs)  8.1 us
    all_to_all x1, starting transfers between devices, per_device(): lax.all_to_all(outgoing, 'wide', split_axis=0, concat_axis=0, tiled=True)  7.39 us
    ppermute x6, starting transfers between devices, mirrored(): return lax.ppermute(value, 'wide', [(i, i ^ flip) for i in range(wide)])  6.37 us
    ppermute x6, starting transfers between devices, gathered(): lax.ppermute(value, 'wide', pairs)  5.46 us
    ppermute x6, waiting for transfers between devices, mirrored(): return lax.ppermute(value, 'wide', [(i, i ^ flip) for i in range(wide)])  3.23 us
    ppermute x2, waiting for transfers between devices, per_device(): lax.ppermute(a, 'narrow', [(i, (i - k) % narrow) for i in range(narrow)])  2.43 us
    all_to_all x1, waiting for transfers between devices, per_device(): lax.all_to_all(outgoing, 'wide', split_axis=0, concat_axis=0, tiled=True)  2.29 us
  transfers between devices with their start and end apart: 16, of which 11 were waited for; matrix products, arithmetic and copies ran while one was open for 0% of the time, Pallas kernels for 17%

profile of v4, /device:TPU:0, one launch (start us, length us, event | category | flops | bytes accessed | tf_op | source)
XLA Modules:
  0.0 57.8 jit_solution(885078908936586194)
XLA Ops:
  0.6 2.5 %outgoing.1 = (bf16[16,16,128]{2,1,0:T(8,128)(2,1)}, bf16[256,512]{1,0:T(8,128)(2,1)S(1)}, s32[32,256]{1,0:T(8,128)S(1)}) custom-call(bf16[256,1024]{1,0:T(8,128)(2,1)} %edge_hbm.3, bf16[64,1024]{1,0:T(8,128)(2,1)} %bitcast.12, s32[1,512]{1,0:T(1,128)} %rows_hbm.1, bf16[256,512]{1,0:T(8,128)(2,1)} %basis_hbm.1, s32[32,256]{1,0:T(8,128)} %bitcast.13), custom_call_target="tpu_custom_call" | custom-call | tf_op jit(solution)/shard_map/outgoing/pallas_call | solution.py:74
  3.2 7.4 %all-to-all-start = ((bf16[16,16,128]{2,1,0:T(8,128)(2,1)}), bf16[16,16,128]{2,1,0:T(8,128)(2,1)S(1)}, u32[]{:S(2)}, u32[]{:S(2)}) async-start(bf16[16,16,128]{2,1,0:T(8,128)(2,1)} %get-tuple-element.26), calls=%async_computation | async-start | bytes 131072 | tf_op jit(solution)/shard_map/all_to_all | solution.py:515
  10.6 4.6 %mixer.1 = (bf16[12,256,512]{2,1,0:T(8,128)(2,1)S(1)}, bf16[4,256,512]{2,1,0:T(8,128)(2,1)}) custom-call(bf16[256,512]{1,0:T(8,128)(2,1)S(1)} %get-tuple-element.27.basis, s32[32,256]{1,0:T(8,128)S(1)} %get-tuple-element.28.slots_t), custom_call_target="tpu_custom_call" | custom-call | flops 1073741824 | bytes 6291456 | tf_op jit(solution)/shard_map/mixer/pallas_call | solution.py:74
  15.2 2.3 %all-to-all-done.received = bf16[16,16,128]{2,1,0:T(8,128)(2,1)S(1)} async-done(((bf16[16,16,128]{2,1,0:T(8,128)(2,1)}), bf16[16,16,128]{2,1,0:T(8,128)(2,1)S(1)}, u32[]{:S(2)}, u32[]{:S(2)}) %all-to-all-start) | async-done | bytes 65568 | tf_op jit(solution)/shard_map/all_to_all | solution.py:515
  17.5 3.3 %edge.1 = (bf16[256,1024]{1,0:T(8,128)(2,1)}, bf16[144,256]{1,0:T(8,128)(2,1)S(1)}, bf16[144,256]{1,0:T(8,128)(2,1)S(1)}, bf16[144,256]{1,0:T(8,128)(2,1)S(1)}, bf16[144,256]{1,0:T(8,128)(2,1)S(1)}) custom-call(bf16[16,16,128]{2,1,0:T(8,128)(2,1)S(1)} %all-to-all-done.received, s32[1,256]{1,0:T(1,128)S(1)} %bitcast.7, ...), custom_call_target="tpu_custom_call" | custom-call | tf_op jit(solution)/shard_map/edge/pallas_call | solution.py:74
  20.9 0.2 collective-permute-start.2
  21.1 1.6 %collective-permute-start.3 = (bf16[144,256]{1,0:T(8,128)(2,1)S(1)}, bf16[144,256]{1,0:T(8,128)(2,1)S(1)}, u32[]{:S(2)}, u32[]{:S(2)}) collective-permute-start(bf16[144,256]{1,0:T(8,128)(2,1)S(1)} %get-tuple-element.38), channel_id=1, source_target_pairs={{0,6},{2,4},{4,2},{6,0},{8,14},{10,12},{12,10},{14,8},{16,22},{18,... | collective-permute-start | bytes 221192 | tf_op jit(solution)/shard_map/ppermute | solution.py:555
  22.7 1.5 %collective-permute-start.1 = (s32[1,256]{1,0:T(1,128)S(1)}, s32[1,256]{1,0:T(1,128)S(1)}, u32[]{:S(2)}, u32[]{:S(2)}) collective-permute-start(s32[1,256]{1,0:T(1,128)S(1)} %bitcast.9), channel_id=1, source_target_pairs={{0,1},{1,0},{2,3},{3,2},{4,5},{5,4},{6,7},{7,6},{8,9},{9,8},{10,11... | collective-permute-start | bytes 3080 | tf_op jit(solution)/shard_map/ppermute | solution.py:560
  24.3 1.8 %collective-permute-done.2.refs_2_ = bf16[144,256]{1,0:T(8,128)(2,1)S(1)} collective-permute-done((bf16[144,256]{1,0:T(8,128)(2,1)S(1)}, bf16[144,256]{1,0:T(8,128)(2,1)S(1)}, u32[]{:S(2)}, u32[]{:S(2)}) %collective-permute-start.2) | collective-permute-done | bytes 73760 | tf_op jit(solution)/shard_map/ppermute | solution.py:555
  26.1 0.5 collective-permute-done.3.refs_3_
  26.6 0.5 sums.1
  27.1 1.9 %collective-permute-start.4 = (bf16[32,512]{1,0:T(8,128)(2,1)S(1)}, bf16[32,512]{1,0:T(8,128)(2,1)S(1)}, u32[]{:S(2)}, u32[]{:S(2)}) collective-permute-start(bf16[32,512]{1,0:T(8,128)(2,1)S(1)} %get-tuple-element.40), channel_id=1, source_target_pairs={{0,24},{2,26},{4,28},{6,30},{8,16},{10,18},{12,20},{14,22},{16,8},... | collective-permute-start | bytes 98312 | tf_op jit(solution)/shard_map/ppermute | solution.py:555
  29.0 2.5 %collective-permute-start.6 = (bf16[32,512]{1,0:T(8,128)(2,1)S(1)}, bf16[32,512]{1,0:T(8,128)(2,1)S(1)}, u32[]{:S(2)}, u32[]{:S(2)}) collective-permute-start(bf16[32,512]{1,0:T(8,128)(2,1)S(1)} %get-tuple-element.42), channel_id=1, source_target_pairs={{0,8},{2,10},{4,12},{6,14},{8,0},{10,2},{12,4},{14,6},{16,24},{18,... | collective-permute-start | bytes 98312 | tf_op jit(solution)/shard_map/ppermute | solution.py:555
  31.5 1.6 %picks.1 = (bf16[128,512]{1,0:T(8,128)(2,1)S(1)}, bf16[128,512]{1,0:T(8,128)(2,1)S(1)}, bf16[128,512]{1,0:T(8,128)(2,1)S(1)}, bf16[128,512]{1,0:T(8,128)(2,1)S(1...) custom-call(s32[1,256]{1,0:T(1,128)S(1)} %collective-permute-done.1.refs_0_.refs_4_, ...), custom_call_target="tpu_custom_call" | custom-call | flops 67108864 | bytes 2097152 | tf_op jit(solution)/shard_map/picks/pallas_call | solution.py:74
  33.2 0.8 %collective-permute-done.5.refs_2_ = bf16[32,512]{1,0:T(8,128)(2,1)S(1)} collective-permute-done((bf16[32,512]{1,0:T(8,128)(2,1)S(1)}, bf16[32,512]{1,0:T(8,128)(2,1)S(1)}, u32[]{:S(2)}, u32[]{:S(2)}) %collective-permute-start.5) | collective-permute-done | bytes 32800 | tf_op jit(solution)/shard_map/ppermute | solution.py:555
  34.1 1.9 %collective-permute-start.9 = (bf16[32,512]{1,0:T(8,128)(2,1)S(1)}, bf16[32,512]{1,0:T(8,128)(2,1)S(1)}, u32[]{:S(2)}, u32[]{:S(2)}) collective-permute-start(bf16[32,512]{1,0:T(8,128)(2,1)S(1)} %add.1), channel_id=1, source_target_pairs={{0,24},{2,26},{4,28},{6,30},{8,16},{10,18},{12,20},{14,22},{16,8},... | collective-permute-start | bytes 98312 | tf_op jit(solution)/shard_map/ppermute | solution.py:441
  36.0 1.0 %collective-permute-start.8 = (bf16[32,512]{1,0:T(8,128)(2,1)S(1)}, bf16[32,512]{1,0:T(8,128)(2,1)S(1)}, u32[]{:S(2)}, u32[]{:S(2)}) collective-permute-start(bf16[32,512]{1,0:T(8,128)(2,1)S(1)} %add.1), channel_id=1, source_target_pairs={{0,16},{2,18},{4,20},{6,22},{8,24},{10,26},{12,28},{14,30},{16,0},... | collective-permute-start | bytes 98312 | tf_op jit(solution)/shard_map/ppermute | solution.py:441
  37.0 1.5 %collective-permute-start.7 = (bf16[32,512]{1,0:T(8,128)(2,1)S(1)}, bf16[32,512]{1,0:T(8,128)(2,1)S(1)}, u32[]{:S(2)}, u32[]{:S(2)}) collective-permute-start(bf16[32,512]{1,0:T(8,128)(2,1)S(1)} %add.1), channel_id=1, source_target_pairs={{0,8},{2,10},{4,12},{6,14},{8,0},{10,2},{12,4},{14,6},{16,24},{18,... | collective-permute-start | bytes 98312 | tf_op jit(solution)/shard_map/ppermute | solution.py:441
  38.5 1.4 %collective-permute-done.9 = bf16[32,512]{1,0:T(8,128)(2,1)S(1)} collective-permute-done((bf16[32,512]{1,0:T(8,128)(2,1)S(1)}, bf16[32,512]{1,0:T(8,128)(2,1)S(1)}, u32[]{:S(2)}, u32[]{:S(2)}) %collective-permute-start.9) | collective-permute-done | bytes 32800 | tf_op jit(solution)/shard_map/ppermute | solution.py:441
  39.9 1.2 %collective-permute-done.8 = bf16[32,512]{1,0:T(8,128)(2,1)S(1)} collective-permute-done((bf16[32,512]{1,0:T(8,128)(2,1)S(1)}, bf16[32,512]{1,0:T(8,128)(2,1)S(1)}, u32[]{:S(2)}, u32[]{:S(2)}) %collective-permute-start.8) | collective-permute-done | bytes 32800 | tf_op jit(solution)/shard_map/ppermute | solution.py:441
  41.3 1.0 %collective-permute-start.11 = (bf16[128,512]{1,0:T(8,128)(2,1)S(1)}, bf16[128,512]{1,0:T(8,128)(2,1)S(1)}, u32[]{:S(2)}, u32[]{:S(2)}) collective-permute-start(bf16[128,512]{1,0:T(8,128)(2,1)S(1)} %pad_maximum_fusion.refs_0_.refs_4_), channel_id=1, source_target_pairs={{0,4},{2,6},{4,0},{6,2},{8,12},{10,14},{12,8},{14,10},{16,20},{18,... | collective-permute-start | bytes 393224 | tf_op jit(solution)/shard_map/ppermute | solution.py:441
  42.3 4.0 %collective-permute-done.11.refs_2_.refs_6_ = bf16[128,512]{1,0:T(8,128)(2,1)S(1)} collective-permute-done((bf16[128,512]{1,0:T(8,128)(2,1)S(1)}, bf16[128,512]{1,0:T(8,128)(2,1)S(1)}, u32[]{:S(2)}, u32[]{:S(2)}) %collective-permute-start.11) | collective-permute-done | bytes 131104 | tf_op jit(solution)/shard_map/ppermute | solution.py:441
  46.3 1.3 %collective-permute-done.12.refs_3_.refs_7_ = bf16[128,512]{1,0:T(8,128)(2,1)S(1)} collective-permute-done((bf16[128,512]{1,0:T(8,128)(2,1)S(1)}, bf16[128,512]{1,0:T(8,128)(2,1)S(1)}, u32[]{:S(2)}, u32[]{:S(2)}) %collective-permute-start.12) | collective-permute-done | bytes 131104 | tf_op jit(solution)/shard_map/ppermute | solution.py:441
  47.7 0.6 %asked0.1 = bf16[128,512]{1,0:T(8,128)(2,1)S(1)} custom-call(bf16[128,512]{1,0:T(8,128)(2,1)S(1)} %get-tuple-element.43.refs_4_.refs_0_, bf16[128,512]{1,0:T(8,128)(2,1)S(1)} %get-tuple-element.44.refs_5_.refs_1_, f32[8,512]{1,0:T(8,128)S(1)} %get-tuple-element.33.gain.refs_2_, bf16[512,512]{1,0:T(8,128)(2,1)S(1)} %get-tuple-element.34.w_atom.refs_3_, ...), custom_call_target="tpu_custom_call" | custom-call | tf_op jit(solution)/shard_map/asked0/pallas_call | solution.py:74
  48.3 1.6 %collective-permute-start.14 = (bf16[128,512]{1,0:T(8,128)(2,1)S(1)}, bf16[128,512]{1,0:T(8,128)(2,1)S(1)}, u32[]{:S(2)}, u32[]{:S(2)}) collective-permute-start(bf16[128,512]{1,0:T(8,128)(2,1)S(1)} %asked0.1), channel_id=1, source_target_pairs={{0,1},{1,0},{2,3},{3,2},{4,5},{5,4},{6,7},{7,6},{8,9},{9,8},{10,11... | collective-permute-start | bytes 393224 | tf_op jit(solution)/shard_map/ppermute | solution.py:616
  49.9 0.6 %asked1.1 = bf16[128,512]{1,0:T(8,128)(2,1)S(1)} custom-call(bf16[128,512]{1,0:T(8,128)(2,1)S(1)} %get-tuple-element.45.refs_6_.refs_0_, bf16[128,512]{1,0:T(8,128)(2,1)S(1)} %get-tuple-element.46.refs_7_.refs_1_, f32[8,512]{1,0:T(8,128)S(1)} %get-tuple-element.33.gain.refs_2_, bf16[512,512]{1,0:T(8,128)(2,1)S(1)} %get-tuple-element.34.w_atom.refs_3_, ...), custom_call_target="tpu_custom_call" | custom-call | tf_op jit(solution)/shard_map/asked1/pallas_call | solution.py:74
  50.5 0.6 collective-permute-start.13
  51.1 2.1 %local.1 = (bf16[512,512]{1,0:T(8,128)(2,1)}, f32[256,1024]{1,0:T(8,128)S(1)}) custom-call(f32[8,512]{1,0:T(8,128)S(1)} %get-tuple-element.33.gain.refs_2_, bf16[512,512]{1,0:T(8,128)(2,1)S(1)} %get-tuple-element.34.w_atom.refs_3_, bf16[512,512]{1,0:T(8,128)(2,1)S(1)} %copy-done.2, s32[1,256]{1,0:T(1,128)S(1)} %bitcast.10, s32[1,256]{1,0:T(1,128)S(1)} %bitcast.8, ...), custom_call_target="tpu_custom_call" | custom-call | flops 1073741824 | bytes 4194304 | tf_op jit(solution)/shard_map/local/pallas_call | solution.py:74
  53.2 1.5 %collective-permute-done.14.refs_3_ = bf16[128,512]{1,0:T(8,128)(2,1)S(1)} collective-permute-done((bf16[128,512]{1,0:T(8,128)(2,1)S(1)}, bf16[128,512]{1,0:T(8,128)(2,1)S(1)}, u32[]{:S(2)}, u32[]{:S(2)}) %collective-permute-start.14) | collective-permute-done | bytes 131104 | tf_op jit(solution)/shard_map/ppermute | solution.py:616
  54.7 1.1 %final0.1.refs_4_ = bf16[256,1024]{1,0:T(8,128)(2,1)} custom-call(f32[256,1024]{1,0:T(8,128)S(1)} %get-tuple-element.47.refs_0_, bf16[256,1024]{1,0:T(8,128)(2,1)S(1)} %copy-done.1, bf16[512,1024]{1,0:T(8,128)(2,1)S(1)} %copy-done, bf16[128,512]{1,0:T(8,128)(2,1)S(1)} %collective-permute-done.14.refs_3_), custom_call_target="tpu_custom_call" | custom-call | tf_op jit(solution)/shard_map/final0/pallas_call | solution.py:74
  55.8 0.9 %collective-permute-done.13.refs_3_ = bf16[128,512]{1,0:T(8,128)(2,1)S(1)} collective-permute-done((bf16[128,512]{1,0:T(8,128)(2,1)S(1)}, bf16[128,512]{1,0:T(8,128)(2,1)S(1)}, u32[]{:S(2)}, u32[]{:S(2)}) %collective-permute-start.13) | collective-permute-done | bytes 131104 | tf_op jit(solution)/shard_map/ppermute | solution.py:616
  56.7 1.1 %final1.1 = bf16[256,1024]{1,0:T(8,128)(2,1)} custom-call(f32[256,1024]{1,0:T(8,128)S(1)} %get-tuple-element.47.refs_0_, bf16[256,1024]{1,0:T(8,128)(2,1)S(1)} %copy-done.1, bf16[512,1024]{1,0:T(8,128)(2,1)S(1)} %copy-done, bf16[128,512]{1,0:T(8,128)(2,1)S(1)} %collective-permute-done.13.refs_3_, ...), custom_call_target="tpu_custom_call", output_to_operand_aliasing={{}: (4, {})} | custom-call | tf_op jit(solution)/shard_map/final1/pallas_call | solution.py:74
  (26 shorter events, 0.4 us)
Async XLA Ops:
  0.6 16.8 %copy-start.4 = (s32[256]{0:T(256)S(1)}, s32[256]{0:T(256)}, u32[]{:S(2)}) copy-start(s32[256]{0:T(256)} %param.19) | copy-start | bytes 3076
  3.2 14.3 %all-to-all-start = ((bf16[16,16,128]{2,1,0:T(8,128)(2,1)}), bf16[16,16,128]{2,1,0:T(8,128)(2,1)S(1)}, u32[]{:S(2)}, u32[]{:S(2)}) async-start(bf16[16,16,128]{2,1,0:T(8,128)(2,1)} %get-tuple-element.26), calls=%async_computation | async-start | bytes 131072 | tf_op jit(solution)/shard_map/all_to_all | solution.py:515
  15.2 7.6 %copy-start.6 = (s32[256]{0:T(256)S(1)}, s32[256]{0:T(256)}, u32[]{:S(2)}) copy-start(s32[256]{0:T(256)} %param.18) | copy-start | bytes 3076
  17.5 14.1 %copy-start.2 = (bf16[512,512]{1,0:T(8,128)(2,1)S(1)}, bf16[512,512]{1,0:T(8,128)(2,1)}, u32[]{:S(2)}) copy-start(bf16[512,512]{1,0:T(8,128)(2,1)} %atom_h.1) | copy-start | bytes 1572868
  17.5 14.1 %copy-start.3 = (f32[512]{0:T(512)S(1)}, f32[512]{0:T(512)}, u32[]{:S(2)}) copy-start(f32[512]{0:T(512)} %param.26) | copy-start | bytes 6148
  20.8 30.3 %copy-start = (bf16[512,1024]{1,0:T(8,128)(2,1)S(1)}, bf16[512,1024]{1,0:T(8,128)(2,1)}, u32[]{:S(2)}) copy-start(bf16[512,1024]{1,0:T(8,128)(2,1)} %refs_2_.3) | copy-start | bytes 3145732
  20.8 30.3 %copy-start.5 = (bf16[512,1024]{1,0:T(8,128)(2,1)S(1)}, bf16[512,1024]{1,0:T(8,128)(2,1)}, u32[]{:S(2)}) copy-start(bf16[512,1024]{1,0:T(8,128)(2,1)} %w_tgt.1) | copy-start | bytes 3145732
  20.8 1.9 %collective-permute-start = (bf16[144,256]{1,0:T(8,128)(2,1)S(1)}, bf16[144,256]{1,0:T(8,128)(2,1)S(1)}, u32[]{:S(2)}, u32[]{:S(2)}) collective-permute-start(bf16[144,256]{1,0:T(8,128)(2,1)S(1)} %get-tuple-element.31), channel_id=1, source_target_pairs={{0,2},{2,0},{4,6},{6,4},{8,10},{10,8},{12,14},{14,12},{16,18},{18,... | collective-permute-start | bytes 221192 | tf_op jit(solution)/shard_map/ppermute | solution.py:555
  20.9 5.2 %collective-permute-start.2 = (bf16[144,256]{1,0:T(8,128)(2,1)S(1)}, bf16[144,256]{1,0:T(8,128)(2,1)S(1)}, u32[]{:S(2)}, u32[]{:S(2)}) collective-permute-start(bf16[144,256]{1,0:T(8,128)(2,1)S(1)} %get-tuple-element.37), channel_id=1, source_target_pairs={{0,4},{2,6},{4,0},{6,2},{8,12},{10,14},{12,8},{14,10},{16,20},{18,... | collective-permute-start | bytes 221192 | tf_op jit(solution)/shard_map/ppermute | solution.py:555
  21.1 5.5 %collective-permute-start.3 = (bf16[144,256]{1,0:T(8,128)(2,1)S(1)}, bf16[144,256]{1,0:T(8,128)(2,1)S(1)}, u32[]{:S(2)}, u32[]{:S(2)}) collective-permute-start(bf16[144,256]{1,0:T(8,128)(2,1)S(1)} %get-tuple-element.38), channel_id=1, source_target_pairs={{0,6},{2,4},{4,2},{6,0},{8,14},{10,12},{12,10},{14,8},{16,22},{18,... | collective-permute-start | bytes 221192 | tf_op jit(solution)/shard_map/ppermute | solution.py:555
  22.7 3.9 %collective-permute-start.1 = (s32[1,256]{1,0:T(1,128)S(1)}, s32[1,256]{1,0:T(1,128)S(1)}, u32[]{:S(2)}, u32[]{:S(2)}) collective-permute-start(s32[1,256]{1,0:T(1,128)S(1)} %bitcast.9), channel_id=1, source_target_pairs={{0,1},{1,0},{2,3},{3,2},{4,5},{5,4},{6,7},{7,6},{8,9},{9,8},{10,11... | collective-permute-start | bytes 3080 | tf_op jit(solution)/shard_map/ppermute | solution.py:560
  27.1 6.1 %collective-permute-start.4 = (bf16[32,512]{1,0:T(8,128)(2,1)S(1)}, bf16[32,512]{1,0:T(8,128)(2,1)S(1)}, u32[]{:S(2)}, u32[]{:S(2)}) collective-permute-start(bf16[32,512]{1,0:T(8,128)(2,1)S(1)} %get-tuple-element.40), channel_id=1, source_target_pairs={{0,24},{2,26},{4,28},{6,30},{8,16},{10,18},{12,20},{14,22},{16,8},... | collective-permute-start | bytes 98312 | tf_op jit(solution)/shard_map/ppermute | solution.py:555
  29.0 5.0 %collective-permute-start.5 = (bf16[32,512]{1,0:T(8,128)(2,1)S(1)}, bf16[32,512]{1,0:T(8,128)(2,1)S(1)}, u32[]{:S(2)}, u32[]{:S(2)}) collective-permute-start(bf16[32,512]{1,0:T(8,128)(2,1)S(1)} %get-tuple-element.41), channel_id=1, source_target_pairs={{0,16},{2,18},{4,20},{6,22},{8,24},{10,26},{12,28},{14,30},{16,0},... | collective-permute-start | bytes 98312 | tf_op jit(solution)/shard_map/ppermute | solution.py:555
  29.0 5.1 %collective-permute-start.6 = (bf16[32,512]{1,0:T(8,128)(2,1)S(1)}, bf16[32,512]{1,0:T(8,128)(2,1)S(1)}, u32[]{:S(2)}, u32[]{:S(2)}) collective-permute-start(bf16[32,512]{1,0:T(8,128)(2,1)S(1)} %get-tuple-element.42), channel_id=1, source_target_pairs={{0,8},{2,10},{4,12},{6,14},{8,0},{10,2},{12,4},{14,6},{16,24},{18,... | collective-permute-start | bytes 98312 | tf_op jit(solution)/shard_map/ppermute | solution.py:555
  34.1 5.8 %collective-permute-start.9 = (bf16[32,512]{1,0:T(8,128)(2,1)S(1)}, bf16[32,512]{1,0:T(8,128)(2,1)S(1)}, u32[]{:S(2)}, u32[]{:S(2)}) collective-permute-start(bf16[32,512]{1,0:T(8,128)(2,1)S(1)} %add.1), channel_id=1, source_target_pairs={{0,24},{2,26},{4,28},{6,30},{8,16},{10,18},{12,20},{14,22},{16,8},... | collective-permute-start | bytes 98312 | tf_op jit(solution)/shard_map/ppermute | solution.py:441
  36.0 5.1 %collective-permute-start.8 = (bf16[32,512]{1,0:T(8,128)(2,1)S(1)}, bf16[32,512]{1,0:T(8,128)(2,1)S(1)}, u32[]{:S(2)}, u32[]{:S(2)}) collective-permute-start(bf16[32,512]{1,0:T(8,128)(2,1)S(1)} %add.1), channel_id=1, source_target_pairs={{0,16},{2,18},{4,20},{6,22},{8,24},{10,26},{12,28},{14,30},{16,0},... | collective-permute-start | bytes 98312 | tf_op jit(solution)/shard_map/ppermute | solution.py:441
  37.0 4.3 %collective-permute-start.7 = (bf16[32,512]{1,0:T(8,128)(2,1)S(1)}, bf16[32,512]{1,0:T(8,128)(2,1)S(1)}, u32[]{:S(2)}, u32[]{:S(2)}) collective-permute-start(bf16[32,512]{1,0:T(8,128)(2,1)S(1)} %add.1), channel_id=1, source_target_pairs={{0,8},{2,10},{4,12},{6,14},{8,0},{10,2},{12,4},{14,6},{16,24},{18,... | collective-permute-start | bytes 98312 | tf_op jit(solution)/shard_map/ppermute | solution.py:441
  41.3 5.0 %collective-permute-start.11 = (bf16[128,512]{1,0:T(8,128)(2,1)S(1)}, bf16[128,512]{1,0:T(8,128)(2,1)S(1)}, u32[]{:S(2)}, u32[]{:S(2)}) collective-permute-start(bf16[128,512]{1,0:T(8,128)(2,1)S(1)} %pad_maximum_fusion.refs_0_.refs_4_), channel_id=1, source_target_pairs={{0,4},{2,6},{4,0},{6,2},{8,12},{10,14},{12,8},{14,10},{16,20},{18,... | collective-permute-start | bytes 393224 | tf_op jit(solution)/shard_map/ppermute | solution.py:441
  42.3 4.0 %collective-permute-start.10 = (bf16[128,512]{1,0:T(8,128)(2,1)S(1)}, bf16[128,512]{1,0:T(8,128)(2,1)S(1)}, u32[]{:S(2)}, u32[]{:S(2)}) collective-permute-start(bf16[128,512]{1,0:T(8,128)(2,1)S(1)} %pad_maximum_fusion.refs_0_.refs_4_), channel_id=1, source_target_pairs={{0,2},{2,0},{4,6},{6,4},{8,10},{10,8},{12,14},{14,12},{16,18},{18,... | collective-permute-start | bytes 393224 | tf_op jit(solution)/shard_map/ppermute | solution.py:441
  46.3 1.3 %collective-permute-start.12 = (bf16[128,512]{1,0:T(8,128)(2,1)S(1)}, bf16[128,512]{1,0:T(8,128)(2,1)S(1)}, u32[]{:S(2)}, u32[]{:S(2)}) collective-permute-start(bf16[128,512]{1,0:T(8,128)(2,1)S(1)} %collective-permute-done.11.refs_2_.refs_6_), channel_id=1, source_target_pairs={{0,2},{2,0},{4,6},{6,4},{8,10},{10,8},{12,14},{14,12},{16,18},{18,... | collective-permute-start | bytes 393224 | tf_op jit(solution)/shard_map/ppermute | solution.py:441
  47.7 7.1 %copy-start.1 = (bf16[256,1024]{1,0:T(8,128)(2,1)S(1)}, bf16[256,1024]{1,0:T(8,128)(2,1)}, u32[]{:S(2)}) copy-start(bf16[256,1024]{1,0:T(8,128)(2,1)} %get-tuple-element.48.refs_1_) | copy-start | bytes 1572868
  48.3 6.4 %collective-permute-start.14 = (bf16[128,512]{1,0:T(8,128)(2,1)S(1)}, bf16[128,512]{1,0:T(8,128)(2,1)S(1)}, u32[]{:S(2)}, u32[]{:S(2)}) collective-permute-start(bf16[128,512]{1,0:T(8,128)(2,1)S(1)} %asked0.1), channel_id=1, source_target_pairs={{0,1},{1,0},{2,3},{3,2},{4,5},{5,4},{6,7},{7,6},{8,9},{9,8},{10,11... | collective-permute-start | bytes 393224 | tf_op jit(solution)/shard_map/ppermute | solution.py:616
  50.5 6.2 %collective-permute-start.13 = (bf16[128,512]{1,0:T(8,128)(2,1)S(1)}, bf16[128,512]{1,0:T(8,128)(2,1)S(1)}, u32[]{:S(2)}, u32[]{:S(2)}) collective-permute-start(bf16[128,512]{1,0:T(8,128)(2,1)S(1)} %asked1.1), channel_id=1, source_target_pairs={{0,1},{1,0},{2,3},{3,2},{4,5},{5,4},{6,7},{7,6},{8,9},{9,8},{10,11... | collective-permute-start | bytes 393224 | tf_op jit(solution)/shard_map/ppermute | solution.py:616

commit v5 on v4

--- a/solution.py
+++ b/solution.py
@@ -443,12 +443,15 @@
                     )
                 )
             if size > 2:
-                fresh.append(
-                    (
-                        None if value is None else jnp.concatenate([v for v, _ in got], axis=0),
-                        [o for _, os in got for o in os],
+                ranked = [got[0]] + got[:0:-1]
+                for part in (ranked[: size // 2], ranked[size // 2 :]):
+                    values = [v for v, _ in part]
+                    fresh.append(
+                        (
+                            None if value is None else jnp.concatenate(values, axis=0),
+                            [o for _, os in part for o in os],
+                        )
                     )
-                )
             else:
                 fresh.extend(got)
         groups = fresh

time: 58 us -> 57.3 us (0.988)
  waiting for transfers between devices: 16.1 us -> 13.8 us
  starting transfers between devices: 22.9 us -> 24.4 us
    ppermute x6 -> x9, waiting for transfers between devices: 8.1 us -> 5.8 us  [gathered(): lax.ppermute(value, 'wide', pairs)]
    ppermute x6 -> x9, starting transfers between devices: 5.46 us -> 6.98 us  [gathered(): lax.ppermute(value, 'wide', pairs)]
  transfers between devices with their start and end apart: 16 -> 19, of which waited for: 11 -> 11; matrix products, arithmetic and copies ran while one was open for 0% -> 0% of each run, Pallas kernels for 17% -> 18%
where the time goes in v5:
time: 57.3 us; the launch traced here: 57 us
  starting transfers between devices  24.4 us (43%)
  Pallas kernels  18 us (31%)
  waiting for transfers between devices  13.8 us (24%)
  between operations  0.8 us (1%)
    pallas_call x11, Pallas kernels, apply(): return run(*held)  18 us
    all_to_all x1, starting transfers between devices, per_device(): lax.all_to_all(outgoing, 'wide', split_axis=0, concat_axis=0, tiled=True)  7.39 us
    ppermute x9, starting transfers between devices, gathered(): lax.ppermute(value, 'wide', pairs)  6.98 us
    ppermute x6, starting transfers between devices, mirrored(): return lax.ppermute(value, 'wide', [(i, i ^ flip) for i in range(wide)])  6.37 us
    ppermute x9, waiting for transfers between devices, gathered(): lax.ppermute(value, 'wide', pairs)  5.8 us
    ppermute x6, waiting for transfers between devices, mirrored(): return lax.ppermute(value, 'wide', [(i, i ^ flip) for i in range(wide)])  3.23 us
    ppermute x2, waiting for transfers between devices, per_device(): lax.ppermute(a, 'narrow', [(i, (i - k) % narrow) for i in range(narrow)])  2.44 us
    all_to_all x1, waiting for transfers between devices, per_device(): lax.all_to_all(outgoing, 'wide', split_axis=0, concat_axis=0, tiled=True)  2.3 us
  transfers between devices with their start and end apart: 19, of which 11 were waited for; matrix products, arithmetic and copies ran while one was open for 0% of the time, Pallas kernels for 18%

profile of v5, /device:TPU:0, one launch (start us, length us, event | category | flops | bytes accessed | tf_op | source)
XLA Modules:
  0.0 57.0 jit_solution(5448377191235878234)
XLA Ops:
  0.6 2.5 %outgoing.1 = (bf16[16,16,128]{2,1,0:T(8,128)(2,1)}, bf16[256,512]{1,0:T(8,128)(2,1)S(1)}, s32[32,256]{1,0:T(8,128)S(1)}) custom-call(bf16[256,1024]{1,0:T(8,128)(2,1)} %edge_hbm.3, bf16[64,1024]{1,0:T(8,128)(2,1)} %bitcast.12, s32[1,512]{1,0:T(1,128)} %rows_hbm.1, bf16[256,512]{1,0:T(8,128)(2,1)} %basis_hbm.1, s32[32,256]{1,0:T(8,128)} %bitcast.13), custom_call_target="tpu_custom_call" | custom-call | tf_op jit(solution)/shard_map/outgoing/pallas_call | solution.py:74
  3.2 7.4 %all-to-all-start = ((bf16[16,16,128]{2,1,0:T(8,128)(2,1)}), bf16[16,16,128]{2,1,0:T(8,128)(2,1)S(1)}, u32[]{:S(2)}, u32[]{:S(2)}) async-start(bf16[16,16,128]{2,1,0:T(8,128)(2,1)} %get-tuple-element.26), calls=%async_computation | async-start | bytes 131072 | tf_op jit(solution)/shard_map/all_to_all | solution.py:518
  10.6 4.6 %mixer.1 = (bf16[12,256,512]{2,1,0:T(8,128)(2,1)S(1)}, bf16[4,256,512]{2,1,0:T(8,128)(2,1)}) custom-call(bf16[256,512]{1,0:T(8,128)(2,1)S(1)} %get-tuple-element.27.basis, s32[32,256]{1,0:T(8,128)S(1)} %get-tuple-element.28.slots_t), custom_call_target="tpu_custom_call" | custom-call | flops 1073741824 | bytes 6291456 | tf_op jit(solution)/shard_map/mixer/pallas_call | solution.py:74
  15.2 2.3 %all-to-all-done.received = bf16[16,16,128]{2,1,0:T(8,128)(2,1)S(1)} async-done(((bf16[16,16,128]{2,1,0:T(8,128)(2,1)}), bf16[16,16,128]{2,1,0:T(8,128)(2,1)S(1)}, u32[]{:S(2)}, u32[]{:S(2)}) %all-to-all-start) | async-done | bytes 65568 | tf_op jit(solution)/shard_map/all_to_all | solution.py:518
  17.5 3.3 %edge.1 = (bf16[256,1024]{1,0:T(8,128)(2,1)}, bf16[144,256]{1,0:T(8,128)(2,1)S(1)}, bf16[144,256]{1,0:T(8,128)(2,1)S(1)}, bf16[144,256]{1,0:T(8,128)(2,1)S(1)}, bf16[144,256]{1,0:T(8,128)(2,1)S(1)}) custom-call(bf16[16,16,128]{2,1,0:T(8,128)(2,1)S(1)} %all-to-all-done.received, s32[1,256]{1,0:T(1,128)S(1)} %bitcast.7, ...), custom_call_target="tpu_custom_call" | custom-call | tf_op jit(solution)/shard_map/edge/pallas_call | solution.py:74
  21.1 1.6 %collective-permute-start.3 = (bf16[144,256]{1,0:T(8,128)(2,1)S(1)}, bf16[144,256]{1,0:T(8,128)(2,1)S(1)}, u32[]{:S(2)}, u32[]{:S(2)}) collective-permute-start(bf16[144,256]{1,0:T(8,128)(2,1)S(1)} %get-tuple-element.38), channel_id=1, source_target_pairs={{0,6},{2,4},{4,2},{6,0},{8,14},{10,12},{12,10},{14,8},{16,22},{18,... | collective-permute-start | bytes 221192 | tf_op jit(solution)/shard_map/ppermute | solution.py:558
  22.7 1.5 %collective-permute-start.1 = (s32[1,256]{1,0:T(1,128)S(1)}, s32[1,256]{1,0:T(1,128)S(1)}, u32[]{:S(2)}, u32[]{:S(2)}) collective-permute-start(s32[1,256]{1,0:T(1,128)S(1)} %bitcast.9), channel_id=1, source_target_pairs={{0,1},{1,0},{2,3},{3,2},{4,5},{5,4},{6,7},{7,6},{8,9},{9,8},{10,11... | collective-permute-start | bytes 3080 | tf_op jit(solution)/shard_map/ppermute | solution.py:563
  24.3 1.8 %collective-permute-done.2.refs_2_ = bf16[144,256]{1,0:T(8,128)(2,1)S(1)} collective-permute-done((bf16[144,256]{1,0:T(8,128)(2,1)S(1)}, bf16[144,256]{1,0:T(8,128)(2,1)S(1)}, u32[]{:S(2)}, u32[]{:S(2)}) %collective-permute-start.2) | collective-permute-done | bytes 73760 | tf_op jit(solution)/shard_map/ppermute | solution.py:558
  26.1 0.5 collective-permute-done.3.refs_3_
  27.1 1.9 %collective-permute-start.4 = (bf16[32,512]{1,0:T(8,128)(2,1)S(1)}, bf16[32,512]{1,0:T(8,128)(2,1)S(1)}, u32[]{:S(2)}, u32[]{:S(2)}) collective-permute-start(bf16[32,512]{1,0:T(8,128)(2,1)S(1)} %get-tuple-element.40), channel_id=1, source_target_pairs={{0,24},{2,26},{4,28},{6,30},{8,16},{10,18},{12,20},{14,22},{16,8},... | collective-permute-start | bytes 98312 | tf_op jit(solution)/shard_map/ppermute | solution.py:558
  29.0 2.5 %collective-permute-start.6 = (bf16[32,512]{1,0:T(8,128)(2,1)S(1)}, bf16[32,512]{1,0:T(8,128)(2,1)S(1)}, u32[]{:S(2)}, u32[]{:S(2)}) collective-permute-start(bf16[32,512]{1,0:T(8,128)(2,1)S(1)} %get-tuple-element.42), channel_id=1, source_target_pairs={{0,8},{2,10},{4,12},{6,14},{8,0},{10,2},{12,4},{14,6},{16,24},{18,... | collective-permute-start | bytes 98312 | tf_op jit(solution)/shard_map/ppermute | solution.py:558
  31.5 1.6 %picks.1 = (bf16[128,512]{1,0:T(8,128)(2,1)S(1)}, bf16[128,512]{1,0:T(8,128)(2,1)S(1)}, bf16[128,512]{1,0:T(8,128)(2,1)S(1)}, bf16[128,512]{1,0:T(8,128)(2,1)S(1...) custom-call(s32[1,256]{1,0:T(1,128)S(1)} %collective-permute-done.1.refs_0_.refs_4_, ...), custom_call_target="tpu_custom_call" | custom-call | flops 67108864 | bytes 2097152 | tf_op jit(solution)/shard_map/picks/pallas_call | solution.py:74
  33.2 0.8 %collective-permute-done.5.refs_2_ = bf16[32,512]{1,0:T(8,128)(2,1)S(1)} collective-permute-done((bf16[32,512]{1,0:T(8,128)(2,1)S(1)}, bf16[32,512]{1,0:T(8,128)(2,1)S(1)}, u32[]{:S(2)}, u32[]{:S(2)}) %collective-permute-start.5) | collective-permute-done | bytes 32800 | tf_op jit(solution)/shard_map/ppermute | solution.py:558
  34.1 1.9 %collective-permute-start.7 = (bf16[32,512]{1,0:T(8,128)(2,1)S(1)}, bf16[32,512]{1,0:T(8,128)(2,1)S(1)}, u32[]{:S(2)}, u32[]{:S(2)}) collective-permute-start(bf16[32,512]{1,0:T(8,128)(2,1)S(1)} %add.1), channel_id=1, source_target_pairs={{0,24},{2,26},{4,28},{6,30},{8,16},{10,18},{12,20},{14,22},{16,8},... | collective-permute-start | bytes 98312 | tf_op jit(solution)/shard_map/ppermute | solution.py:441
  36.5 2.1 %collective-permute-start.11 = (bf16[32,512]{1,0:T(8,128)(2,1)S(1)}, bf16[32,512]{1,0:T(8,128)(2,1)S(1)}, u32[]{:S(2)}, u32[]{:S(2)}) collective-permute-start(bf16[32,512]{1,0:T(8,128)(2,1)S(1)} %add.1), channel_id=1, source_target_pairs={{0,16},{2,18},{4,20},{6,22},{8,24},{10,26},{12,28},{14,30},{16,0},... | collective-permute-start | bytes 98312 | tf_op jit(solution)/shard_map/ppermute | solution.py:441
  38.5 1.4 %collective-permute-done.7 = bf16[32,512]{1,0:T(8,128)(2,1)S(1)} collective-permute-done((bf16[32,512]{1,0:T(8,128)(2,1)S(1)}, bf16[32,512]{1,0:T(8,128)(2,1)S(1)}, u32[]{:S(2)}, u32[]{:S(2)}) %collective-permute-start.7) | collective-permute-done | bytes 32800 | tf_op jit(solution)/shard_map/ppermute | solution.py:441
  39.9 0.9 %collective-permute-start.9 = (bf16[64,512]{1,0:T(8,128)(2,1)S(1)}, bf16[64,512]{1,0:T(8,128)(2,1)S(1)}, u32[]{:S(2)}, u32[]{:S(2)}) collective-permute-start(bf16[64,512]{1,0:T(8,128)(2,1)S(1)} %pad_maximum_fusion.refs_0_.refs_4_), channel_id=1, source_target_pairs={{0,4},{2,6},{4,0},{6,2},{8,12},{10,14},{12,8},{14,10},{16,20},{18,... | collective-permute-start | bytes 196616 | tf_op jit(solution)/shard_map/ppermute | solution.py:441
  40.8 0.5 collective-permute-done.11
  41.3 1.1 %collective-permute-start.14 = (bf16[64,512]{1,0:T(8,128)(2,1)S(1)}, bf16[64,512]{1,0:T(8,128)(2,1)S(1)}, u32[]{:S(2)}, u32[]{:S(2)}) collective-permute-start(bf16[64,512]{1,0:T(8,128)(2,1)S(1)} %constant_dynamic-update-slice_fusion.refs_4_.refs_8_), channel_id=1, source_target_pairs={{0,4},{2,6},{4,0},{6,2},{8,12},{10,14},{12,8},{14,10},{16,20},{18,... | collective-permute-start | bytes 196616 | tf_op jit(solution)/shard_map/ppermute | solution.py:441
  42.5 0.5 collective-permute-start.13
  43.0 1.2 %collective-permute-done.9.refs_2_.refs_6_ = bf16[64,512]{1,0:T(8,128)(2,1)S(1)} collective-permute-done((bf16[64,512]{1,0:T(8,128)(2,1)S(1)}, bf16[64,512]{1,0:T(8,128)(2,1)S(1)}, u32[]{:S(2)}, u32[]{:S(2)}) %collective-permute-start.9) | collective-permute-done | bytes 65568 | tf_op jit(solution)/shard_map/ppermute | solution.py:441
  44.2 1.4 %collective-permute-done.14.refs_6_.refs_10_ = bf16[64,512]{1,0:T(8,128)(2,1)S(1)} collective-permute-done((bf16[64,512]{1,0:T(8,128)(2,1)S(1)}, bf16[64,512]{1,0:T(8,128)(2,1)S(1)}, u32[]{:S(2)}, u32[]{:S(2)}) %collective-permute-start.14) | collective-permute-done | bytes 65568 | tf_op jit(solution)/shard_map/ppermute | solution.py:441
  45.7 1.2 %collective-permute-done.15.refs_7_.refs_11_ = bf16[64,512]{1,0:T(8,128)(2,1)S(1)} collective-permute-done((bf16[64,512]{1,0:T(8,128)(2,1)S(1)}, bf16[64,512]{1,0:T(8,128)(2,1)S(1)}, u32[]{:S(2)}, u32[]{:S(2)}) %collective-permute-start.15) | collective-permute-done | bytes 65568 | tf_op jit(solution)/shard_map/ppermute | solution.py:441
  46.9 0.6 %asked0.1 = bf16[128,512]{1,0:T(8,128)(2,1)S(1)} custom-call(bf16[128,512]{1,0:T(8,128)(2,1)S(1)} %get-tuple-element.43.refs_4_.refs_0_, bf16[128,512]{1,0:T(8,128)(2,1)S(1)} %get-tuple-element.44.refs_5_.refs_1_, f32[8,512]{1,0:T(8,128)S(1)} %get-tuple-element.33.gain.refs_2_, bf16[512,512]{1,0:T(8,128)(2,1)S(1)} %get-tuple-element.34.w_atom.refs_3_, ...), custom_call_target="tpu_custom_call" | custom-call | tf_op jit(solution)/shard_map/asked0/pallas_call | solution.py:74
  47.5 1.6 %collective-permute-start.17 = (bf16[128,512]{1,0:T(8,128)(2,1)S(1)}, bf16[128,512]{1,0:T(8,128)(2,1)S(1)}, u32[]{:S(2)}, u32[]{:S(2)}) collective-permute-start(bf16[128,512]{1,0:T(8,128)(2,1)S(1)} %asked0.1), channel_id=1, source_target_pairs={{0,1},{1,0},{2,3},{3,2},{4,5},{5,4},{6,7},{7,6},{8,9},{9,8},{10,11... | collective-permute-start | bytes 393224 | tf_op jit(solution)/shard_map/ppermute | solution.py:619
  49.1 0.6 %asked1.1 = bf16[128,512]{1,0:T(8,128)(2,1)S(1)} custom-call(bf16[128,512]{1,0:T(8,128)(2,1)S(1)} %get-tuple-element.45.refs_6_.refs_0_, bf16[128,512]{1,0:T(8,128)(2,1)S(1)} %get-tuple-element.46.refs_7_.refs_1_, f32[8,512]{1,0:T(8,128)S(1)} %get-tuple-element.33.gain.refs_2_, bf16[512,512]{1,0:T(8,128)(2,1)S(1)} %get-tuple-element.34.w_atom.refs_3_, ...), custom_call_target="tpu_custom_call" | custom-call | tf_op jit(solution)/shard_map/asked1/pallas_call | solution.py:74
  49.7 0.6 %collective-permute-start.16 = (bf16[128,512]{1,0:T(8,128)(2,1)S(1)}, bf16[128,512]{1,0:T(8,128)(2,1)S(1)}, u32[]{:S(2)}, u32[]{:S(2)}) collective-permute-start(bf16[128,512]{1,0:T(8,128)(2,1)S(1)} %asked1.1), channel_id=1, source_target_pairs={{0,1},{1,0},{2,3},{3,2},{4,5},{5,4},{6,7},{7,6},{8,9},{9,8},{10,11... | collective-permute-start | bytes 393224 | tf_op jit(solution)/shard_map/ppermute | solution.py:619
  50.3 2.1 %local.1 = (bf16[512,512]{1,0:T(8,128)(2,1)}, f32[256,1024]{1,0:T(8,128)S(1)}) custom-call(f32[8,512]{1,0:T(8,128)S(1)} %get-tuple-element.33.gain.refs_2_, bf16[512,512]{1,0:T(8,128)(2,1)S(1)} %get-tuple-element.34.w_atom.refs_3_, bf16[512,512]{1,0:T(8,128)(2,1)S(1)} %copy-done.2, s32[1,256]{1,0:T(1,128)S(1)} %bitcast.10, s32[1,256]{1,0:T(1,128)S(1)} %bitcast.8, ...), custom_call_target="tpu_custom_call" | custom-call | flops 1073741824 | bytes 4194304 | tf_op jit(solution)/shard_map/local/pallas_call | solution.py:74
  52.4 1.5 %collective-permute-done.17.refs_3_ = bf16[128,512]{1,0:T(8,128)(2,1)S(1)} collective-permute-done((bf16[128,512]{1,0:T(8,128)(2,1)S(1)}, bf16[128,512]{1,0:T(8,128)(2,1)S(1)}, u32[]{:S(2)}, u32[]{:S(2)}) %collective-permute-start.17) | collective-permute-done | bytes 131104 | tf_op jit(solution)/shard_map/ppermute | solution.py:619
  54.0 1.1 %final0.1.refs_4_ = bf16[256,1024]{1,0:T(8,128)(2,1)} custom-call(f32[256,1024]{1,0:T(8,128)S(1)} %get-tuple-element.47.refs_0_, bf16[256,1024]{1,0:T(8,128)(2,1)S(1)} %copy-done.1, bf16[512,1024]{1,0:T(8,128)(2,1)S(1)} %copy-done, bf16[128,512]{1,0:T(8,128)(2,1)S(1)} %collective-permute-done.17.refs_3_), custom_call_target="tpu_custom_call" | custom-call | tf_op jit(solution)/shard_map/final0/pallas_call | solution.py:74
  55.0 0.9 %collective-permute-done.16.refs_3_ = bf16[128,512]{1,0:T(8,128)(2,1)S(1)} collective-permute-done((bf16[128,512]{1,0:T(8,128)(2,1)S(1)}, bf16[128,512]{1,0:T(8,128)(2,1)S(1)}, u32[]{:S(2)}, u32[]{:S(2)}) %collective-permute-start.16) | collective-permute-done | bytes 131104 | tf_op jit(solution)/shard_map/ppermute | solution.py:619
  56.0 1.1 %final1.1 = bf16[256,1024]{1,0:T(8,128)(2,1)} custom-call(f32[256,1024]{1,0:T(8,128)S(1)} %get-tuple-element.47.refs_0_, bf16[256,1024]{1,0:T(8,128)(2,1)S(1)} %copy-done.1, bf16[512,1024]{1,0:T(8,128)(2,1)S(1)} %copy-done, bf16[128,512]{1,0:T(8,128)(2,1)S(1)} %collective-permute-done.16.refs_3_, ...), custom_call_target="tpu_custom_call", output_to_operand_aliasing={{}: (4, {})} | custom-call | tf_op jit(solution)/shard_map/final1/pallas_call | solution.py:74
  (34 shorter events, 1.4 us)
Async XLA Ops:
  0.6 16.8 %copy-start.4 = (s32[256]{0:T(256)S(1)}, s32[256]{0:T(256)}, u32[]{:S(2)}) copy-start(s32[256]{0:T(256)} %param.19) | copy-start | bytes 3076
  3.2 14.3 %all-to-all-start = ((bf16[16,16,128]{2,1,0:T(8,128)(2,1)}), bf16[16,16,128]{2,1,0:T(8,128)(2,1)S(1)}, u32[]{:S(2)}, u32[]{:S(2)}) async-start(bf16[16,16,128]{2,1,0:T(8,128)(2,1)} %get-tuple-element.26), calls=%async_computation | async-start | bytes 131072 | tf_op jit(solution)/shard_map/all_to_all | solution.py:518
  15.2 7.6 %copy-start.6 = (s32[256]{0:T(256)S(1)}, s32[256]{0:T(256)}, u32[]{:S(2)}) copy-start(s32[256]{0:T(256)} %param.18) | copy-start | bytes 3076
  17.5 14.1 %copy-start.2 = (bf16[512,512]{1,0:T(8,128)(2,1)S(1)}, bf16[512,512]{1,0:T(8,128)(2,1)}, u32[]{:S(2)}) copy-start(bf16[512,512]{1,0:T(8,128)(2,1)} %atom_h.1) | copy-start | bytes 1572868
  17.5 14.1 %copy-start.3 = (f32[512]{0:T(512)S(1)}, f32[512]{0:T(512)}, u32[]{:S(2)}) copy-start(f32[512]{0:T(512)} %param.26) | copy-start | bytes 6148
  20.8 29.5 %copy-start = (bf16[512,1024]{1,0:T(8,128)(2,1)S(1)}, bf16[512,1024]{1,0:T(8,128)(2,1)}, u32[]{:S(2)}) copy-start(bf16[512,1024]{1,0:T(8,128)(2,1)} %refs_2_.3) | copy-start | bytes 3145732
  20.8 29.5 %copy-start.5 = (bf16[512,1024]{1,0:T(8,128)(2,1)S(1)}, bf16[512,1024]{1,0:T(8,128)(2,1)}, u32[]{:S(2)}) copy-start(bf16[512,1024]{1,0:T(8,128)(2,1)} %w_tgt.1) | copy-start | bytes 3145732
  20.8 1.9 %collective-permute-start = (bf16[144,256]{1,0:T(8,128)(2,1)S(1)}, bf16[144,256]{1,0:T(8,128)(2,1)S(1)}, u32[]{:S(2)}, u32[]{:S(2)}) collective-permute-start(bf16[144,256]{1,0:T(8,128)(2,1)S(1)} %get-tuple-element.31), channel_id=1, source_target_pairs={{0,2},{2,0},{4,6},{6,4},{8,10},{10,8},{12,14},{14,12},{16,18},{18,... | collective-permute-start | bytes 221192 | tf_op jit(solution)/shard_map/ppermute | solution.py:558
  20.9 5.2 %collective-permute-start.2 = (bf16[144,256]{1,0:T(8,128)(2,1)S(1)}, bf16[144,256]{1,0:T(8,128)(2,1)S(1)}, u32[]{:S(2)}, u32[]{:S(2)}) collective-permute-start(bf16[144,256]{1,0:T(8,128)(2,1)S(1)} %get-tuple-element.37), channel_id=1, source_target_pairs={{0,4},{2,6},{4,0},{6,2},{8,12},{10,14},{12,8},{14,10},{16,20},{18,... | collective-permute-start | bytes 221192 | tf_op jit(solution)/shard_map/ppermute | solution.py:558
  21.1 5.5 %collective-permute-start.3 = (bf16[144,256]{1,0:T(8,128)(2,1)S(1)}, bf16[144,256]{1,0:T(8,128)(2,1)S(1)}, u32[]{:S(2)}, u32[]{:S(2)}) collective-permute-start(bf16[144,256]{1,0:T(8,128)(2,1)S(1)} %get-tuple-element.38), channel_id=1, source_target_pairs={{0,6},{2,4},{4,2},{6,0},{8,14},{10,12},{12,10},{14,8},{16,22},{18,... | collective-permute-start | bytes 221192 | tf_op jit(solution)/shard_map/ppermute | solution.py:558
  22.7 3.9 %collective-permute-start.1 = (s32[1,256]{1,0:T(1,128)S(1)}, s32[1,256]{1,0:T(1,128)S(1)}, u32[]{:S(2)}, u32[]{:S(2)}) collective-permute-start(s32[1,256]{1,0:T(1,128)S(1)} %bitcast.9), channel_id=1, source_target_pairs={{0,1},{1,0},{2,3},{3,2},{4,5},{5,4},{6,7},{7,6},{8,9},{9,8},{10,11... | collective-permute-start | bytes 3080 | tf_op jit(solution)/shard_map/ppermute | solution.py:563
  27.1 6.1 %collective-permute-start.4 = (bf16[32,512]{1,0:T(8,128)(2,1)S(1)}, bf16[32,512]{1,0:T(8,128)(2,1)S(1)}, u32[]{:S(2)}, u32[]{:S(2)}) collective-permute-start(bf16[32,512]{1,0:T(8,128)(2,1)S(1)} %get-tuple-element.40), channel_id=1, source_target_pairs={{0,24},{2,26},{4,28},{6,30},{8,16},{10,18},{12,20},{14,22},{16,8},... | collective-permute-start | bytes 98312 | tf_op jit(solution)/shard_map/ppermute | solution.py:558
  29.0 5.0 %collective-permute-start.5 = (bf16[32,512]{1,0:T(8,128)(2,1)S(1)}, bf16[32,512]{1,0:T(8,128)(2,1)S(1)}, u32[]{:S(2)}, u32[]{:S(2)}) collective-permute-start(bf16[32,512]{1,0:T(8,128)(2,1)S(1)} %get-tuple-element.41), channel_id=1, source_target_pairs={{0,16},{2,18},{4,20},{6,22},{8,24},{10,26},{12,28},{14,30},{16,0},... | collective-permute-start | bytes 98312 | tf_op jit(solution)/shard_map/ppermute | solution.py:558
  29.0 5.1 %collective-permute-start.6 = (bf16[32,512]{1,0:T(8,128)(2,1)S(1)}, bf16[32,512]{1,0:T(8,128)(2,1)S(1)}, u32[]{:S(2)}, u32[]{:S(2)}) collective-permute-start(bf16[32,512]{1,0:T(8,128)(2,1)S(1)} %get-tuple-element.42), channel_id=1, source_target_pairs={{0,8},{2,10},{4,12},{6,14},{8,0},{10,2},{12,4},{14,6},{16,24},{18,... | collective-permute-start | bytes 98312 | tf_op jit(solution)/shard_map/ppermute | solution.py:558
  34.1 5.8 %collective-permute-start.7 = (bf16[32,512]{1,0:T(8,128)(2,1)S(1)}, bf16[32,512]{1,0:T(8,128)(2,1)S(1)}, u32[]{:S(2)}, u32[]{:S(2)}) collective-permute-start(bf16[32,512]{1,0:T(8,128)(2,1)S(1)} %add.1), channel_id=1, source_target_pairs={{0,24},{2,26},{4,28},{6,30},{8,16},{10,18},{12,20},{14,22},{16,8},... | collective-permute-start | bytes 98312 | tf_op jit(solution)/shard_map/ppermute | solution.py:441
  36.0 5.3 %collective-permute-start.12 = (bf16[32,512]{1,0:T(8,128)(2,1)S(1)}, bf16[32,512]{1,0:T(8,128)(2,1)S(1)}, u32[]{:S(2)}, u32[]{:S(2)}) collective-permute-start(bf16[32,512]{1,0:T(8,128)(2,1)S(1)} %add.1), channel_id=1, source_target_pairs={{0,8},{2,10},{4,12},{6,14},{8,0},{10,2},{12,4},{14,6},{16,24},{18,... | collective-permute-start | bytes 98312 | tf_op jit(solution)/shard_map/ppermute | solution.py:441
  36.5 4.8 %collective-permute-start.11 = (bf16[32,512]{1,0:T(8,128)(2,1)S(1)}, bf16[32,512]{1,0:T(8,128)(2,1)S(1)}, u32[]{:S(2)}, u32[]{:S(2)}) collective-permute-start(bf16[32,512]{1,0:T(8,128)(2,1)S(1)} %add.1), channel_id=1, source_target_pairs={{0,16},{2,18},{4,20},{6,22},{8,24},{10,26},{12,28},{14,30},{16,0},... | collective-permute-start | bytes 98312 | tf_op jit(solution)/shard_map/ppermute | solution.py:441
  39.9 4.3 %collective-permute-start.9 = (bf16[64,512]{1,0:T(8,128)(2,1)S(1)}, bf16[64,512]{1,0:T(8,128)(2,1)S(1)}, u32[]{:S(2)}, u32[]{:S(2)}) collective-permute-start(bf16[64,512]{1,0:T(8,128)(2,1)S(1)} %pad_maximum_fusion.refs_0_.refs_4_), channel_id=1, source_target_pairs={{0,4},{2,6},{4,0},{6,2},{8,12},{10,14},{12,8},{14,10},{16,20},{18,... | collective-permute-start | bytes 196616 | tf_op jit(solution)/shard_map/ppermute | solution.py:441
  41.3 4.3 %collective-permute-start.14 = (bf16[64,512]{1,0:T(8,128)(2,1)S(1)}, bf16[64,512]{1,0:T(8,128)(2,1)S(1)}, u32[]{:S(2)}, u32[]{:S(2)}) collective-permute-start(bf16[64,512]{1,0:T(8,128)(2,1)S(1)} %constant_dynamic-update-slice_fusion.refs_4_.refs_8_), channel_id=1, source_target_pairs={{0,4},{2,6},{4,0},{6,2},{8,12},{10,14},{12,8},{14,10},{16,20},{18,... | collective-permute-start | bytes 196616 | tf_op jit(solution)/shard_map/ppermute | solution.py:441
  42.4 3.2 %collective-permute-start.8 = (bf16[64,512]{1,0:T(8,128)(2,1)S(1)}, bf16[64,512]{1,0:T(8,128)(2,1)S(1)}, u32[]{:S(2)}, u32[]{:S(2)}) collective-permute-start(bf16[64,512]{1,0:T(8,128)(2,1)S(1)} %pad_maximum_fusion.refs_0_.refs_4_), channel_id=1, source_target_pairs={{0,2},{2,0},{4,6},{6,4},{8,10},{10,8},{12,14},{14,12},{16,18},{18,... | collective-permute-start | bytes 196616 | tf_op jit(solution)/shard_map/ppermute | solution.py:441
  42.5 3.2 %collective-permute-start.13 = (bf16[64,512]{1,0:T(8,128)(2,1)S(1)}, bf16[64,512]{1,0:T(8,128)(2,1)S(1)}, u32[]{:S(2)}, u32[]{:S(2)}) collective-permute-start(bf16[64,512]{1,0:T(8,128)(2,1)S(1)} %constant_dynamic-update-slice_fusion.refs_4_.refs_8_), channel_id=1, source_target_pairs={{0,2},{2,0},{4,6},{6,4},{8,10},{10,8},{12,14},{14,12},{16,18},{18,... | collective-permute-start | bytes 196616 | tf_op jit(solution)/shard_map/ppermute | solution.py:441
  44.2 1.5 %collective-permute-start.10 = (bf16[64,512]{1,0:T(8,128)(2,1)S(1)}, bf16[64,512]{1,0:T(8,128)(2,1)S(1)}, u32[]{:S(2)}, u32[]{:S(2)}) collective-permute-start(bf16[64,512]{1,0:T(8,128)(2,1)S(1)} %collective-permute-done.9.refs_2_.refs_6_), channel_id=1, source_target_pairs={{0,2},{2,0},{4,6},{6,4},{8,10},{10,8},{12,14},{14,12},{16,18},{18,... | collective-permute-start | bytes 196616 | tf_op jit(solution)/shard_map/ppermute | solution.py:441
  45.6 1.3 %collective-permute-start.15 = (bf16[64,512]{1,0:T(8,128)(2,1)S(1)}, bf16[64,512]{1,0:T(8,128)(2,1)S(1)}, u32[]{:S(2)}, u32[]{:S(2)}) collective-permute-start(bf16[64,512]{1,0:T(8,128)(2,1)S(1)} %collective-permute-done.14.refs_6_.refs_10_), channel_id=1, source_target_pairs={{0,2},{2,0},{4,6},{6,4},{8,10},{10,8},{12,14},{14,12},{16,18},{18,... | collective-permute-start | bytes 196616 | tf_op jit(solution)/shard_map/ppermute | solution.py:441
  46.9 7.1 %copy-start.1 = (bf16[256,1024]{1,0:T(8,128)(2,1)S(1)}, bf16[256,1024]{1,0:T(8,128)(2,1)}, u32[]{:S(2)}) copy-start(bf16[256,1024]{1,0:T(8,128)(2,1)} %get-tuple-element.48.refs_1_) | copy-start | bytes 1572868
  47.5 6.4 %collective-permute-start.17 = (bf16[128,512]{1,0:T(8,128)(2,1)S(1)}, bf16[128,512]{1,0:T(8,128)(2,1)S(1)}, u32[]{:S(2)}, u32[]{:S(2)}) collective-permute-start(bf16[128,512]{1,0:T(8,128)(2,1)S(1)} %asked0.1), channel_id=1, source_target_pairs={{0,1},{1,0},{2,3},{3,2},{4,5},{5,4},{6,7},{7,6},{8,9},{9,8},{10,11... | collective-permute-start | bytes 393224 | tf_op jit(solution)/shard_map/ppermute | solution.py:619
  49.7 6.2 %collective-permute-start.16 = (bf16[128,512]{1,0:T(8,128)(2,1)S(1)}, bf16[128,512]{1,0:T(8,128)(2,1)S(1)}, u32[]{:S(2)}, u32[]{:S(2)}) collective-permute-start(bf16[128,512]{1,0:T(8,128)(2,1)S(1)} %asked1.1), channel_id=1, source_target_pairs={{0,1},{1,0},{2,3},{3,2},{4,5},{5,4},{6,7},{7,6},{8,9},{9,8},{10,11... | collective-permute-start | bytes 393224 | tf_op jit(solution)/shard_map/ppermute | solution.py:619

commit v6 on v5

--- a/solution.py
+++ b/solution.py
@@ -511,7 +511,7 @@
             pltpu.VMEM((edges, de), BF16),
             pltpu.VMEM((width, de), BF16),
             pltpu.VMEM((1, slots), jnp.int32),
-            dma((6,)),
+            dma((5,)),
         ],
         name="outgoing",
     )(edge_msg, w_down.T, send_rows, basis, trip_slot.T)

time: 57.3 us -> 57.2 us (level)
  no operation moved by 1% of the time
where the time goes in v6:
time: 57.2 us; the launch traced here: 56.9 us
  starting transfers between devices  24.4 us (43%)
  Pallas kernels  17.9 us (31%)
  waiting for transfers between devices  13.8 us (24%)
  between operations  0.8 us (1%)
    pallas_call x11, Pallas kernels, apply(): return run(*held)  17.9 us
    all_to_all x1, starting transfers between devices, per_device(): lax.all_to_all(outgoing, 'wide', split_axis=0, concat_axis=0, tiled=True)  7.4 us
    ppermute x9, starting transfers between devices, gathered(): lax.ppermute(value, 'wide', pairs)  6.98 us
    ppermute x6, starting transfers between devices, mirrored(): return lax.ppermute(value, 'wide', [(i, i ^ flip) for i in range(wide)])  6.37 us
    ppermute x9, waiting for transfers between devices, gathered(): lax.ppermute(value, 'wide', pairs)  5.8 us
    ppermute x6, waiting for transfers between devices, mirrored(): return lax.ppermute(value, 'wide', [(i, i ^ flip) for i in range(wide)])  3.23 us
    ppermute x2, waiting for transfers between devices, per_device(): lax.ppermute(a, 'narrow', [(i, (i - k) % narrow) for i in range(narrow)])  2.44 us
    all_to_all x1, waiting for transfers between devices, per_device(): lax.all_to_all(outgoing, 'wide', split_axis=0, concat_axis=0, tiled=True)  2.3 us
  transfers between devices with their start and end apart: 19, of which 11 were waited for; matrix products, arithmetic and copies ran while one was open for 0% of the time, Pallas kernels for 18%

profile of v6, /device:TPU:0, one launch (start us, length us, event | category | flops | bytes accessed | tf_op | source)
XLA Modules:
  0.0 56.9 jit_solution(18238841487208458953)
XLA Ops:
  0.6 2.4 %outgoing.1 = (bf16[16,16,128]{2,1,0:T(8,128)(2,1)}, bf16[256,512]{1,0:T(8,128)(2,1)S(1)}, s32[32,256]{1,0:T(8,128)S(1)}) custom-call(bf16[256,1024]{1,0:T(8,128)(2,1)} %edge_hbm.3, bf16[64,1024]{1,0:T(8,128)(2,1)} %bitcast.12, s32[1,512]{1,0:T(1,128)} %rows_hbm.1, bf16[256,512]{1,0:T(8,128)(2,1)} %basis_hbm.1, s32[32,256]{1,0:T(8,128)} %bitcast.13), custom_call_target="tpu_custom_call" | custom-call | tf_op jit(solution)/shard_map/outgoing/pallas_call | solution.py:74
  3.1 7.4 %all-to-all-start = ((bf16[16,16,128]{2,1,0:T(8,128)(2,1)}), bf16[16,16,128]{2,1,0:T(8,128)(2,1)S(1)}, u32[]{:S(2)}, u32[]{:S(2)}) async-start(bf16[16,16,128]{2,1,0:T(8,128)(2,1)} %get-tuple-element.26), calls=%async_computation | async-start | bytes 131072 | tf_op jit(solution)/shard_map/all_to_all | solution.py:518
  10.5 4.6 %mixer.1 = (bf16[12,256,512]{2,1,0:T(8,128)(2,1)S(1)}, bf16[4,256,512]{2,1,0:T(8,128)(2,1)}) custom-call(bf16[256,512]{1,0:T(8,128)(2,1)S(1)} %get-tuple-element.27.basis, s32[32,256]{1,0:T(8,128)S(1)} %get-tuple-element.28.slots_t), custom_call_target="tpu_custom_call" | custom-call | flops 1073741824 | bytes 6291456 | tf_op jit(solution)/shard_map/mixer/pallas_call | solution.py:74
  15.1 2.3 %all-to-all-done.received = bf16[16,16,128]{2,1,0:T(8,128)(2,1)S(1)} async-done(((bf16[16,16,128]{2,1,0:T(8,128)(2,1)}), bf16[16,16,128]{2,1,0:T(8,128)(2,1)S(1)}, u32[]{:S(2)}, u32[]{:S(2)}) %all-to-all-start) | async-done | bytes 65568 | tf_op jit(solution)/shard_map/all_to_all | solution.py:518
  17.4 3.3 %edge.1 = (bf16[256,1024]{1,0:T(8,128)(2,1)}, bf16[144,256]{1,0:T(8,128)(2,1)S(1)}, bf16[144,256]{1,0:T(8,128)(2,1)S(1)}, bf16[144,256]{1,0:T(8,128)(2,1)S(1)}, bf16[144,256]{1,0:T(8,128)(2,1)S(1)}) custom-call(bf16[16,16,128]{2,1,0:T(8,128)(2,1)S(1)} %all-to-all-done.received, s32[1,256]{1,0:T(1,128)S(1)} %bitcast.7, ...), custom_call_target="tpu_custom_call" | custom-call | tf_op jit(solution)/shard_map/edge/pallas_call | solution.py:74
  21.0 1.6 %collective-permute-start.3 = (bf16[144,256]{1,0:T(8,128)(2,1)S(1)}, bf16[144,256]{1,0:T(8,128)(2,1)S(1)}, u32[]{:S(2)}, u32[]{:S(2)}) collective-permute-start(bf16[144,256]{1,0:T(8,128)(2,1)S(1)} %get-tuple-element.38), channel_id=1, source_target_pairs={{0,6},{2,4},{4,2},{6,0},{8,14},{10,12},{12,10},{14,8},{16,22},{18,... | collective-permute-start | bytes 221192 | tf_op jit(solution)/shard_map/ppermute | solution.py:558
  22.6 1.5 %collective-permute-start.1 = (s32[1,256]{1,0:T(1,128)S(1)}, s32[1,256]{1,0:T(1,128)S(1)}, u32[]{:S(2)}, u32[]{:S(2)}) collective-permute-start(s32[1,256]{1,0:T(1,128)S(1)} %bitcast.9), channel_id=1, source_target_pairs={{0,1},{1,0},{2,3},{3,2},{4,5},{5,4},{6,7},{7,6},{8,9},{9,8},{10,11... | collective-permute-start | bytes 3080 | tf_op jit(solution)/shard_map/ppermute | solution.py:563
  24.2 1.8 %collective-permute-done.2.refs_2_ = bf16[144,256]{1,0:T(8,128)(2,1)S(1)} collective-permute-done((bf16[144,256]{1,0:T(8,128)(2,1)S(1)}, bf16[144,256]{1,0:T(8,128)(2,1)S(1)}, u32[]{:S(2)}, u32[]{:S(2)}) %collective-permute-start.2) | collective-permute-done | bytes 73760 | tf_op jit(solution)/shard_map/ppermute | solution.py:558
  26.0 0.5 collective-permute-done.3.refs_3_
  27.0 1.9 %collective-permute-start.4 = (bf16[32,512]{1,0:T(8,128)(2,1)S(1)}, bf16[32,512]{1,0:T(8,128)(2,1)S(1)}, u32[]{:S(2)}, u32[]{:S(2)}) collective-permute-start(bf16[32,512]{1,0:T(8,128)(2,1)S(1)} %get-tuple-element.40), channel_id=1, source_target_pairs={{0,24},{2,26},{4,28},{6,30},{8,16},{10,18},{12,20},{14,22},{16,8},... | collective-permute-start | bytes 98312 | tf_op jit(solution)/shard_map/ppermute | solution.py:558
  28.9 2.5 %collective-permute-start.6 = (bf16[32,512]{1,0:T(8,128)(2,1)S(1)}, bf16[32,512]{1,0:T(8,128)(2,1)S(1)}, u32[]{:S(2)}, u32[]{:S(2)}) collective-permute-start(bf16[32,512]{1,0:T(8,128)(2,1)S(1)} %get-tuple-element.42), channel_id=1, source_target_pairs={{0,8},{2,10},{4,12},{6,14},{8,0},{10,2},{12,4},{14,6},{16,24},{18,... | collective-permute-start | bytes 98312 | tf_op jit(solution)/shard_map/ppermute | solution.py:558
  31.5 1.6 %picks.1 = (bf16[128,512]{1,0:T(8,128)(2,1)S(1)}, bf16[128,512]{1,0:T(8,128)(2,1)S(1)}, bf16[128,512]{1,0:T(8,128)(2,1)S(1)}, bf16[128,512]{1,0:T(8,128)(2,1)S(1...) custom-call(s32[1,256]{1,0:T(1,128)S(1)} %collective-permute-done.1.refs_0_.refs_4_, ...), custom_call_target="tpu_custom_call" | custom-call | flops 67108864 | bytes 2097152 | tf_op jit(solution)/shard_map/picks/pallas_call | solution.py:74
  33.1 0.8 %collective-permute-done.5.refs_2_ = bf16[32,512]{1,0:T(8,128)(2,1)S(1)} collective-permute-done((bf16[32,512]{1,0:T(8,128)(2,1)S(1)}, bf16[32,512]{1,0:T(8,128)(2,1)S(1)}, u32[]{:S(2)}, u32[]{:S(2)}) %collective-permute-start.5) | collective-permute-done | bytes 32800 | tf_op jit(solution)/shard_map/ppermute | solution.py:558
  34.0 1.9 %collective-permute-start.7 = (bf16[32,512]{1,0:T(8,128)(2,1)S(1)}, bf16[32,512]{1,0:T(8,128)(2,1)S(1)}, u32[]{:S(2)}, u32[]{:S(2)}) collective-permute-start(bf16[32,512]{1,0:T(8,128)(2,1)S(1)} %add.1), channel_id=1, source_target_pairs={{0,24},{2,26},{4,28},{6,30},{8,16},{10,18},{12,20},{14,22},{16,8},... | collective-permute-start | bytes 98312 | tf_op jit(solution)/shard_map/ppermute | solution.py:441
  36.4 2.1 %collective-permute-start.11 = (bf16[32,512]{1,0:T(8,128)(2,1)S(1)}, bf16[32,512]{1,0:T(8,128)(2,1)S(1)}, u32[]{:S(2)}, u32[]{:S(2)}) collective-permute-start(bf16[32,512]{1,0:T(8,128)(2,1)S(1)} %add.1), channel_id=1, source_target_pairs={{0,16},{2,18},{4,20},{6,22},{8,24},{10,26},{12,28},{14,30},{16,0},... | collective-permute-start | bytes 98312 | tf_op jit(solution)/shard_map/ppermute | solution.py:441
  38.5 1.4 %collective-permute-done.7 = bf16[32,512]{1,0:T(8,128)(2,1)S(1)} collective-permute-done((bf16[32,512]{1,0:T(8,128)(2,1)S(1)}, bf16[32,512]{1,0:T(8,128)(2,1)S(1)}, u32[]{:S(2)}, u32[]{:S(2)}) %collective-permute-start.7) | collective-permute-done | bytes 32800 | tf_op jit(solution)/shard_map/ppermute | solution.py:441
  39.8 0.9 %collective-permute-start.9 = (bf16[64,512]{1,0:T(8,128)(2,1)S(1)}, bf16[64,512]{1,0:T(8,128)(2,1)S(1)}, u32[]{:S(2)}, u32[]{:S(2)}) collective-permute-start(bf16[64,512]{1,0:T(8,128)(2,1)S(1)} %pad_maximum_fusion.refs_0_.refs_4_), channel_id=1, source_target_pairs={{0,4},{2,6},{4,0},{6,2},{8,12},{10,14},{12,8},{14,10},{16,20},{18,... | collective-permute-start | bytes 196616 | tf_op jit(solution)/shard_map/ppermute | solution.py:441
  40.7 0.5 collective-permute-done.11
  41.2 1.1 %collective-permute-start.14 = (bf16[64,512]{1,0:T(8,128)(2,1)S(1)}, bf16[64,512]{1,0:T(8,128)(2,1)S(1)}, u32[]{:S(2)}, u32[]{:S(2)}) collective-permute-start(bf16[64,512]{1,0:T(8,128)(2,1)S(1)} %constant_dynamic-update-slice_fusion.refs_4_.refs_8_), channel_id=1, source_target_pairs={{0,4},{2,6},{4,0},{6,2},{8,12},{10,14},{12,8},{14,10},{16,20},{18,... | collective-permute-start | bytes 196616 | tf_op jit(solution)/shard_map/ppermute | solution.py:441
  42.4 0.5 collective-permute-start.13
  42.9 1.2 %collective-permute-done.9.refs_2_.refs_6_ = bf16[64,512]{1,0:T(8,128)(2,1)S(1)} collective-permute-done((bf16[64,512]{1,0:T(8,128)(2,1)S(1)}, bf16[64,512]{1,0:T(8,128)(2,1)S(1)}, u32[]{:S(2)}, u32[]{:S(2)}) %collective-permute-start.9) | collective-permute-done | bytes 65568 | tf_op jit(solution)/shard_map/ppermute | solution.py:441
  44.1 1.4 %collective-permute-done.14.refs_6_.refs_10_ = bf16[64,512]{1,0:T(8,128)(2,1)S(1)} collective-permute-done((bf16[64,512]{1,0:T(8,128)(2,1)S(1)}, bf16[64,512]{1,0:T(8,128)(2,1)S(1)}, u32[]{:S(2)}, u32[]{:S(2)}) %collective-permute-start.14) | collective-permute-done | bytes 65568 | tf_op jit(solution)/shard_map/ppermute | solution.py:441
  45.6 1.2 %collective-permute-done.15.refs_7_.refs_11_ = bf16[64,512]{1,0:T(8,128)(2,1)S(1)} collective-permute-done((bf16[64,512]{1,0:T(8,128)(2,1)S(1)}, bf16[64,512]{1,0:T(8,128)(2,1)S(1)}, u32[]{:S(2)}, u32[]{:S(2)}) %collective-permute-start.15) | collective-permute-done | bytes 65568 | tf_op jit(solution)/shard_map/ppermute | solution.py:441
  46.8 0.6 %asked0.1 = bf16[128,512]{1,0:T(8,128)(2,1)S(1)} custom-call(bf16[128,512]{1,0:T(8,128)(2,1)S(1)} %get-tuple-element.43.refs_4_.refs_0_, bf16[128,512]{1,0:T(8,128)(2,1)S(1)} %get-tuple-element.44.refs_5_.refs_1_, f32[8,512]{1,0:T(8,128)S(1)} %get-tuple-element.33.gain.refs_2_, bf16[512,512]{1,0:T(8,128)(2,1)S(1)} %get-tuple-element.34.w_atom.refs_3_, ...), custom_call_target="tpu_custom_call" | custom-call | tf_op jit(solution)/shard_map/asked0/pallas_call | solution.py:74
  47.4 1.6 %collective-permute-start.17 = (bf16[128,512]{1,0:T(8,128)(2,1)S(1)}, bf16[128,512]{1,0:T(8,128)(2,1)S(1)}, u32[]{:S(2)}, u32[]{:S(2)}) collective-permute-start(bf16[128,512]{1,0:T(8,128)(2,1)S(1)} %asked0.1), channel_id=1, source_target_pairs={{0,1},{1,0},{2,3},{3,2},{4,5},{5,4},{6,7},{7,6},{8,9},{9,8},{10,11... | collective-permute-start | bytes 393224 | tf_op jit(solution)/shard_map/ppermute | solution.py:619
  49.0 0.6 %asked1.1 = bf16[128,512]{1,0:T(8,128)(2,1)S(1)} custom-call(bf16[128,512]{1,0:T(8,128)(2,1)S(1)} %get-tuple-element.45.refs_6_.refs_0_, bf16[128,512]{1,0:T(8,128)(2,1)S(1)} %get-tuple-element.46.refs_7_.refs_1_, f32[8,512]{1,0:T(8,128)S(1)} %get-tuple-element.33.gain.refs_2_, bf16[512,512]{1,0:T(8,128)(2,1)S(1)} %get-tuple-element.34.w_atom.refs_3_, ...), custom_call_target="tpu_custom_call" | custom-call | tf_op jit(solution)/shard_map/asked1/pallas_call | solution.py:74
  49.6 0.6 %collective-permute-start.16 = (bf16[128,512]{1,0:T(8,128)(2,1)S(1)}, bf16[128,512]{1,0:T(8,128)(2,1)S(1)}, u32[]{:S(2)}, u32[]{:S(2)}) collective-permute-start(bf16[128,512]{1,0:T(8,128)(2,1)S(1)} %asked1.1), channel_id=1, source_target_pairs={{0,1},{1,0},{2,3},{3,2},{4,5},{5,4},{6,7},{7,6},{8,9},{9,8},{10,11... | collective-permute-start | bytes 393224 | tf_op jit(solution)/shard_map/ppermute | solution.py:619
  50.2 2.1 %local.1 = (bf16[512,512]{1,0:T(8,128)(2,1)}, f32[256,1024]{1,0:T(8,128)S(1)}) custom-call(f32[8,512]{1,0:T(8,128)S(1)} %get-tuple-element.33.gain.refs_2_, bf16[512,512]{1,0:T(8,128)(2,1)S(1)} %get-tuple-element.34.w_atom.refs_3_, bf16[512,512]{1,0:T(8,128)(2,1)S(1)} %copy-done.2, s32[1,256]{1,0:T(1,128)S(1)} %bitcast.10, s32[1,256]{1,0:T(1,128)S(1)} %bitcast.8, ...), custom_call_target="tpu_custom_call" | custom-call | flops 1073741824 | bytes 4194304 | tf_op jit(solution)/shard_map/local/pallas_call | solution.py:74
  52.4 1.5 %collective-permute-done.17.refs_3_ = bf16[128,512]{1,0:T(8,128)(2,1)S(1)} collective-permute-done((bf16[128,512]{1,0:T(8,128)(2,1)S(1)}, bf16[128,512]{1,0:T(8,128)(2,1)S(1)}, u32[]{:S(2)}, u32[]{:S(2)}) %collective-permute-start.17) | collective-permute-done | bytes 131104 | tf_op jit(solution)/shard_map/ppermute | solution.py:619
  53.9 1.1 %final0.1.refs_4_ = bf16[256,1024]{1,0:T(8,128)(2,1)} custom-call(f32[256,1024]{1,0:T(8,128)S(1)} %get-tuple-element.47.refs_0_, bf16[256,1024]{1,0:T(8,128)(2,1)S(1)} %copy-done.1, bf16[512,1024]{1,0:T(8,128)(2,1)S(1)} %copy-done, bf16[128,512]{1,0:T(8,128)(2,1)S(1)} %collective-permute-done.17.refs_3_), custom_call_target="tpu_custom_call" | custom-call | tf_op jit(solution)/shard_map/final0/pallas_call | solution.py:74
  54.9 0.9 %collective-permute-done.16.refs_3_ = bf16[128,512]{1,0:T(8,128)(2,1)S(1)} collective-permute-done((bf16[128,512]{1,0:T(8,128)(2,1)S(1)}, bf16[128,512]{1,0:T(8,128)(2,1)S(1)}, u32[]{:S(2)}, u32[]{:S(2)}) %collective-permute-start.16) | collective-permute-done | bytes 131104 | tf_op jit(solution)/shard_map/ppermute | solution.py:619
  55.9 1.1 %final1.1 = bf16[256,1024]{1,0:T(8,128)(2,1)} custom-call(f32[256,1024]{1,0:T(8,128)S(1)} %get-tuple-element.47.refs_0_, bf16[256,1024]{1,0:T(8,128)(2,1)S(1)} %copy-done.1, bf16[512,1024]{1,0:T(8,128)(2,1)S(1)} %copy-done, bf16[128,512]{1,0:T(8,128)(2,1)S(1)} %collective-permute-done.16.refs_3_, ...), custom_call_target="tpu_custom_call", output_to_operand_aliasing={{}: (4, {})} | custom-call | tf_op jit(solution)/shard_map/final1/pallas_call | solution.py:74
  (34 shorter events, 1.4 us)
Async XLA Ops:
  0.6 16.7 %copy-start.4 = (s32[256]{0:T(256)S(1)}, s32[256]{0:T(256)}, u32[]{:S(2)}) copy-start(s32[256]{0:T(256)} %param.19) | copy-start | bytes 3076
  3.1 14.3 %all-to-all-start = ((bf16[16,16,128]{2,1,0:T(8,128)(2,1)}), bf16[16,16,128]{2,1,0:T(8,128)(2,1)S(1)}, u32[]{:S(2)}, u32[]{:S(2)}) async-start(bf16[16,16,128]{2,1,0:T(8,128)(2,1)} %get-tuple-element.26), calls=%async_computation | async-start | bytes 131072 | tf_op jit(solution)/shard_map/all_to_all | solution.py:518
  15.1 7.6 %copy-start.6 = (s32[256]{0:T(256)S(1)}, s32[256]{0:T(256)}, u32[]{:S(2)}) copy-start(s32[256]{0:T(256)} %param.18) | copy-start | bytes 3076
  17.4 14.1 %copy-start.2 = (bf16[512,512]{1,0:T(8,128)(2,1)S(1)}, bf16[512,512]{1,0:T(8,128)(2,1)}, u32[]{:S(2)}) copy-start(bf16[512,512]{1,0:T(8,128)(2,1)} %atom_h.1) | copy-start | bytes 1572868
  17.4 14.1 %copy-start.3 = (f32[512]{0:T(512)S(1)}, f32[512]{0:T(512)}, u32[]{:S(2)}) copy-start(f32[512]{0:T(512)} %param.26) | copy-start | bytes 6148
  20.7 29.5 %copy-start = (bf16[512,1024]{1,0:T(8,128)(2,1)S(1)}, bf16[512,1024]{1,0:T(8,128)(2,1)}, u32[]{:S(2)}) copy-start(bf16[512,1024]{1,0:T(8,128)(2,1)} %refs_2_.3) | copy-start | bytes 3145732
  20.7 29.5 %copy-start.5 = (bf16[512,1024]{1,0:T(8,128)(2,1)S(1)}, bf16[512,1024]{1,0:T(8,128)(2,1)}, u32[]{:S(2)}) copy-start(bf16[512,1024]{1,0:T(8,128)(2,1)} %w_tgt.1) | copy-start | bytes 3145732
  20.7 1.9 %collective-permute-start = (bf16[144,256]{1,0:T(8,128)(2,1)S(1)}, bf16[144,256]{1,0:T(8,128)(2,1)S(1)}, u32[]{:S(2)}, u32[]{:S(2)}) collective-permute-start(bf16[144,256]{1,0:T(8,128)(2,1)S(1)} %get-tuple-element.31), channel_id=1, source_target_pairs={{0,2},{2,0},{4,6},{6,4},{8,10},{10,8},{12,14},{14,12},{16,18},{18,... | collective-permute-start | bytes 221192 | tf_op jit(solution)/shard_map/ppermute | solution.py:558
  20.8 5.2 %collective-permute-start.2 = (bf16[144,256]{1,0:T(8,128)(2,1)S(1)}, bf16[144,256]{1,0:T(8,128)(2,1)S(1)}, u32[]{:S(2)}, u32[]{:S(2)}) collective-permute-start(bf16[144,256]{1,0:T(8,128)(2,1)S(1)} %get-tuple-element.37), channel_id=1, source_target_pairs={{0,4},{2,6},{4,0},{6,2},{8,12},{10,14},{12,8},{14,10},{16,20},{18,... | collective-permute-start | bytes 221192 | tf_op jit(solution)/shard_map/ppermute | solution.py:558
  21.0 5.5 %collective-permute-start.3 = (bf16[144,256]{1,0:T(8,128)(2,1)S(1)}, bf16[144,256]{1,0:T(8,128)(2,1)S(1)}, u32[]{:S(2)}, u32[]{:S(2)}) collective-permute-start(bf16[144,256]{1,0:T(8,128)(2,1)S(1)} %get-tuple-element.38), channel_id=1, source_target_pairs={{0,6},{2,4},{4,2},{6,0},{8,14},{10,12},{12,10},{14,8},{16,22},{18,... | collective-permute-start | bytes 221192 | tf_op jit(solution)/shard_map/ppermute | solution.py:558
  22.6 3.9 %collective-permute-start.1 = (s32[1,256]{1,0:T(1,128)S(1)}, s32[1,256]{1,0:T(1,128)S(1)}, u32[]{:S(2)}, u32[]{:S(2)}) collective-permute-start(s32[1,256]{1,0:T(1,128)S(1)} %bitcast.9), channel_id=1, source_target_pairs={{0,1},{1,0},{2,3},{3,2},{4,5},{5,4},{6,7},{7,6},{8,9},{9,8},{10,11... | collective-permute-start | bytes 3080 | tf_op jit(solution)/shard_map/ppermute | solution.py:563
  27.0 6.1 %collective-permute-start.4 = (bf16[32,512]{1,0:T(8,128)(2,1)S(1)}, bf16[32,512]{1,0:T(8,128)(2,1)S(1)}, u32[]{:S(2)}, u32[]{:S(2)}) collective-permute-start(bf16[32,512]{1,0:T(8,128)(2,1)S(1)} %get-tuple-element.40), channel_id=1, source_target_pairs={{0,24},{2,26},{4,28},{6,30},{8,16},{10,18},{12,20},{14,22},{16,8},... | collective-permute-start | bytes 98312 | tf_op jit(solution)/shard_map/ppermute | solution.py:558
  28.9 5.0 %collective-permute-start.5 = (bf16[32,512]{1,0:T(8,128)(2,1)S(1)}, bf16[32,512]{1,0:T(8,128)(2,1)S(1)}, u32[]{:S(2)}, u32[]{:S(2)}) collective-permute-start(bf16[32,512]{1,0:T(8,128)(2,1)S(1)} %get-tuple-element.41), channel_id=1, source_target_pairs={{0,16},{2,18},{4,20},{6,22},{8,24},{10,26},{12,28},{14,30},{16,0},... | collective-permute-start | bytes 98312 | tf_op jit(solution)/shard_map/ppermute | solution.py:558
  28.9 5.1 %collective-permute-start.6 = (bf16[32,512]{1,0:T(8,128)(2,1)S(1)}, bf16[32,512]{1,0:T(8,128)(2,1)S(1)}, u32[]{:S(2)}, u32[]{:S(2)}) collective-permute-start(bf16[32,512]{1,0:T(8,128)(2,1)S(1)} %get-tuple-element.42), channel_id=1, source_target_pairs={{0,8},{2,10},{4,12},{6,14},{8,0},{10,2},{12,4},{14,6},{16,24},{18,... | collective-permute-start | bytes 98312 | tf_op jit(solution)/shard_map/ppermute | solution.py:558
  34.0 5.8 %collective-permute-start.7 = (bf16[32,512]{1,0:T(8,128)(2,1)S(1)}, bf16[32,512]{1,0:T(8,128)(2,1)S(1)}, u32[]{:S(2)}, u32[]{:S(2)}) collective-permute-start(bf16[32,512]{1,0:T(8,128)(2,1)S(1)} %add.1), channel_id=1, source_target_pairs={{0,24},{2,26},{4,28},{6,30},{8,16},{10,18},{12,20},{14,22},{16,8},... | collective-permute-start | bytes 98312 | tf_op jit(solution)/shard_map/ppermute | solution.py:441
  35.9 5.3 %collective-permute-start.12 = (bf16[32,512]{1,0:T(8,128)(2,1)S(1)}, bf16[32,512]{1,0:T(8,128)(2,1)S(1)}, u32[]{:S(2)}, u32[]{:S(2)}) collective-permute-start(bf16[32,512]{1,0:T(8,128)(2,1)S(1)} %add.1), channel_id=1, source_target_pairs={{0,8},{2,10},{4,12},{6,14},{8,0},{10,2},{12,4},{14,6},{16,24},{18,... | collective-permute-start | bytes 98312 | tf_op jit(solution)/shard_map/ppermute | solution.py:441
  36.4 4.8 %collective-permute-start.11 = (bf16[32,512]{1,0:T(8,128)(2,1)S(1)}, bf16[32,512]{1,0:T(8,128)(2,1)S(1)}, u32[]{:S(2)}, u32[]{:S(2)}) collective-permute-start(bf16[32,512]{1,0:T(8,128)(2,1)S(1)} %add.1), channel_id=1, source_target_pairs={{0,16},{2,18},{4,20},{6,22},{8,24},{10,26},{12,28},{14,30},{16,0},... | collective-permute-start | bytes 98312 | tf_op jit(solution)/shard_map/ppermute | solution.py:441
  39.8 4.3 %collective-permute-start.9 = (bf16[64,512]{1,0:T(8,128)(2,1)S(1)}, bf16[64,512]{1,0:T(8,128)(2,1)S(1)}, u32[]{:S(2)}, u32[]{:S(2)}) collective-permute-start(bf16[64,512]{1,0:T(8,128)(2,1)S(1)} %pad_maximum_fusion.refs_0_.refs_4_), channel_id=1, source_target_pairs={{0,4},{2,6},{4,0},{6,2},{8,12},{10,14},{12,8},{14,10},{16,20},{18,... | collective-permute-start | bytes 196616 | tf_op jit(solution)/shard_map/ppermute | solution.py:441
  41.2 4.3 %collective-permute-start.14 = (bf16[64,512]{1,0:T(8,128)(2,1)S(1)}, bf16[64,512]{1,0:T(8,128)(2,1)S(1)}, u32[]{:S(2)}, u32[]{:S(2)}) collective-permute-start(bf16[64,512]{1,0:T(8,128)(2,1)S(1)} %constant_dynamic-update-slice_fusion.refs_4_.refs_8_), channel_id=1, source_target_pairs={{0,4},{2,6},{4,0},{6,2},{8,12},{10,14},{12,8},{14,10},{16,20},{18,... | collective-permute-start | bytes 196616 | tf_op jit(solution)/shard_map/ppermute | solution.py:441
  42.4 3.2 %collective-permute-start.8 = (bf16[64,512]{1,0:T(8,128)(2,1)S(1)}, bf16[64,512]{1,0:T(8,128)(2,1)S(1)}, u32[]{:S(2)}, u32[]{:S(2)}) collective-permute-start(bf16[64,512]{1,0:T(8,128)(2,1)S(1)} %pad_maximum_fusion.refs_0_.refs_4_), channel_id=1, source_target_pairs={{0,2},{2,0},{4,6},{6,4},{8,10},{10,8},{12,14},{14,12},{16,18},{18,... | collective-permute-start | bytes 196616 | tf_op jit(solution)/shard_map/ppermute | solution.py:441
  42.4 3.2 %collective-permute-start.13 = (bf16[64,512]{1,0:T(8,128)(2,1)S(1)}, bf16[64,512]{1,0:T(8,128)(2,1)S(1)}, u32[]{:S(2)}, u32[]{:S(2)}) collective-permute-start(bf16[64,512]{1,0:T(8,128)(2,1)S(1)} %constant_dynamic-update-slice_fusion.refs_4_.refs_8_), channel_id=1, source_target_pairs={{0,2},{2,0},{4,6},{6,4},{8,10},{10,8},{12,14},{14,12},{16,18},{18,... | collective-permute-start | bytes 196616 | tf_op jit(solution)/shard_map/ppermute | solution.py:441
  44.1 1.5 %collective-permute-start.10 = (bf16[64,512]{1,0:T(8,128)(2,1)S(1)}, bf16[64,512]{1,0:T(8,128)(2,1)S(1)}, u32[]{:S(2)}, u32[]{:S(2)}) collective-permute-start(bf16[64,512]{1,0:T(8,128)(2,1)S(1)} %collective-permute-done.9.refs_2_.refs_6_), channel_id=1, source_target_pairs={{0,2},{2,0},{4,6},{6,4},{8,10},{10,8},{12,14},{14,12},{16,18},{18,... | collective-permute-start | bytes 196616 | tf_op jit(solution)/shard_map/ppermute | solution.py:441
  45.6 1.3 %collective-permute-start.15 = (bf16[64,512]{1,0:T(8,128)(2,1)S(1)}, bf16[64,512]{1,0:T(8,128)(2,1)S(1)}, u32[]{:S(2)}, u32[]{:S(2)}) collective-permute-start(bf16[64,512]{1,0:T(8,128)(2,1)S(1)} %collective-permute-done.14.refs_6_.refs_10_), channel_id=1, source_target_pairs={{0,2},{2,0},{4,6},{6,4},{8,10},{10,8},{12,14},{14,12},{16,18},{18,... | collective-permute-start | bytes 196616 | tf_op jit(solution)/shard_map/ppermute | solution.py:441
  46.8 7.1 %copy-start.1 = (bf16[256,1024]{1,0:T(8,128)(2,1)S(1)}, bf16[256,1024]{1,0:T(8,128)(2,1)}, u32[]{:S(2)}) copy-start(bf16[256,1024]{1,0:T(8,128)(2,1)} %get-tuple-element.48.refs_1_) | copy-start | bytes 1572868
  47.4 6.4 %collective-permute-start.17 = (bf16[128,512]{1,0:T(8,128)(2,1)S(1)}, bf16[128,512]{1,0:T(8,128)(2,1)S(1)}, u32[]{:S(2)}, u32[]{:S(2)}) collective-permute-start(bf16[128,512]{1,0:T(8,128)(2,1)S(1)} %asked0.1), channel_id=1, source_target_pairs={{0,1},{1,0},{2,3},{3,2},{4,5},{5,4},{6,7},{7,6},{8,9},{9,8},{10,11... | collective-permute-start | bytes 393224 | tf_op jit(solution)/shard_map/ppermute | solution.py:619
  49.6 6.2 %collective-permute-start.16 = (bf16[128,512]{1,0:T(8,128)(2,1)S(1)}, bf16[128,512]{1,0:T(8,128)(2,1)S(1)}, u32[]{:S(2)}, u32[]{:S(2)}) collective-permute-start(bf16[128,512]{1,0:T(8,128)(2,1)S(1)} %asked1.1), channel_id=1, source_target_pairs={{0,1},{1,0},{2,3},{3,2},{4,5},{5,4},{6,7},{7,6},{8,9},{9,8},{10,11... | collective-permute-start | bytes 393224 | tf_op jit(solution)/shard_map/ppermute | solution.py:619
